TPU v7x, 512 devices: a whole 4x4x16 slice. The times are simulated.
512 devices in a mesh: section: 4 (over x), dp: 4 (over y), tensor: 32 (over z, core).
Axes of the slice: x: 4, y: 4, z: 16, core: 2. Of those that a mesh axis runs over, the one named last changes fastest.
Arguments:
- activations: bfloat16 [512, 8192], P('dp', 'tensor'), may hold values from -6 to 6
- targets: bfloat16 [4, 512, 8192], P('section', 'dp', 'tensor'), may hold values from -12 to 12
- packed_floors: int32 [4, 2048, 8192], P('section', 'dp', 'tensor'), may hold values from 0 to 4095
- rounding: float32 [4, 8192, 8192], P('section', 'dp', 'tensor'), may hold values from -8 to 8
- scales: float32 [4, 8192], P('section', 'tensor'), may hold values from 0.001 to 0.006
- norm_gains: float32 [4, 8192], P('section'), may hold values from 0.5 to 1.5
Outputs:
- rounding_next: float32 [4, 8192, 8192], P('section', 'dp', 'tensor')
- block_outputs: bfloat16 [4, 512, 8192], P('section', 'dp', 'tensor')
- losses: float32 [4], P('section')
Inputs may be any that keep to these rules, and one draw needn't show every extreme that they name: `packed_floors`: each word holds four 3-bit codes in its lowest 12 bits, lowest bits first: code k of word r of a column is row 4 r + k; the floor is the code minus 4.
All inputs are finite; a program needn't handle non-finite values.
Results may differ from a plain program's by a relative error of at most 0.0045.
The roundings to bfloat16 on the way count: a program that leaves them out, or rounds other values in their place, can miss the bound.
Values may be sent and summed in bfloat16 or wider, within the bound.
No kernel may reach another device: no remote copies, remote signals or barrier semaphores. Data moves between devices by JAX's collectives and lax.ppermute only.
A program may use at most 64 MiB of HBM per device.

v0:
```python
import functools

import jax
import jax.numpy as jnp
from jax import lax
from jax.sharding import Mesh
from jax.sharding import PartitionSpec as P

MICRO = 4
TENSOR = ("tensor_0", "tensor_1")
DP_TENSOR = ("dp", "tensor_0", "tensor_1")


norm_eps = 1e-06
grad_eps = 1e-06
reg_weight = 0.3
step_rate = 0.25
error_scale = 600.0


def passed_along(value, axis, steps):
    count = lax.axis_size(axis)
    leading, last = (max(0, -steps), min(count, count - steps))
    return lax.ppermute(value, axis, [(source, source + steps) for source in range(leading, last)])


def copy_for_each(x, axis):
    peers = lax.axis_size(axis)
    return lax.all_to_all(jnp.broadcast_to(x[None], (peers, *x.shape)), axis, 0, 0, tiled=True)


def in_order(parts, dim):
    shape = list(parts.shape[1:])
    shape[dim] *= parts.shape[0]
    return jnp.moveaxis(parts, 0, dim).reshape(shape)


def gather_directly(x, axis, dim):
    parts = copy_for_each(x, axis)
    return in_order(parts, dim)


def over_axes(x, axes):
    return functools.reduce(lax.psum, axes, x)


def unpack(words):
    shifts = 3 * jnp.arange(4, dtype=jnp.int32)
    codes = jnp.right_shift(words[:, None, :], shifts[None, :, None]) & 7
    return codes.reshape(words.shape[0] * 4, words.shape[1]).astype(jnp.float32) - 4.0


def soft_round(values):
    sig = jax.nn.sigmoid(values)
    linear = 1.2 * sig - 0.1
    soft_part = jnp.clip(linear, 0.0, 1.0)
    soft_slope = jnp.where((linear > 0.0) & (linear < 1.0), 1.2 * sig * (1.0 - sig), 0.0)
    return (soft_part, soft_slope)


def normalize(features, gain_row):
    inputs = features.astype(jnp.float32)
    mean_sq = jnp.mean(inputs * inputs, axis=1, keepdims=True)
    return (inputs * lax.rsqrt(mean_sq + norm_eps) * gain_row[None, :]).astype(jnp.bfloat16)


def per_device(activations, targets, packed_floors, rounding, scales, norm_gains):
    section_index = lax.axis_index("section")
    section_count = lax.axis_size("section")
    dp_count = lax.axis_size("dp")
    tok_dev, width_local = activations.shape
    width_full = norm_gains.shape[1]
    token_total = tok_dev * dp_count
    floors = unpack(packed_floors[0])
    soft_part, soft_slope = soft_round(rounding[0])
    channel_scale = scales[0][None, :]
    soft_weight = (channel_scale * (floors + soft_part)).astype(jnp.bfloat16)
    gain_row = norm_gains[0]
    tok_micro = tok_dev // MICRO
    group_size = 1
    block_rows = group_size * tok_micro
    block_count = MICRO // group_size
    full_weight = lax.all_gather(soft_weight, "dp", axis=0, tiled=True)
    stored_rows = jnp.zeros((tok_dev, width_full), jnp.bfloat16)
    outputs_buf = jnp.zeros((tok_dev, width_local), jnp.bfloat16)
    received = jnp.zeros((block_rows, width_local), jnp.bfloat16)
    tick_count = block_count + section_count - 1
    for tick_index in range(tick_count):
        block_index = tick_index - section_index
        active = (block_index >= 0) & (block_index < block_count)
        block_slot = jnp.clip(block_index, 0, block_count - 1)
        first_row = block_slot * block_rows
        fresh = lax.dynamic_slice_in_dim(activations, first_row, block_rows, 0)
        block_input = jnp.where(section_index == 0, fresh, received)
        whole_rows = lax.all_gather(block_input, TENSOR, axis=1, tiled=True)
        normed = normalize(whole_rows, gain_row)
        branch = jnp.dot(normed, full_weight, preferred_element_type=jnp.float32)
        earlier = lax.dynamic_slice_in_dim(stored_rows, first_row, block_rows, 0)
        stored_rows = lax.dynamic_update_slice_in_dim(
            stored_rows, jnp.where(active, normed, earlier), first_row, 0
        )
        block_result = (block_input.astype(jnp.float32) + branch).astype(jnp.bfloat16)
        earlier_out = lax.dynamic_slice_in_dim(outputs_buf, first_row, block_rows, 0)
        outputs_buf = lax.dynamic_update_slice_in_dim(
            outputs_buf, jnp.where(active, block_result, earlier_out), first_row, 0
        )
        if tick_index + 1 < tick_count:
            received = passed_along(block_result, "section", 1)
    residue = outputs_buf.astype(jnp.float32) - targets[0].astype(jnp.float32)
    delta = (error_scale / token_total**0.5 * residue).astype(jnp.bfloat16)
    delta_all = gather_directly(delta, "dp", 0)
    rows_all = lax.all_to_all(stored_rows, "dp", split_axis=1, concat_axis=0, tiled=True)
    grad_w = lax.dot_general(
        rows_all, delta_all, (((0,), (0,)), ((), ())), preferred_element_type=jnp.float32
    )
    polarity = 2.0 * soft_part - 1.0
    grad = soft_slope * (channel_scale * grad_w - 8.0 * reg_weight * polarity**3)
    recon_sum, penalty_sum, square_sum = (
        over_axes(jnp.sum(residue * residue), DP_TENSOR),
        over_axes(jnp.sum(1.0 - polarity**4), DP_TENSOR),
        over_axes(jnp.sum(grad * grad), DP_TENSOR),
    )
    mean_grad = square_sum / (width_full * width_full) + grad_eps
    rounding_next = rounding[0] - step_rate * grad * lax.rsqrt(mean_grad)
    loss_value = recon_sum / (token_total * width_full) + reg_weight * penalty_sum / (
        width_full * width_full
    )
    return (rounding_next[None], outputs_buf[None], loss_value.reshape(1))


def solution(mesh):
    torus = Mesh(
        mesh.devices.reshape(mesh.shape["section"], mesh.shape["dp"], 16, 2),
        ("section", "dp", "tensor_0", "tensor_1"),
    )
    return jax.shard_map(
        per_device,
        mesh=torus,
        in_specs=(
            P("dp", TENSOR),
            P("section", "dp", TENSOR),
            P("section", "dp", TENSOR),
            P("section", "dp", TENSOR),
            P("section", TENSOR),
            P("section", None),
        ),
        out_specs=(P("section", "dp", TENSOR), P("section", "dp", TENSOR), P("section")),
        check_vma=False,
    )
```

profile of v0, /device:TPU:1, one launch (start us, length us, event | category | flops | bytes accessed | tf_op | source)
XLA Modules:
  0.0 404.9 jit_solution(3104763950380739635)
XLA Ops:
  10.1 3.1 shift_right_arithmetic.24
  13.3 4.2 %fusion.5 = (f32[]{:T(128)}, bf16[2048,256]{1,0:T(8,128)(2,1)}) fusion(f32[1,2048,256]{2,1,0:T(8,128)S(1)} %copy-done.1, s32[2048,256]{1,0:T(8,128)} %shift_right_arithmetic.24, s32[2048]{0:T(1024)S(1)} %shift_right_arithmetic.26, f32[256]{0:T(256)S(1)} %bitcast.67), kind=kLoop, calls=%fused_computation.8 | loop fusion | flops 9961471 | bytes 5252100 | tf_op jit(solution)/shard_map/reduce_sum | solution.py:120
  17.5 39.0 %all_gather.24 = bf16[32,8192]{1,0:T(8,128)(2,1)S(1)} all-gather(bf16[32,256]{1,0:T(8,128)(2,1)S(1)} %dynamic-slice_select_fusion.6), channel_id=1, replica_groups=mesh['section'=4,'dp'=4,'tensor_0'=16,'tensor_1'=2] {'tensor_0','tensor_1'}, dimensions={1}, use_global_device_ids=true | all-gather | bytes 540672 | tf_op jit(solution)/shard_map/all_gather | solution.py:95
  56.8 22.1 %all-gather.2.cloned.1.call-done = bf16[8192,256]{1,0:T(8,128)(2,1)} async-done(((bf16[2048,256]{1,0:T(8,128)(2,1)}), bf16[8192,256]{1,0:T(8,128)(2,1)}) %all-gather.2.cloned.1.call-update) | async-done | bytes 4194320 | tf_op jit(solution)/shard_map/all_gather | solution.py:83
  85.9 33.8 %all_gather.26 = bf16[32,8192]{1,0:T(8,128)(2,1)S(1)} all-gather(bf16[32,256]{1,0:T(8,128)(2,1)S(1)} %dynamic-slice_select_fusion.5), channel_id=1, replica_groups=mesh['section'=4,'dp'=4,'tensor_0'=16,'tensor_1'=2] {'tensor_0','tensor_1'}, dimensions={1}, use_global_device_ids=true | all-gather | bytes 540672 | tf_op jit(solution)/shard_map/all_gather | solution.py:95
  120.0 3.2 select_dynamic-update-slice_fusion.11
  123.2 3.9 collective-permute-start.1
  128.0 30.4 %all_gather.27 = bf16[32,8192]{1,0:T(8,128)(2,1)S(1)} all-gather(bf16[32,256]{1,0:T(8,128)(2,1)S(1)} %dynamic-slice_select_fusion.4), channel_id=1, replica_groups=mesh['section'=4,'dp'=4,'tensor_0'=16,'tensor_1'=2] {'tensor_0','tensor_1'}, dimensions={1}, use_global_device_ids=true | all-gather | bytes 540672 | tf_op jit(solution)/shard_map/all_gather | solution.py:95
  159.5 4.0 collective-permute-start.2
  164.4 30.9 %all_gather.28 = bf16[32,8192]{1,0:T(8,128)(2,1)S(1)} all-gather(bf16[32,256]{1,0:T(8,128)(2,1)S(1)} %dynamic-slice_select_fusion.3), channel_id=1, replica_groups=mesh['section'=4,'dp'=4,'tensor_0'=16,'tensor_1'=2] {'tensor_0','tensor_1'}, dimensions={1}, use_global_device_ids=true | all-gather | bytes 540672 | tf_op jit(solution)/shard_map/all_gather | solution.py:95
  196.4 4.0 collective-permute-start.3
  201.2 29.9 %all_gather.29 = bf16[32,8192]{1,0:T(8,128)(2,1)S(1)} all-gather(bf16[32,256]{1,0:T(8,128)(2,1)S(1)} %dynamic-slice_select_fusion.2), channel_id=1, replica_groups=mesh['section'=4,'dp'=4,'tensor_0'=16,'tensor_1'=2] {'tensor_0','tensor_1'}, dimensions={1}, use_global_device_ids=true | all-gather | bytes 540672 | tf_op jit(solution)/shard_map/all_gather | solution.py:95
  232.2 4.0 collective-permute-start.4
  237.0 30.1 %all_gather.30 = bf16[32,8192]{1,0:T(8,128)(2,1)S(1)} all-gather(bf16[32,256]{1,0:T(8,128)(2,1)S(1)} %dynamic-slice_select_fusion.1), channel_id=1, replica_groups=mesh['section'=4,'dp'=4,'tensor_0'=16,'tensor_1'=2] {'tensor_0','tensor_1'}, dimensions={1}, use_global_device_ids=true | all-gather | bytes 540672 | tf_op jit(solution)/shard_map/all_gather | solution.py:95
  268.3 4.0 collective-permute-start.5
  273.1 30.1 %all_gather.31 = bf16[32,8192]{1,0:T(8,128)(2,1)S(1)} all-gather(bf16[32,256]{1,0:T(8,128)(2,1)S(1)} %dynamic-slice_select_fusion), channel_id=1, replica_groups=mesh['section'=4,'dp'=4,'tensor_0'=16,'tensor_1'=2] {'tensor_0','tensor_1'}, dimensions={1}, use_global_device_ids=true | all-gather | bytes 540672 | tf_op jit(solution)/shard_map/all_gather | solution.py:95
  305.8 3.4 all-to-all-start.1
  312.0 3.8 all-to-all-done.1
  315.8 29.1 %all_to_all.21 = bf16[128,4,2048]{0,2,1:T(8,128)(2,1)S(1)} all-to-all(bf16[128,4,2048]{0,2,1:T(8,128)(2,1)} %bitcast.50), channel_id=1, replica_groups=mesh['section'=4,'dp'=4,'tensor_0'=16,'tensor_1'=2] {'dp'}, dimensions={1} | all-to-all | bytes 4194304 | tf_op jit(solution)/shard_map/all_to_all | solution.py:112
  344.9 3.7 multiply_reduce_fusion
  348.6 7.6 %all-reduce.1 = (f32[]{:T(128)}, f32[]{:T(128)}, f32[]{:T(128)}) all-reduce(f32[]{:T(128)} %get-tuple-element.28, f32[]{:T(128)} %get-tuple-element.24, f32[]{:T(128)} %get-tuple-element.22), channel_id=1, replica_groups=mesh['section'=4,'dp'=4,'tensor_0'=16,'tensor_1'=2] {'dp'}, use_global_device_ids=true, to_apply=%region_8.9 | all-reduce | flops 3 | bytes 24 | tf_op jit(solution)/shard_map/psum | solution.py:44
  356.2 21.6 %all-reduce = (f32[]{:T(128)}, f32[]{:T(128)}, f32[]{:T(128)}) all-reduce(f32[]{:T(128)} %get-tuple-element.6, f32[]{:T(128)} %get-tuple-element.7, f32[]{:T(128)} %get-tuple-element.8), channel_id=1, replica_groups=mesh['section'=4,'dp'=4,'tensor_0'=16,'tensor_1'=2] {'tensor_0'}, use_global_device_ids=true, to_apply=%region_9.10 | all-reduce | flops 3 | bytes 24 | tf_op jit(solution)/shard_map/psum | solution.py:44
  377.8 13.9 %all-reduce.2 = (f32[]{:T(128)}, f32[]{:T(128)}, f32[]{:T(128)}) all-reduce(f32[]{:T(128)} %get-tuple-element.3, f32[]{:T(128)} %get-tuple-element.4, f32[]{:T(128)} %get-tuple-element.5), channel_id=1, replica_groups=mesh['section'=4,'dp'=4,'tensor_0'=16,'tensor_1'=2] {'tensor_1'}, use_global_device_ids=true, to_apply=%region_10.11 | all-reduce | flops 3 | bytes 24 | tf_op jit(solution)/shard_map/psum | solution.py:44
  393.7 3.2 fusion.10
  (68 shorter events, 24.6 us)
Async XLA Ops:
  7.2 71.7 %all-gather.2.cloned.1.call-start = ((), (), s32[]{:S(2)}) async-start(), calls=%async_computation.2 | async-start | bytes 5242880 | tf_op jit(solution)/shard_map/all_gather | solution.py:83
  10.1 3.1 copy-start.1
  10.1 3.1 copy-start.7
  13.3 4.2 %copy-start.5 = (bf16[128,256]{1,0:T(8,128)(2,1)S(1)}, bf16[128,256]{1,0:T(8,128)(2,1)}, u32[]{:S(2)}) copy-start(bf16[128,256]{1,0:T(8,128)(2,1)} %param.6) | copy-start | bytes 196612
  17.4 61.5 %copy-start.3 = (f32[1,8192]{1,0:T(1,128)S(1)}, f32[1,8192]{1,0:T(1,128)}, u32[]{:S(2)}) copy-start(f32[1,8192]{1,0:T(1,128)} %param.11) | copy-start | bytes 98308
  82.0 4.0 collective-permute-start
  120.0 38.7 %copy-start = (bf16[8192,256]{1,0:T(8,128)(2,1)S(1)}, bf16[8192,256]{1,0:T(8,128)(2,1)}, u32[]{:S(2)}) copy-start(bf16[8192,256]{1,0:T(8,128)(2,1)} %all-gather.2.cloned.1.call-done) | copy-start | bytes 12582916
  123.2 4.8 %collective-permute-start.1 = (bf16[32,256]{1,0:T(8,128)(2,1)S(1)}, bf16[32,256]{1,0:T(8,128)(2,1)S(1)}, u32[]{:S(2)}, u32[]{:S(2)}) collective-permute-start(bf16[32,256]{1,0:T(8,128)(2,1)S(1)} %get-tuple-element.21), channel_id=1, source_target_pairs={{0,128},{128,256},{256,384},{1,129},{129,257},{257,385},{2,130},{1... | collective-permute-start | bytes 49160 | tf_op jit(solution)/shard_map/ppermute | solution.py:24
  159.5 4.8 %collective-permute-start.2 = (bf16[32,256]{1,0:T(8,128)(2,1)S(1)}, bf16[32,256]{1,0:T(8,128)(2,1)S(1)}, u32[]{:S(2)}, u32[]{:S(2)}) collective-permute-start(bf16[32,256]{1,0:T(8,128)(2,1)S(1)} %get-tuple-element.19), channel_id=1, source_target_pairs={{0,128},{128,256},{256,384},{1,129},{129,257},{257,385},{2,130},{1... | collective-permute-start | bytes 49160 | tf_op jit(solution)/shard_map/ppermute | solution.py:24
  196.4 4.8 %collective-permute-start.3 = (bf16[32,256]{1,0:T(8,128)(2,1)S(1)}, bf16[32,256]{1,0:T(8,128)(2,1)S(1)}, u32[]{:S(2)}, u32[]{:S(2)}) collective-permute-start(bf16[32,256]{1,0:T(8,128)(2,1)S(1)} %get-tuple-element.17), channel_id=1, source_target_pairs={{0,128},{128,256},{256,384},{1,129},{129,257},{257,385},{2,130},{1... | collective-permute-start | bytes 49160 | tf_op jit(solution)/shard_map/ppermute | solution.py:24
  232.2 4.8 %collective-permute-start.4 = (bf16[32,256]{1,0:T(8,128)(2,1)S(1)}, bf16[32,256]{1,0:T(8,128)(2,1)S(1)}, u32[]{:S(2)}, u32[]{:S(2)}) collective-permute-start(bf16[32,256]{1,0:T(8,128)(2,1)S(1)} %get-tuple-element.15), channel_id=1, source_target_pairs={{0,128},{128,256},{256,384},{1,129},{129,257},{257,385},{2,130},{1... | collective-permute-start | bytes 49160 | tf_op jit(solution)/shard_map/ppermute | solution.py:24
  268.3 4.8 %collective-permute-start.5 = (bf16[32,256]{1,0:T(8,128)(2,1)S(1)}, bf16[32,256]{1,0:T(8,128)(2,1)S(1)}, u32[]{:S(2)}, u32[]{:S(2)}) collective-permute-start(bf16[32,256]{1,0:T(8,128)(2,1)S(1)} %get-tuple-element.13), channel_id=1, source_target_pairs={{0,128},{128,256},{256,384},{1,129},{129,257},{257,385},{2,130},{1... | collective-permute-start | bytes 49160 | tf_op jit(solution)/shard_map/ppermute | solution.py:24
  303.4 0.9 copy-start.6
  304.3 7.6 %copy-start.4 = (bf16[128,256]{1,0:T(8,128)(2,1)}, bf16[128,256]{1,0:T(8,128)(2,1)S(1)}, u32[]{:S(2)}) copy-start(bf16[128,256]{1,0:T(8,128)(2,1)S(1)} %fusion.47) | copy-start | bytes 196612
  305.8 10.0 %all-to-all-start.1 = ((bf16[4,128,256]{2,1,0:T(8,128)(2,1)}), bf16[4,128,256]{2,1,0:T(8,128)(2,1)S(1)}, u32[]{:S(2)}, u32[]{:S(2)}) async-start(bf16[4,128,256]{2,1,0:T(8,128)(2,1)} %broadcast_in_dim.14), calls=%async_computation.1 | async-start | bytes 524288 | tf_op jit(solution)/shard_map/all_to_all | solution.py:29
  315.8 29.1 %copy-start.2 = (f32[1,2048,256]{2,1,0:T(8,128)S(1)}, f32[1,2048,256]{2,1,0:T(8,128)}, u32[]{:S(2)}) copy-start(f32[1,2048,256]{2,1,0:T(8,128)} %param.9) | copy-start | bytes 6291460
Sparse Core Ops, SparseCore 0:
  17.6 61.2 all-gather.1
where the time goes:
time: 406 us; the launch traced here: 405 us
  blocking collectives  296 us (73%)
  waiting for transfers between devices  28.7 us (7%)
  starting transfers between devices  26.3 us (6%)
  between operations  17.4 us (4%)
  matrix products  14.4 us (4%)
  other arithmetic  12.2 us (3%)
  local copies, waits for them, and re-layouts  9.43 us (2%)
    all_gather x7, blocking collectives, per_device(): whole_rows = lax.all_gather(block_input, TENSOR, axis=1, tiled=True)  224 us
    psum x3, blocking collectives, over_axes(): return functools.reduce(lax.psum, axes, x)  43.1 us
    all_to_all x1, blocking collectives, per_device(): lax.all_to_all(stored_rows, 'dp', split_axis=1, concat_axis=0, tiled=True)  29.1 us
    ppermute x6, starting transfers between devices, passed_along(): lax.ppermute(value, axis, [(source, source + steps) for source in range(l...  22.9 us
    all_gather x1, waiting for transfers between devices, per_device(): full_weight = lax.all_gather(soft_weight, 'dp', axis=0, tiled=True)  22.1 us
    dot_general x7, matrix products, per_device(): branch = jnp.dot(normed, full_weight, preferred_element_type=jnp.float32)  10.7 us
  transfers between devices with their start and end apart: 8, of which 8 were waited for; matrix products, arithmetic and copies ran while one was open for 1% of the time, Pallas kernels for 0%

commit v1 on v0

v1 whole, which is shorter than its diff:
```python
import jax
import jax.numpy as jnp
from jax import lax
from jax.sharding import Mesh
from jax.sharding import PartitionSpec as P

TENSOR = ("tensor_0", "tensor_1")
PLANE = ("section", "dp")

norm_eps = 1e-06
grad_eps = 1e-06
reg_weight = 0.3
step_rate = 0.25
error_scale = 600.0


def exchange(x, axes):
    return lax.all_to_all(x, axes, 0, 0, tiled=True)


def total_over(x, axes):
    peers = 1
    for axis in axes if isinstance(axes, tuple) else (axes,):
        peers *= lax.axis_size(axis)
    return jnp.sum(exchange(jnp.broadcast_to(x[None], (peers, *x.shape)), axes), axis=0)


def unpack(words):
    shifts = 3 * jnp.arange(4, dtype=jnp.int32)
    codes = jnp.right_shift(words[:, None, :], shifts[None, :, None]) & 7
    return codes.reshape(words.shape[0] * 4, words.shape[1]).astype(jnp.float32) - 4.0


def soft_round(values):
    sig = jax.nn.sigmoid(values)
    linear = 1.2 * sig - 0.1
    soft_part = jnp.clip(linear, 0.0, 1.0)
    soft_slope = jnp.where((linear > 0.0) & (linear < 1.0), 1.2 * sig * (1.0 - sig), 0.0)
    return (soft_part, soft_slope)


def per_device(activations, targets, packed_floors, rounding, scales, norm_gains):
    sections = lax.axis_size("section")
    dps = lax.axis_size("dp")
    tensors = lax.axis_size("tensor_0") * lax.axis_size("tensor_1")
    section_index = lax.axis_index("section")
    dp_index = lax.axis_index("dp")
    tok_dev, width_local = activations.shape
    width_full = norm_gains.shape[1]
    token_total = tok_dev * dps
    rows_local = width_full // dps
    near = tensors // dps
    own = width_local // dps
    tok_part = tok_dev // sections
    tok_group = tok_part * dps

    soft_part, soft_slope = soft_round(rounding[0])
    channel_scale = scales[0][None, :]
    weight = (channel_scale * (unpack(packed_floors[0]) + soft_part)).astype(jnp.bfloat16)
    weight = weight.reshape(near, dps, own, width_local).transpose(1, 0, 2, 3)
    weight = exchange(weight.reshape(dps, near * own, width_local), "dp")
    weights = lax.all_gather(weight.reshape(rows_local, width_local), "section", axis=0)

    gains_own = norm_gains[0].reshape(tensors, dps, own)
    gains_own = lax.dynamic_index_in_dim(gains_own, dp_index, 1, keepdims=False).reshape(1, rows_local)
    gains = lax.all_gather(gains_own, "section", axis=0, tiled=True)

    fresh = lax.dynamic_slice_in_dim(activations, section_index * tok_part, tok_part, 0)
    fresh = exchange(fresh.reshape(tok_part, dps, own).transpose(1, 0, 2), "dp")
    current = fresh.reshape(tok_group, own).T

    target_all = lax.all_gather(targets[0], "dp", axis=0)
    target_all = target_all.reshape(dps, sections, tok_part, width_local).transpose(1, 0, 2, 3)
    target_all = target_all.reshape(token_total, width_local).astype(jnp.float32)

    sent = []
    for block in range(sections):
        features = lax.all_gather(current, TENSOR, axis=0, tiled=True).astype(jnp.float32)
        gain = gains[block][:, None]
        scaled = (features * gain).astype(jnp.bfloat16)
        partial = lax.dot_general(
            weights[block], scaled, (((0,), (0,)), ((), ())), preferred_element_type=jnp.float32
        )
        squares = jnp.sum(features * features, axis=0)
        piece = jnp.concatenate(
            [
                partial.reshape(dps, own, tok_group),
                jnp.broadcast_to(squares[None, None], (dps, 8, tok_group)),
            ],
            axis=1,
        )
        summed = jnp.sum(exchange(piece, "dp"), axis=0)
        rate = lax.rsqrt(summed[own : own + 1] / width_full + norm_eps)
        current = (current.astype(jnp.float32) + rate * summed[:own]).astype(jnp.bfloat16)
        normed = (features * rate * gain).astype(jnp.bfloat16)
        sent.append(
            jnp.concatenate(
                [
                    normed.reshape(dps, near * own, tok_group),
                    jnp.broadcast_to(current[None], (dps, own, tok_group)),
                ],
                axis=1,
            )
        )
    came = exchange(jnp.concatenate(sent, axis=0), PLANE)
    came = came.reshape(sections, dps, near * own + own, tok_group)
    rows = came[:, :, : near * own].reshape(sections, dps, near, own, tok_group)
    rows = rows.transpose(2, 1, 3, 0, 4).reshape(rows_local, token_total)
    result = came[:, :, near * own :].transpose(0, 3, 1, 2).reshape(token_total, width_local)
    residue = result.astype(jnp.float32) - target_all
    delta = (error_scale / token_total**0.5 * residue).astype(jnp.bfloat16)
    grad_w = jnp.dot(rows, delta, preferred_element_type=jnp.float32)
    polarity = 2.0 * soft_part - 1.0
    grad = soft_slope * (channel_scale * grad_w - 8.0 * reg_weight * polarity**3)
    sums = jnp.stack(
        [jnp.sum(residue * residue) / dps, jnp.sum(1.0 - polarity**4), jnp.sum(grad * grad)]
    )
    sums = jnp.broadcast_to(jnp.pad(sums, (0, 5))[:, None], (8, 128))
    sums = total_over(total_over(sums, TENSOR), "dp")[:, 0]
    mean_grad = sums[2] / (width_full * width_full) + grad_eps
    rounding_next = rounding[0] - step_rate * grad * lax.rsqrt(mean_grad)
    loss_value = sums[0] / (token_total * width_full) + reg_weight * sums[1] / (
        width_full * width_full
    )
    outputs = lax.dynamic_index_in_dim(
        result.reshape(sections, dps, tok_part, width_local), dp_index, 1, keepdims=False
    )
    return (rounding_next[None], outputs.reshape(1, tok_dev, width_local), loss_value.reshape(1))


def solution(mesh):
    torus = Mesh(
        mesh.devices.reshape(mesh.shape["section"], mesh.shape["dp"], 16, 2),
        ("section", "dp", "tensor_0", "tensor_1"),
    )
    return jax.shard_map(
        per_device,
        mesh=torus,
        in_specs=(
            P("dp", TENSOR),
            P("section", "dp", TENSOR),
            P("section", "dp", TENSOR),
            P("section", "dp", TENSOR),
            P("section", TENSOR),
            P("section", None),
        ),
        out_specs=(P("section", "dp", TENSOR), P("section", "dp", TENSOR), P("section")),
        check_vma=False,
    )
```

time: 406 us -> 360 us (0.89)
  blocking collectives: 296 us -> 196 us
  local copies, waits for them, and re-layouts: 9.43 us -> 31.9 us
  other arithmetic: 12.2 us -> 28.4 us
  starting transfers between devices: 26.3 us -> 40 us
    psum x3 -> x0, blocking collectives: 43.1 us -> none  [over_axes(): return functools.reduce(lax.psum, axes, x)]
    all_gather x7 -> x6, blocking collectives: 224 us -> 181 us  [the longest x4 137 us: per_device(): lax.all_gather(current, TENSOR, axis=0, tiled=True).astype(jnp.float32)]
    all_to_all x1 -> x8, starting transfers between devices: 3.4 us -> 40 us  [exchange(): return lax.all_to_all(x, axes, 0, 0, tiled=True)]
    all_to_all x1 -> x8, waiting for transfers between devices: 3.81 us -> 29.3 us  [exchange(): return lax.all_to_all(x, axes, 0, 0, tiled=True)]
    ppermute x6 -> x0, starting transfers between devices: 22.9 us -> none  [passed_along(): lax.ppermute(value, axis, [(source, source + steps) for source in range(l...]
    all_gather x1, waiting for transfers between devices: 22.1 us -> 2.06 us  [per_device(): lax.all_gather(weight.reshape(rows_local, width_local), 'section', axis=0)]
    all_to_all x1, blocking collectives: 29.1 us -> 14.7 us  [exchange(): return lax.all_to_all(x, axes, 0, 0, tiled=True)]
    dot_general x0 -> x5, local copies, waits for them, and re-layouts: none -> 13.4 us  [per_device(): lax.dot_general(weights[block], scaled, (((0,), (0,)), ((), ())), preferr...]
  transfers between devices with their start and end apart: 8 -> 9, of which waited for: 8 -> 6; matrix products, arithmetic and copies ran while one was open for 1% -> 6% of each run, Pallas kernels for 0% -> 0%
where the time goes in v1:
time: 360 us; the launch traced here: 357 us
  blocking collectives  196 us (54%)
  starting transfers between devices  40 us (11%)
  local copies, waits for them, and re-layouts  31.9 us (9%)
  waiting for transfers between devices  31.4 us (9%)
  other arithmetic  28.4 us (8%)
  between operations  18.2 us (5%)
  matrix products  11 us (3%)
    all_gather x4, blocking collectives, per_device(): lax.all_gather(current, TENSOR, axis=0, tiled=True).astype(jnp.float32)  137 us
    all_to_all x8, starting transfers between devices, exchange(): return lax.all_to_all(x, axes, 0, 0, tiled=True)  40 us
    all_gather x1, blocking collectives, per_device(): target_all = lax.all_gather(targets[0], 'dp', axis=0)  30 us
    all_to_all x8, waiting for transfers between devices, exchange(): return lax.all_to_all(x, axes, 0, 0, tiled=True)  29.3 us
    all_to_all x1, blocking collectives, exchange(): return lax.all_to_all(x, axes, 0, 0, tiled=True)  14.7 us
    all_gather x1, blocking collectives, per_device(): gains = lax.all_gather(gains_own, 'section', axis=0, tiled=True)  14 us
    dot_general x5, local copies, waits for them, and re-layouts, per_device(): lax.dot_general(weights[block], scaled, (((0,), (0,)), ((), ())), preferr...  13.4 us
  transfers between devices with their start and end apart: 9, of which 6 were waited for; matrix products, arithmetic and copies ran while one was open for 6% of the time, Pallas kernels for 0%

profile of v1, /device:TPU:1, one launch (start us, length us, event | category | flops | bytes accessed | tf_op | source)
XLA Modules:
  0.0 356.9 jit_solution(6779789227103633169)
XLA Ops:
  18.0 14.7 %all_to_all.45 = bf16[4,512,256]{2,1,0:T(8,128)(2,1)} all-to-all(bf16[4,512,256]{2,1,0:T(8,128)(2,1)S(1)} %bitcast.124), channel_id=1, replica_groups=mesh['section'=4,'dp'=4,'tensor_0'=16,'tensor_1'=2] {'dp'}, dimensions={0} | all-to-all | bytes 2097152 | tf_op jit(solution)/shard_map/all_to_all | solution.py:18
  33.5 3.3 all-to-all-start
  38.3 14.0 %all-gather = f32[4,1,2048]{2,1,0:T(1,128)S(1)} all-gather(f32[1,1,2048]{2,1,0:T(1,128)S(1)} %reshape.147), channel_id=1, replica_groups=mesh['section'=4,'dp'=4,'tensor_0'=16,'tensor_1'=2] {'section'}, dimensions={0}, use_global_device_ids=true | all-gather | bytes 40960 | tf_op jit(solution)/shard_map/all_gather | solution.py:66
  52.5 42.0 %all_gather.21 = bf16[2048,128]{1,0:T(8,128)(2,1)S(1)} all-gather(bf16[64,128]{1,0:T(8,128)(2,1)S(1)} %bitcast.137), channel_id=1, replica_groups=mesh['section'=4,'dp'=4,'tensor_0'=16,'tensor_1'=2] {'tensor_0','tensor_1'}, dimensions={0}, use_global_device_ids=true | all-gather | bytes 540672 | tf_op jit(solution)/shard_map/all_gather | solution.py:78
  96.8 4.3 %slice_bitcast_fusion = (bf16[256,2048]{0,1:T(8,128)(2,1)}, bf16[256,2048]{0,1:T(8,128)(2,1)}, bf16[256,2048]{0,1:T(8,128)(2,1)}, bf16[256,2048]{0,1:T(8,128)(2,1)}) fusion(bf16[4,2048,256]{2,1,0:T(8,128)(2,1)} %all-gather.3.cloned.1.call-done), kind=kLoop, calls=%fused_computation.50 | loop fusion | bytes 8388608 | tf_op jit(solution)/shard_map/dot_general | solution.py:81
  105.8 4.0 %all-to-all-start.2 = ((f32[4,72,128]{2,1,0:T(8,128)}), f32[4,72,128]{2,1,0:T(8,128)S(1)}, u32[]{:S(2)}, u32[]{:S(2)}) async-start(f32[4,72,128]{2,1,0:T(8,128)} %pad_maximum_fusion), calls=%async_computation.2 | async-start | bytes 294912 | tf_op jit(solution)/shard_map/all_to_all | solution.py:18
  116.7 33.2 %all_gather.24 = bf16[2048,128]{1,0:T(8,128)(2,1)S(1)} all-gather(bf16[64,128]{1,0:T(8,128)(2,1)S(1)} %fusion.53), channel_id=1, replica_groups=mesh['section'=4,'dp'=4,'tensor_0'=16,'tensor_1'=2] {'tensor_0','tensor_1'}, dimensions={0}, use_global_device_ids=true | all-gather | bytes 540672 | tf_op jit(solution)/shard_map/all_gather | solution.py:78
  152.7 4.5 %all-to-all-start.3 = ((f32[4,72,128]{2,1,0:T(8,128)}), f32[4,72,128]{2,1,0:T(8,128)S(1)}, u32[]{:S(2)}, u32[]{:S(2)}) async-start(f32[4,72,128]{2,1,0:T(8,128)} %pad_maximum_fusion.1), calls=%async_computation.3 | async-start | bytes 294912 | tf_op jit(solution)/shard_map/all_to_all | solution.py:18
  158.3 3.8 %all-to-all-done.3 = f32[4,72,128]{2,1,0:T(8,128)S(1)} async-done(((f32[4,72,128]{2,1,0:T(8,128)}), f32[4,72,128]{2,1,0:T(8,128)S(1)}, u32[]{:S(2)}, u32[]{:S(2)}) %all-to-all-start.3) | async-done | bytes 147488 | tf_op jit(solution)/shard_map/all_to_all | solution.py:18
  162.2 31.0 %all_gather.25 = bf16[2048,128]{1,0:T(8,128)(2,1)S(1)} all-gather(bf16[64,128]{1,0:T(8,128)(2,1)S(1)} %fusion.51), channel_id=1, replica_groups=mesh['section'=4,'dp'=4,'tensor_0'=16,'tensor_1'=2] {'tensor_0','tensor_1'}, dimensions={0}, use_global_device_ids=true | all-gather | bytes 540672 | tf_op jit(solution)/shard_map/all_gather | solution.py:78
  195.9 3.3 all-to-all-start.4
  200.4 4.0 %all-to-all-done.4 = f32[4,72,128]{2,1,0:T(8,128)S(1)} async-done(((f32[4,72,128]{2,1,0:T(8,128)}), f32[4,72,128]{2,1,0:T(8,128)S(1)}, u32[]{:S(2)}, u32[]{:S(2)}) %all-to-all-start.4) | async-done | bytes 147488 | tf_op jit(solution)/shard_map/all_to_all | solution.py:18
  204.4 31.1 %all_gather.26 = bf16[2048,128]{1,0:T(8,128)(2,1)S(1)} all-gather(bf16[64,128]{1,0:T(8,128)(2,1)S(1)} %fusion.49), channel_id=1, replica_groups=mesh['section'=4,'dp'=4,'tensor_0'=16,'tensor_1'=2] {'tensor_0','tensor_1'}, dimensions={0}, use_global_device_ids=true | all-gather | bytes 540672 | tf_op jit(solution)/shard_map/all_gather | solution.py:78
  238.3 3.5 all-to-all-start.5
  242.9 3.8 %all-to-all-done.5 = f32[4,72,128]{2,1,0:T(8,128)S(1)} async-done(((f32[4,72,128]{2,1,0:T(8,128)}), f32[4,72,128]{2,1,0:T(8,128)S(1)}, u32[]{:S(2)}, u32[]{:S(2)}) %all-to-all-start.5) | async-done | bytes 147488 | tf_op jit(solution)/shard_map/all_to_all | solution.py:18
  247.1 6.8 %maximum_maximum_fusion = bf16[16,576,128]{2,1,0:T(8,128)(2,1)} fusion(bf16[4,64,128]{2,1,0:T(8,128)(2,1)S(1)} %broadcast_in_dim.29, bf16[4,512,128]{2,1,0:T(8,128)(2,1)S(1)} %bitcast.128, bf16[4,64,128]{2,1,0:T(8,128)(2,1)S(1)} %broadcast_in_dim.27, bf16[4,512,128]{2,1,0:T(8,128)(2,1)} %bitcast.127, bf16[4,64,128]{2,1,0:T(8,128)(2,1)S(1)} %broadcast_in_dim.25, ...), kind=kLoop, calls=%fused_computation.5 | loop fusion | flops 18874368 | bytes 4718592 | tf_op jit(solution)/shard_map/concatenate | solution.py:105
  254.0 4.6 %all-to-all-start.6 = ((bf16[16,576,128]{2,1,0:T(8,128)(2,1)}), bf16[16,576,128]{2,1,0:T(8,128)(2,1)}, u32[]{:S(2)}, u32[]{:S(2)}) async-start(bf16[16,576,128]{2,1,0:T(8,128)(2,1)} %maximum_maximum_fusion), calls=%async_computation.6 | async-start | bytes 4718592 | tf_op jit(solution)/shard_map/all_to_all | solution.py:18
  258.6 30.0 %all_gather.27 = bf16[4,128,256]{2,1,0:T(8,128)(2,1)S(1)} all-gather(bf16[1,128,256]{2,1,0:T(8,128)(2,1)S(1)} %copy-done.3), channel_id=1, replica_groups=mesh['section'=4,'dp'=4,'tensor_0'=16,'tensor_1'=2] {'dp'}, dimensions={0}, use_global_device_ids=true | all-gather | bytes 327680 | tf_op jit(solution)/shard_map/all_gather | solution.py:72
  299.1 3.9 %multiply_reduce_fusion = (f32[]{:T(128)}, f32[2048,256]{1,0:T(8,128)}) fusion(bf16[32,8,4,128]{3,2,1,0:T(4,128)(2,1)S(1)} %bitcast.136, bf16[256,8,4,128]{3,2,1,0:T(4,128)(2,1)S(1)} %bitcast.129, f32[256]{0:T(256)S(1)} %bitcast.151, f32[1,2048,256]{2,1,0:T(8,128)S(1)} %copy-done.1), kind=kOutput, calls=%fused_computation.18 | convolution fusion | flops 548405248 | bytes 6554628 | tf_op jit(solution)/shard_map/dot_general | solution.py:112
  305.7 13.6 %all-to-all-start.7 = ((f32[32,8,128]{2,1,0:T(8,128)}), f32[32,8,128]{2,1,0:T(8,128)S(1)}, u32[]{:S(2)}, u32[]{:S(2)}) async-start(f32[32,8,128]{2,1,0:T(8,128)} %broadcast_in_dim_broadcast_in_dim_broadcast_in_dim.2), calls=%async_computation.7 | async-start | bytes 262144 | tf_op jit(solution)/shard_map/all_to_all | solution.py:18
  320.9 14.2 %all-to-all-done.7 = f32[32,8,128]{2,1,0:T(8,128)S(1)} async-done(((f32[32,8,128]{2,1,0:T(8,128)}), f32[32,8,128]{2,1,0:T(8,128)S(1)}, u32[]{:S(2)}, u32[]{:S(2)}) %all-to-all-start.7) | async-done | bytes 131104 | tf_op jit(solution)/shard_map/all_to_all | solution.py:18
  335.8 3.2 all-to-all-start.8
  339.7 3.5 all-to-all-done.8
  345.7 3.2 fusion.10
  (96 shorter events, 55.2 us)
Async XLA Ops:
  7.2 25.5 %copy-start = (bf16[128,256]{1,0:T(8,128)(2,1)S(1)}, bf16[128,256]{1,0:T(8,128)(2,1)}, u32[]{:S(2)}) copy-start(bf16[128,256]{1,0:T(8,128)(2,1)} %param.6) | copy-start | bytes 196612
  7.2 89.6 %all-gather.3.cloned.1.call-start = ((), (), s32[]{:S(2)}) async-start(), calls=%async_computation.9 | async-start | bytes 5242880 | tf_op jit(solution)/shard_map/all_gather | solution.py:62
  10.0 3.1 copy-start.1
  13.1 2.0 copy-start.5
  18.0 19.4 %copy-start.4 = (f32[1,8192]{1,0:T(1,128)S(1)}, f32[1,8192]{1,0:T(1,128)}, u32[]{:S(2)}) copy-start(f32[1,8192]{1,0:T(1,128)} %param.11) | copy-start | bytes 98308
  33.5 18.7 %all-to-all-start = ((bf16[4,2,1024]{2,1,0:T(2,128)(2,1)}), bf16[4,2,1024]{2,1,0:T(2,128)(2,1)S(1)}, u32[]{:S(2)}, u32[]{:S(2)}) async-start(bf16[4,2,1024]{2,1,0:T(2,128)(2,1)} %reshape.171), calls=%async_computation | async-start | bytes 32768 | tf_op jit(solution)/shard_map/all_to_all | solution.py:18
  105.8 10.9 %all-to-all-start.2 = ((f32[4,72,128]{2,1,0:T(8,128)}), f32[4,72,128]{2,1,0:T(8,128)S(1)}, u32[]{:S(2)}, u32[]{:S(2)}) async-start(f32[4,72,128]{2,1,0:T(8,128)} %pad_maximum_fusion), calls=%async_computation.2 | async-start | bytes 294912 | tf_op jit(solution)/shard_map/all_to_all | solution.py:18
  152.7 9.5 %all-to-all-start.3 = ((f32[4,72,128]{2,1,0:T(8,128)}), f32[4,72,128]{2,1,0:T(8,128)S(1)}, u32[]{:S(2)}, u32[]{:S(2)}) async-start(f32[4,72,128]{2,1,0:T(8,128)} %pad_maximum_fusion.1), calls=%async_computation.3 | async-start | bytes 294912 | tf_op jit(solution)/shard_map/all_to_all | solution.py:18
  195.9 8.4 %all-to-all-start.4 = ((f32[4,72,128]{2,1,0:T(8,128)}), f32[4,72,128]{2,1,0:T(8,128)S(1)}, u32[]{:S(2)}, u32[]{:S(2)}) async-start(f32[4,72,128]{2,1,0:T(8,128)} %pad_maximum_fusion.2), calls=%async_computation.4 | async-start | bytes 294912 | tf_op jit(solution)/shard_map/all_to_all | solution.py:18
  238.3 8.4 %all-to-all-start.5 = ((f32[4,72,128]{2,1,0:T(8,128)}), f32[4,72,128]{2,1,0:T(8,128)S(1)}, u32[]{:S(2)}, u32[]{:S(2)}) async-start(f32[4,72,128]{2,1,0:T(8,128)} %pad_maximum_fusion.3), calls=%async_computation.5 | async-start | bytes 294912 | tf_op jit(solution)/shard_map/all_to_all | solution.py:18
  254.0 4.6 %copy-start.3 = (bf16[1,128,256]{2,1,0:T(8,128)(2,1)S(1)}, bf16[1,128,256]{2,1,0:T(8,128)(2,1)}, u32[]{:S(2)}) copy-start(bf16[1,128,256]{2,1,0:T(8,128)(2,1)} %param.7) | copy-start | bytes 196612
  254.0 39.5 %all-to-all-start.6 = ((bf16[16,576,128]{2,1,0:T(8,128)(2,1)}), bf16[16,576,128]{2,1,0:T(8,128)(2,1)}, u32[]{:S(2)}, u32[]{:S(2)}) async-start(bf16[16,576,128]{2,1,0:T(8,128)(2,1)} %maximum_maximum_fusion), calls=%async_computation.6 | async-start | bytes 4718592 | tf_op jit(solution)/shard_map/all_to_all | solution.py:18
  295.2 2.0 copy-start.2
  305.7 29.4 %all-to-all-start.7 = ((f32[32,8,128]{2,1,0:T(8,128)}), f32[32,8,128]{2,1,0:T(8,128)S(1)}, u32[]{:S(2)}, u32[]{:S(2)}) async-start(f32[32,8,128]{2,1,0:T(8,128)} %broadcast_in_dim_broadcast_in_dim_broadcast_in_dim.2), calls=%async_computation.7 | async-start | bytes 262144 | tf_op jit(solution)/shard_map/all_to_all | solution.py:18
  335.8 7.4 %all-to-all-start.8 = ((f32[4,8,128]{2,1,0:T(8,128)}), f32[4,8,128]{2,1,0:T(8,128)S(1)}, u32[]{:S(2)}, u32[]{:S(2)}) async-start(f32[4,8,128]{2,1,0:T(8,128)} %broadcast_in_dim.30), calls=%async_computation.8 | async-start | bytes 32768 | tf_op jit(solution)/shard_map/all_to_all | solution.py:18
Sparse Core Ops, SparseCore 0:
  32.8 63.9 all-gather.2

commit v2 on v1

v2 whole, which is shorter than its diff:
```python
import functools

import jax
import jax.numpy as jnp
from jax import lax
from jax.experimental import pallas as pl
from jax.experimental.pallas import tpu as pltpu
from jax.sharding import Mesh
from jax.sharding import PartitionSpec as P

TENSOR = ("tensor_0", "tensor_1")
PLANE = ("section", "dp")
SPREAD = ("section", "tensor_1")
NEAR = ("dp", "tensor_1")

norm_eps = 1e-06
grad_eps = 1e-06
reg_weight = 0.3
step_rate = 0.25
error_scale = 600.0

RUN = 64
LANES = 128
ROWS_K = 1024
GAIN_ROWS = 16


def exchange(x, axes):
    return lax.all_to_all(x, axes, 0, 0, tiled=True)


def total_over(x, axes):
    peers = 1
    for axis in axes if isinstance(axes, tuple) else (axes,):
        peers *= lax.axis_size(axis)
    return jnp.sum(exchange(jnp.broadcast_to(x[None], (peers, *x.shape)), axes), axis=0)


def soft_round(values):
    sig = jax.nn.sigmoid(values)
    linear = 1.2 * sig - 0.1
    soft_part = jnp.clip(linear, 0.0, 1.0)
    soft_slope = jnp.where((linear > 0.0) & (linear < 1.0), 1.2 * sig * (1.0 - sig), 0.0)
    return (soft_part, soft_slope)


def low_half(shape):
    return lax.broadcasted_iota(jnp.int32, shape, 1) < RUN


def swap_halves(x):
    return pltpu.roll(x, RUN, 1)


def weight_kernel(words_ref, rounding_ref, scale_ref, gain_ref, out_ref, floors):
    chip = pl.program_id(0)
    words = words_ref[...]
    for k in range(4):
        code = lax.shift_right_logical(words, 3 * k) & 7
        floor = code.astype(jnp.float32) - 4.0
        for pair in range(2):
            floors[pair, pl.ds(k, words.shape[0], stride=4), :] = floor[
                :, pair * LANES : (pair + 1) * LANES
            ]
    scale = scale_ref[...]
    low = low_half((RUN, LANES))

    def rows(start):
        values = pl.ds(start, RUN)
        soft_part, _ = soft_round(rounding_ref[values, :])
        floor = jnp.concatenate([floors[0, values, :], floors[1, values, :]], axis=1)
        return scale * (floor + soft_part)

    for core in range(2):
        for part in range(2):
            first = rows((core * 4 + part) * RUN)
            second = rows((core * 4 + 2 + part) * RUN)
            place = pl.ds(pl.multiple_of(chip * 256 + (part * 2 + core) * RUN, RUN), RUN)
            for pair in range(2):
                a = first[:, pair * LANES : (pair + 1) * LANES]
                b = second[:, pair * LANES : (pair + 1) * LANES]
                out_ref[2 * pair, place, :] = jnp.where(low, a, swap_halves(b)).astype(jnp.bfloat16)
                out_ref[2 * pair + 1, place, :] = jnp.where(low, swap_halves(a), b).astype(
                    jnp.bfloat16
                )

    @pl.when(chip == 0)
    def _():
        for owner in range(4):
            out_ref[owner, pl.ds(ROWS_K, 3 * GAIN_ROWS), :] = gain_ref[...].astype(jnp.bfloat16)


def make_weight(words, rounding, scale, gain_terms):
    rows = ROWS_K + 3 * GAIN_ROWS
    return pl.pallas_call(
        weight_kernel,
        grid=(4,),
        in_specs=[
            pl.BlockSpec((128, 256), lambda i: (i, 0)),
            pl.BlockSpec((512, 256), lambda i: (i, 0)),
            pl.BlockSpec((1, 256), lambda i: (0, 0)),
            pl.BlockSpec((3 * GAIN_ROWS, LANES), lambda i: (0, 0)),
        ],
        out_specs=pl.BlockSpec((4, rows, LANES), lambda i: (0, 0, 0)),
        out_shape=jax.ShapeDtypeStruct((4, rows, LANES), jnp.bfloat16),
        scratch_shapes=[pltpu.VMEM((2, 512, LANES), jnp.float32)],
        name="make_weight",
    )(words, rounding, scale, gain_terms)


def block_kernel(width, place_ref, x_ref, w_ref, cur_ref, held_ref, sent_ref, spread_ref, next_ref, rate, acc, gains):
    slab = pl.program_id(0)
    owner = place_ref[0]

    @pl.when(slab == 0)
    def _():
        total = jnp.zeros((RUN, LANES), jnp.float32)
        for y in range(4):
            for z in range(16):
                value = x_ref[y, z].astype(jnp.float32)
                total += value * value
        mean_sq = jnp.sum(total, axis=1, keepdims=True) / width
        rate[...] = jnp.broadcast_to(lax.rsqrt(mean_sq + norm_eps), (RUN, LANES))
        acc[...] = jnp.zeros_like(acc)

    terms = w_ref[0, 0, pl.ds(ROWS_K, 3 * GAIN_ROWS), :].astype(jnp.float32)
    gains[...] = (
        terms[:GAIN_ROWS] + terms[GAIN_ROWS : 2 * GAIN_ROWS] + terms[2 * GAIN_ROWS :]
    )
    scale = rate[...]

    def normed(y, chip, row):
        value = x_ref[y, slab * 4 + chip].astype(jnp.float32)
        return (value * scale * gains[pl.ds(row, 1), :]).astype(jnp.bfloat16)

    total = acc[...]
    for chip in range(4):
        parts = [normed(y, chip, chip * 4 + y) for y in range(4)]
        left = jnp.concatenate(
            [
                jnp.concatenate([parts[0], parts[1]], axis=1),
                jnp.concatenate([parts[2], parts[3]], axis=1),
            ],
            axis=0,
        )
        rows = pl.ds(chip * 256, 256)
        right = jnp.concatenate([w_ref[0, 0, rows, :], w_ref[1, 0, rows, :]], axis=1)
        total += jnp.dot(left, right, preferred_element_type=jnp.float32)
        sent_ref[0, slab, pl.ds(chip * RUN, RUN), :] = normed(owner, chip, chip * 4 + owner)
    acc[...] = total

    @pl.when(slab == 3)
    def _():
        first, second = total[:RUN], total[RUN:]
        branch = jnp.where(
            low_half((RUN, LANES)),
            first[:, :LANES] + swap_halves(second[:, :LANES]),
            swap_halves(first[:, LANES:]) + second[:, LANES:],
        )
        result = (cur_ref[...].astype(jnp.float32) + branch).astype(jnp.bfloat16)
        next_ref[...] = result
        for z in range(16):
            spread_ref[z] = result
        for d in range(4):
            sent_ref[0, d, pl.ds(4 * RUN, RUN), :] = result


def run_block(block, width, place, features, weights, current, sent):
    rows = ROWS_K + 3 * GAIN_ROWS
    sent_shape = jax.ShapeDtypeStruct((4, 4, 5 * RUN, LANES), jnp.bfloat16)
    in_specs = [
        pl.BlockSpec(memory_space=pltpu.SMEM),
        pl.BlockSpec((4, 16, RUN, LANES), lambda i: (0, 0, 0, 0)),
        pl.BlockSpec((2, 1, rows, LANES), lambda i: (block, i, 0, 0)),
        pl.BlockSpec((RUN, LANES), lambda i: (0, 0)),
    ]
    operands = [place, features, weights, current]
    body = functools.partial(block_kernel, width)
    aliases = {}
    if sent is None:

        def body(place_ref, x_ref, w_ref, cur_ref, *rest):
            block_kernel(width, place_ref, x_ref, w_ref, cur_ref, None, *rest)

    else:
        in_specs.append(pl.BlockSpec(memory_space=pl.ANY))
        operands.append(sent)
        aliases = {4: 0}
    return pl.pallas_call(
        body,
        grid=(4,),
        in_specs=in_specs,
        out_specs=[
            pl.BlockSpec((1, 4, 5 * RUN, LANES), lambda i: (block, 0, 0, 0)),
            pl.BlockSpec((16, RUN, LANES), lambda i: (0, 0, 0)),
            pl.BlockSpec((RUN, LANES), lambda i: (0, 0)),
        ],
        out_shape=[
            sent_shape,
            jax.ShapeDtypeStruct((16, RUN, LANES), jnp.bfloat16),
            jax.ShapeDtypeStruct((RUN, LANES), jnp.bfloat16),
        ],
        scratch_shapes=[
            pltpu.VMEM((RUN, LANES), jnp.float32),
            pltpu.VMEM((2 * RUN, 256), jnp.float32),
            pltpu.VMEM((GAIN_ROWS, LANES), jnp.float32),
        ],
        input_output_aliases=aliases,
        name=f"block_{block}",
    )(*operands)


def grad_kernel(coef, place_ref, mine_ref, other_ref, target_ref, rounding_ref, scale_ref, grad_ref, out_ref, sums_ref, delta, stage):
    chip = pl.program_id(0)
    owner, core = place_ref[0], place_ref[1]
    sources = (mine_ref, other_ref)

    def tile_sum(x):
        return jnp.sum(x.reshape(-1, 8, x.shape[1] // LANES, LANES), axis=(0, 2))

    @pl.when(chip == 0)
    def _():
        low = low_half((RUN, LANES))
        recon = jnp.zeros((8, LANES), jnp.float32)
        for half in range(2):
            token_core = core if half == 0 else 1 - core
            for x in range(4):
                start = pl.multiple_of(x * 32 + token_core * 16, 16)
                for pair in range(2):
                    lanes = pl.ds(pair * LANES, LANES)
                    even = sources[half][x * 4 + 2 * pair, pl.ds(4 * RUN, RUN), :].astype(jnp.float32)
                    odd = sources[half][x * 4 + 2 * pair + 1, pl.ds(4 * RUN, RUN), :].astype(jnp.float32)
                    even = jnp.where(core == 0, even, swap_halves(even))
                    odd = jnp.where(core == 0, swap_halves(odd), odd)
                    result = jnp.where(low, even, odd)
                    stage[:, lanes] = result
                    goal = jnp.concatenate(
                        [
                            target_ref[y, pl.ds(start, 16), lanes].astype(jnp.float32)
                            for y in range(4)
                        ],
                        axis=0,
                    )
                    residue = result - goal
                    square = residue * residue
                    for k in range(8):
                        recon += square[8 * k : 8 * k + 8]
                    delta[pl.ds((half * 4 + x) * RUN, RUN), lanes] = (coef * residue).astype(
                        jnp.bfloat16
                    )
                own = stage[pl.ds(pl.multiple_of(owner * 16, 16), 16), :]
                out_ref[pl.ds(start, 16), :] = own.astype(jnp.bfloat16)
        sums_ref[...] = jnp.zeros_like(sums_ref)
        sums_ref[0] = recon

    error = delta[...]
    scale = scale_ref[...]
    penalty = jnp.zeros((8, LANES), jnp.float32)
    squares = jnp.zeros((8, LANES), jnp.float32)
    rows = pl.ds(pl.multiple_of(chip * RUN, RUN), RUN)
    for y in range(4):
        left = jnp.concatenate(
            [sources[half][x * 4 + y, rows, :] for half in range(2) for x in range(4)], axis=0
        )
        product = lax.dot_general(
            left, error, (((0,), (0,)), ((), ())), preferred_element_type=jnp.float32
        )
        for cs in range(2):
            place = pl.ds((cs * 4 + y) * RUN, RUN)
            soft_part, soft_slope = soft_round(rounding_ref[place, :])
            polarity = 2.0 * soft_part - 1.0
            grad = soft_slope * (
                scale * product[cs * RUN : (cs + 1) * RUN] - 8.0 * reg_weight * polarity**3
            )
            grad_ref[place, :] = grad
            square, fine = grad * grad, 1.0 - polarity**4
            for k in range(8):
                for lane in range(2):
                    cut = (slice(8 * k, 8 * k + 8), slice(lane * LANES, (lane + 1) * LANES))
                    squares += square[cut]
                    penalty += fine[cut]
    sums_ref[1] += penalty
    sums_ref[2] += squares


def make_grad(coef, place, mine, other, target, rounding, scale):
    rows, cols = rounding.shape
    return pl.pallas_call(
        functools.partial(grad_kernel, coef),
        grid=(4,),
        in_specs=[
            pl.BlockSpec(memory_space=pltpu.SMEM),
            pl.BlockSpec(mine.shape, lambda i: (0, 0, 0)),
            pl.BlockSpec(other.shape, lambda i: (0, 0, 0)),
            pl.BlockSpec(target.shape, lambda i: (0, 0, 0)),
            pl.BlockSpec((rows // 4, cols), lambda i: (i, 0)),
            pl.BlockSpec((1, cols), lambda i: (0, 0)),
        ],
        out_specs=[
            pl.BlockSpec((rows // 4, cols), lambda i: (i, 0)),
            pl.BlockSpec((128, cols), lambda i: (0, 0)),
            pl.BlockSpec((3, 8, LANES), lambda i: (0, 0, 0)),
        ],
        out_shape=[
            jax.ShapeDtypeStruct((rows, cols), jnp.float32),
            jax.ShapeDtypeStruct((128, cols), jnp.bfloat16),
            jax.ShapeDtypeStruct((3, 8, LANES), jnp.float32),
        ],
        scratch_shapes=[
            pltpu.VMEM((8 * RUN, cols), jnp.bfloat16),
            pltpu.VMEM((RUN, cols), jnp.float32),
        ],
        name="make_grad",
    )(place, mine, other, target, rounding, scale)


def per_device(activations, targets, packed_floors, rounding, scales, norm_gains):
    sections = lax.axis_size("section")
    dps = lax.axis_size("dp")
    section_index = lax.axis_index("section")
    dp_index = lax.axis_index("dp")
    core_index = lax.axis_index("tensor_1")
    tok_dev, width_local = activations.shape
    width_full = norm_gains.shape[1]
    token_total = tok_dev * dps
    place = jnp.stack([dp_index, core_index]).astype(jnp.int32)

    gain = lax.dynamic_slice_in_dim(norm_gains[0], dp_index * (width_full // dps), width_full // dps)
    gain = gain.reshape(4, 2, 4, RUN).transpose(0, 2, 1, 3).reshape(GAIN_ROWS, LANES)
    high = lax.reduce_precision(gain, 8, 7)
    middle = lax.reduce_precision(gain - high, 8, 7)
    gain_terms = jnp.concatenate([high, middle, gain - high - middle], axis=0)
    weight = make_weight(packed_floors[0], rounding[0], scales, gain_terms)
    weight = exchange(weight, "dp")
    weights = lax.all_gather(weight, SPREAD, axis=0)

    fresh = lax.dynamic_slice_in_dim(activations, section_index * 32, 32, 0)
    fresh = fresh.reshape(2, 16, 4, RUN).transpose(2, 0, 1, 3).reshape(8, 16, RUN)
    fresh = exchange(fresh, NEAR)
    current = fresh.reshape(4, 2, 16, RUN).transpose(0, 2, 1, 3).reshape(RUN, LANES)
    target_all = lax.all_gather(targets[0], "dp", axis=0)

    spread = jnp.broadcast_to(current[None], (16, RUN, LANES))
    sent = None
    for block in range(sections):
        line = exchange(spread, "tensor_0")
        features = exchange(jnp.broadcast_to(line[None], (4, *line.shape)), "dp")
        sent, spread, current = run_block(
            block, width_full, place, features, weights, current, sent
        )
    mine = exchange(sent.reshape(16, 5 * RUN, LANES), PLANE)
    other = lax.ppermute(mine, "tensor_1", [(0, 1), (1, 0)])
    grad, outputs, sums = make_grad(
        error_scale / token_total**0.5, place, mine, other, target_all, rounding[0], scales
    )
    sums = jnp.pad(jnp.sum(sums, axis=1), ((0, 5), (0, 0)))
    sums = jnp.sum(total_over(total_over(sums, NEAR), "tensor_0"), axis=1)
    mean_grad = sums[2] / (width_full * width_full) + grad_eps
    rounding_next = rounding[0] - step_rate * grad * lax.rsqrt(mean_grad)
    loss_value = sums[0] / dps / (token_total * width_full) + reg_weight * sums[1] / (
        width_full * width_full
    )
    return (rounding_next[None], outputs[None], loss_value.reshape(1))


def solution(mesh):
    torus = Mesh(
        mesh.devices.reshape(mesh.shape["section"], mesh.shape["dp"], 16, 2),
        ("section", "dp", "tensor_0", "tensor_1"),
    )
    return jax.shard_map(
        per_device,
        mesh=torus,
        in_specs=(
            P("dp", TENSOR),
            P("section", "dp", TENSOR),
            P("section", "dp", TENSOR),
            P("section", "dp", TENSOR),
            P("section", TENSOR),
            P("section", None),
        ),
        out_specs=(P("section", "dp", TENSOR), P("section", "dp", TENSOR), P("section")),
        check_vma=False,
    )
```

time: 360 us -> 325 us (0.903)
  blocking collectives: 196 us -> 233 us
  Pallas kernels: 0 us -> 28 us
  local copies, waits for them, and re-layouts: 31.9 us -> 4.02 us
  starting transfers between devices: 40 us -> 15.4 us
  other arithmetic: 28.4 us -> 5.25 us
  matrix products: 11 us -> 0 us
  waiting for transfers between devices: 31.4 us -> 20.7 us
    all_to_all x1 -> x12, blocking collectives: 14.7 us -> 223 us  [exchange(): return lax.all_to_all(x, axes, 0, 0, tiled=True)]
    all_gather x5 -> x0, blocking collectives: 151 us -> none  [the longest x4 137 us: per_device(): lax.all_gather(current, TENSOR, axis=0, tiled=True).astype(jnp.float32)]
    all_to_all x8 -> x1, starting transfers between devices: 40 us -> 3.52 us  [exchange(): return lax.all_to_all(x, axes, 0, 0, tiled=True)]
    pallas_call x0 -> x6, Pallas kernels: none -> 28 us  [the longest x4 17.6 us: run_block(): pl.pallas_call(body, grid=(4,), in_specs=in_specs, out_specs=[pl.BlockSpe...]
    all_to_all x8 -> x1, waiting for transfers between devices: 29.3 us -> 9.17 us  [exchange(): return lax.all_to_all(x, axes, 0, 0, tiled=True)]
    all_gather x1, blocking collectives: 30 us -> 10.1 us  [per_device(): target_all = lax.all_gather(targets[0], 'dp', axis=0)]
    dot_general x5 -> x0, local copies, waits for them, and re-layouts: 13.4 us -> none  [per_device(): lax.dot_general(weights[block], scaled, (((0,), (0,)), ((), ())), preferr...]
    ppermute x0 -> x1, starting transfers between devices: none -> 11.8 us  [per_device(): other = lax.ppermute(mine, 'tensor_1', [(0, 1), (1, 0)])]
  transfers between devices with their start and end apart: 9 -> 3, of which waited for: 6 -> 2; matrix products, arithmetic and copies ran while one was open for 6% -> 1% of each run, Pallas kernels for 0% -> 0%
where the time goes in v2:
time: 325 us; the launch traced here: 323 us
  blocking collectives  233 us (72%)
  Pallas kernels  28 us (9%)
  waiting for transfers between devices  20.7 us (6%)
  between operations  17.3 us (5%)
  starting transfers between devices  15.4 us (5%)
  other arithmetic  5.25 us (2%)
  local copies, waits for them, and re-layouts  4.02 us (1%)
    all_to_all x12, blocking collectives, exchange(): return lax.all_to_all(x, axes, 0, 0, tiled=True)  223 us
    pallas_call x4, Pallas kernels, run_block(): pl.pallas_call(body, grid=(4,), in_specs=in_specs, out_specs=[pl.BlockSpe...  17.6 us
    ppermute x1, starting transfers between devices, per_device(): other = lax.ppermute(mine, 'tensor_1', [(0, 1), (1, 0)])  11.8 us
    all_gather x1, waiting for transfers between devices, per_device(): weights = lax.all_gather(weight, SPREAD, axis=0)  11.5 us
    all_gather x1, blocking collectives, per_device(): target_all = lax.all_gather(targets[0], 'dp', axis=0)  10.1 us
    all_to_all x1, waiting for transfers between devices, exchange(): return lax.all_to_all(x, axes, 0, 0, tiled=True)  9.17 us
  transfers between devices with their start and end apart: 3, of which 2 were waited for; matrix products, arithmetic and copies ran while one was open for 1% of the time, Pallas kernels for 0%

profile of v2, /device:TPU:1, one launch (start us, length us, event | category | flops | bytes accessed | tf_op | source)
XLA Modules:
  0.0 323.3 jit_solution(12067808994969872381)
XLA Ops:
  8.8 4.2 %make_weight.1 = bf16[4,1072,128]{2,1,0:T(8,128)(2,1)} custom-call(s32[512,256]{1,0:T(8,128)} %bitcast.24, f32[2048,256]{1,0:T(8,128)} %bitcast.22, f32[1,256]{1,0:T(1,128)} %scale_ref.3, f32[48,128]{1,0:T(8,128)} %pad_maximum_fusion.gain_ref), custom_call_target="tpu_custom_call" | custom-call | tf_op jit(solution)/shard_map/make_weight/pallas_call | solution.py:95
  12.9 15.1 %all_to_all.65 = bf16[4,1072,128]{2,1,0:T(8,128)(2,1)} all-to-all(bf16[4,1072,128]{2,1,0:T(8,128)(2,1)} %make_weight.1), channel_id=1, replica_groups=mesh['section'=4,'dp'=4,'tensor_0'=16,'tensor_1'=2] {'dp'}, dimensions={0} | all-to-all | bytes 2195456 | tf_op jit(solution)/shard_map/all_to_all | solution.py:29
  28.3 14.2 %all_to_all.66 = bf16[8,2,512]{2,1,0:T(2,128)(2,1)S(1)} all-to-all(bf16[8,2,512]{2,1,0:T(2,128)(2,1)S(1)} %reshape.62), channel_id=1, replica_groups=mesh['section'=4,'dp'=4,'tensor_0'=16,'tensor_1'=2] {'dp','tensor_1'}, dimensions={0} | all-to-all | bytes 32768 | tf_op jit(solution)/shard_map/all_to_all | solution.py:29
  42.9 27.2 %all_to_all.67 = bf16[16,64,128]{2,1,0:T(8,128)(2,1)S(1)} all-to-all(bf16[16,64,128]{2,1,0:T(8,128)(2,1)S(1)} %broadcast_in_dim.21), channel_id=1, replica_groups=mesh['section'=4,'dp'=4,'tensor_0'=16,'tensor_1'=2] {'tensor_0'}, dimensions={0} | all-to-all | bytes 524288 | tf_op jit(solution)/shard_map/all_to_all | solution.py:29
  71.3 3.5 %all-to-all-start.2 = ((bf16[4,16,64,128]{3,2,1,0:T(8,128)(2,1)}), bf16[4,16,64,128]{3,2,1,0:T(8,128)(2,1)S(1)}, u32[]{:S(2)}, u32[]{:S(2)}) async-start(bf16[4,16,64,128]{3,2,1,0:T(8,128)(2,1)} %broadcast_in_dim.22), calls=%async_computation.2 | async-start | bytes 2097152 | tf_op jit(solution)/shard_map/all_to_all | solution.py:29
  75.4 9.2 %all-to-all-done.2.x_ref = bf16[4,16,64,128]{3,2,1,0:T(8,128)(2,1)S(1)} async-done(((bf16[4,16,64,128]{3,2,1,0:T(8,128)(2,1)}), bf16[4,16,64,128]{3,2,1,0:T(8,128)(2,1)S(1)}, u32[]{:S(2)}, u32[]{:S(2)}) %all-to-all-start.2) | async-done | bytes 1048608 | tf_op jit(solution)/shard_map/all_to_all | solution.py:29
  84.5 11.5 %all-gather.3.cloned.1.call-done = bf16[32,1072,128]{2,1,0:T(8,128)(2,1)} async-done(((bf16[4,1072,128]{2,1,0:T(8,128)(2,1)}), bf16[32,1072,128]{2,1,0:T(8,128)(2,1)}) %all-gather.3.cloned.1.call-update) | async-done | bytes 8781840 | tf_op jit(solution)/shard_map/all_gather | solution.py:335
  96.1 4.4 %block_0.1 = (bf16[4,4,320,128]{3,2,1,0:T(8,128)(2,1)}, bf16[16,64,128]{2,1,0:T(8,128)(2,1)}, bf16[64,128]{1,0:T(8,128)(2,1)}) custom-call(s32[2]{0:T(128)} %pad_add_fusion.place_ref, bf16[4,16,64,128]{3,2,1,0:T(8,128)(2,1)} %copy-done.3, bf16[8,4,1072,128]{3,2,1,0:T(8,128)(2,1)} %bitcast.17, bf16[64,128]{1,0:T(8,128)(2,1)} %copy-done.4), custom_call_target="tpu_custom_call" | custom-call | tf_op jit(solution)/shard_map/block_0/pallas_call | solution.py:189
  100.5 26.1 %all_to_all.68 = bf16[16,64,128]{2,1,0:T(8,128)(2,1)S(1)} all-to-all(bf16[16,64,128]{2,1,0:T(8,128)(2,1)} %get-tuple-element.16), channel_id=1, replica_groups=mesh['section'=4,'dp'=4,'tensor_0'=16,'tensor_1'=2] {'tensor_0'}, dimensions={0} | all-to-all | bytes 524288 | tf_op jit(solution)/shard_map/all_to_all | solution.py:29
  126.9 13.7 %all_to_all.69.x_ref = bf16[4,16,64,128]{3,2,1,0:T(8,128)(2,1)} all-to-all(bf16[4,16,64,128]{3,2,1,0:T(8,128)(2,1)S(1)} %broadcast_in_dim.23), channel_id=1, replica_groups=mesh['section'=4,'dp'=4,'tensor_0'=16,'tensor_1'=2] {'dp'}, dimensions={0} | all-to-all | bytes 2097152 | tf_op jit(solution)/shard_map/all_to_all | solution.py:29
  140.5 4.4 %block_1.1 = (bf16[4,4,320,128]{3,2,1,0:T(8,128)(2,1)}, bf16[16,64,128]{2,1,0:T(8,128)(2,1)}, bf16[64,128]{1,0:T(8,128)(2,1)}) custom-call(s32[2]{0:T(128)} %pad_add_fusion.place_ref, bf16[4,16,64,128]{3,2,1,0:T(8,128)(2,1)} %all_to_all.69.x_ref, bf16[8,4,1072,128]{3,2,1,0:T(8,128)(2,1)} %bitcast.18, ...), custom_call_target="tpu_custom_call", output_to_operand_aliasing={{0}: (4, {})} | custom-call | tf_op jit(solution)/shard_map/block_1/pallas_call | solution.py:189
  144.9 27.4 %all_to_all.70 = bf16[16,64,128]{2,1,0:T(8,128)(2,1)S(1)} all-to-all(bf16[16,64,128]{2,1,0:T(8,128)(2,1)} %get-tuple-element.19), channel_id=1, replica_groups=mesh['section'=4,'dp'=4,'tensor_0'=16,'tensor_1'=2] {'tensor_0'}, dimensions={0} | all-to-all | bytes 524288 | tf_op jit(solution)/shard_map/all_to_all | solution.py:29
  172.5 12.9 %all_to_all.71.x_ref = bf16[4,16,64,128]{3,2,1,0:T(8,128)(2,1)} all-to-all(bf16[4,16,64,128]{3,2,1,0:T(8,128)(2,1)S(1)} %broadcast_in_dim.24), channel_id=1, replica_groups=mesh['section'=4,'dp'=4,'tensor_0'=16,'tensor_1'=2] {'dp'}, dimensions={0} | all-to-all | bytes 2097152 | tf_op jit(solution)/shard_map/all_to_all | solution.py:29
  185.4 4.4 %block_2.1 = (bf16[4,4,320,128]{3,2,1,0:T(8,128)(2,1)}, bf16[16,64,128]{2,1,0:T(8,128)(2,1)}, bf16[64,128]{1,0:T(8,128)(2,1)}) custom-call(s32[2]{0:T(128)} %pad_add_fusion.place_ref, bf16[4,16,64,128]{3,2,1,0:T(8,128)(2,1)} %all_to_all.71.x_ref, bf16[8,4,1072,128]{3,2,1,0:T(8,128)(2,1)} %bitcast.19, ...), custom_call_target="tpu_custom_call", output_to_operand_aliasing={{0}: (4, {})} | custom-call | tf_op jit(solution)/shard_map/block_2/pallas_call | solution.py:189
  189.8 25.6 %all_to_all.72 = bf16[16,64,128]{2,1,0:T(8,128)(2,1)S(1)} all-to-all(bf16[16,64,128]{2,1,0:T(8,128)(2,1)} %get-tuple-element.22), channel_id=1, replica_groups=mesh['section'=4,'dp'=4,'tensor_0'=16,'tensor_1'=2] {'tensor_0'}, dimensions={0} | all-to-all | bytes 524288 | tf_op jit(solution)/shard_map/all_to_all | solution.py:29
  215.7 12.9 %all_to_all.73.x_ref = bf16[4,16,64,128]{3,2,1,0:T(8,128)(2,1)} all-to-all(bf16[4,16,64,128]{3,2,1,0:T(8,128)(2,1)S(1)} %broadcast_in_dim.25), channel_id=1, replica_groups=mesh['section'=4,'dp'=4,'tensor_0'=16,'tensor_1'=2] {'dp'}, dimensions={0} | all-to-all | bytes 2097152 | tf_op jit(solution)/shard_map/all_to_all | solution.py:29
  228.6 4.4 %block_3.1 = (bf16[4,4,320,128]{3,2,1,0:T(8,128)(2,1)}, bf16[16,64,128]{2,1,0:T(8,128)(2,1)}, bf16[64,128]{1,0:T(8,128)(2,1)}) custom-call(s32[2]{0:T(128)} %pad_add_fusion.place_ref, bf16[4,16,64,128]{3,2,1,0:T(8,128)(2,1)} %all_to_all.73.x_ref, bf16[8,4,1072,128]{3,2,1,0:T(8,128)(2,1)} %bitcast.20, ...), custom_call_target="tpu_custom_call", output_to_operand_aliasing={{0}: (4, {})} | custom-call | tf_op jit(solution)/shard_map/block_3/pallas_call | solution.py:189
  233.0 16.7 %all_to_all.74.mine_ref = bf16[16,320,128]{2,1,0:T(8,128)(2,1)S(1)} all-to-all(bf16[16,320,128]{2,1,0:T(8,128)(2,1)} %bitcast.21), channel_id=1, replica_groups=mesh['section'=4,'dp'=4,'tensor_0'=16,'tensor_1'=2] {'section','dp'}, dimensions={0} | all-to-all | bytes 2621440 | tf_op jit(solution)/shard_map/all_to_all | solution.py:29
  249.7 11.8 %collective-permute-start = (bf16[16,320,128]{2,1,0:T(8,128)(2,1)S(1)}, bf16[16,320,128]{2,1,0:T(8,128)(2,1)}, u32[]{:S(2)}, u32[]{:S(2)}) collective-permute-start(bf16[16,320,128]{2,1,0:T(8,128)(2,1)S(1)} %all_to_all.74.mine_ref), channel_id=1, source_target_pairs={{0,1},{1,0},{2,3},{3,2},{4,5},{5,4},{6,7},{7,6},{8,9},{9,8},{10,11... | collective-permute-start | bytes 3932168 | tf_op jit(solution)/shard_map/ppermute | solution.py:352
  261.6 10.1 %all_gather.11.target_ref = bf16[4,128,256]{2,1,0:T(8,128)(2,1)} all-gather(bf16[1,128,256]{2,1,0:T(8,128)(2,1)S(1)} %copy-done.5), channel_id=1, replica_groups=mesh['section'=4,'dp'=4,'tensor_0'=16,'tensor_1'=2] {'dp'}, dimensions={0}, use_global_device_ids=true | all-gather | bytes 327680 | tf_op jit(solution)/shard_map/all_gather | solution.py:341
  271.7 6.2 %make_grad.1 = (f32[2048,256]{1,0:T(8,128)}, bf16[128,256]{1,0:T(8,128)(2,1)}, f32[3,8,128]{2,1,0:T(8,128)}) custom-call(s32[2]{0:T(128)} %pad_add_fusion.place_ref, bf16[16,320,128]{2,1,0:T(8,128)(2,1)} %copy-done.2, bf16[16,320,128]{2,1,0:T(8,128)(2,1)} %collective-permute-done.other_ref, bf16[4,128,256]{2,1,0:T(8,128)(2,1)} %all_gather.11.target_ref, ...), custom_call_target="tpu_custom_call" | custom-call | tf_op jit(solution)/shard_map/make_grad/pallas_call | solution.py:288
  278.7 10.2 %all_to_all.75 = f32[8,8,128]{2,1,0:T(8,128)S(1)} all-to-all(f32[8,8,128]{2,1,0:T(8,128)S(1)} %broadcast_in_dim.26), channel_id=1, replica_groups=mesh['section'=4,'dp'=4,'tensor_0'=16,'tensor_1'=2] {'dp','tensor_1'}, dimensions={0} | all-to-all | bytes 65536 | tf_op jit(solution)/shard_map/all_to_all | solution.py:29
  288.8 20.6 %all_to_all.76 = f32[16,8,128]{2,1,0:T(8,128)S(1)} all-to-all(f32[16,8,128]{2,1,0:T(8,128)S(1)} %broadcast_in_dim.27), channel_id=1, replica_groups=mesh['section'=4,'dp'=4,'tensor_0'=16,'tensor_1'=2] {'tensor_0'}, dimensions={0} | all-to-all | bytes 131072 | tf_op jit(solution)/shard_map/all_to_all | solution.py:29
  312.2 3.2 subtract_bitcast_fusion
  (41 shorter events, 6.1 us)
Async XLA Ops:
  7.2 20.9 %copy-start = (bf16[128,256]{1,0:T(8,128)(2,1)S(1)}, bf16[128,256]{1,0:T(8,128)(2,1)}, u32[]{:S(2)}) copy-start(bf16[128,256]{1,0:T(8,128)(2,1)} %param.6) | copy-start | bytes 196612
  7.2 88.9 %all-gather.3.cloned.1.call-start = ((), (), s32[]{:S(2)}) async-start(), calls=%async_computation.13 | async-start | bytes 9879552 | tf_op jit(solution)/shard_map/all_gather | solution.py:335
  42.8 28.5 %copy-start.4 = (bf16[64,128]{1,0:T(8,128)(2,1)}, bf16[64,128]{1,0:T(8,128)(2,1)S(1)}, u32[]{:S(2)}) copy-start(bf16[64,128]{1,0:T(8,128)(2,1)S(1)} %broadcast_in_dim.20.cur_ref) | copy-start | bytes 49156
  71.3 13.3 %all-to-all-start.2 = ((bf16[4,16,64,128]{3,2,1,0:T(8,128)(2,1)}), bf16[4,16,64,128]{3,2,1,0:T(8,128)(2,1)S(1)}, u32[]{:S(2)}, u32[]{:S(2)}) async-start(bf16[4,16,64,128]{3,2,1,0:T(8,128)(2,1)} %broadcast_in_dim.22), calls=%async_computation.2 | async-start | bytes 2097152 | tf_op jit(solution)/shard_map/all_to_all | solution.py:29
  84.5 11.5 %copy-start.3 = (bf16[4,16,64,128]{3,2,1,0:T(8,128)(2,1)}, bf16[4,16,64,128]{3,2,1,0:T(8,128)(2,1)S(1)}, u32[]{:S(2)}) copy-start(bf16[4,16,64,128]{3,2,1,0:T(8,128)(2,1)S(1)} %all-to-all-done.2.x_ref) | copy-start | bytes 3145732
  233.0 28.6 %copy-start.5 = (bf16[1,128,256]{2,1,0:T(8,128)(2,1)S(1)}, bf16[1,128,256]{2,1,0:T(8,128)(2,1)}, u32[]{:S(2)}) copy-start(bf16[1,128,256]{2,1,0:T(8,128)(2,1)} %param.7) | copy-start | bytes 196612
  249.7 22.0 %copy-start.2 = (bf16[16,320,128]{2,1,0:T(8,128)(2,1)}, bf16[16,320,128]{2,1,0:T(8,128)(2,1)S(1)}, u32[]{:S(2)}) copy-start(bf16[16,320,128]{2,1,0:T(8,128)(2,1)S(1)} %all_to_all.74.mine_ref) | copy-start | bytes 3932164
  249.7 22.0 %collective-permute-start = (bf16[16,320,128]{2,1,0:T(8,128)(2,1)S(1)}, bf16[16,320,128]{2,1,0:T(8,128)(2,1)}, u32[]{:S(2)}, u32[]{:S(2)}) collective-permute-start(bf16[16,320,128]{2,1,0:T(8,128)(2,1)S(1)} %all_to_all.74.mine_ref), channel_id=1, source_target_pairs={{0,1},{1,0},{2,3},{3,2},{4,5},{5,4},{6,7},{7,6},{8,9},{9,8},{10,11... | collective-permute-start | bytes 3932168 | tf_op jit(solution)/shard_map/ppermute | solution.py:352
  271.7 40.5 %copy-start.1 = (f32[1,2048,256]{2,1,0:T(8,128)S(1)}, f32[1,2048,256]{2,1,0:T(8,128)}, u32[]{:S(2)}) copy-start(f32[1,2048,256]{2,1,0:T(8,128)} %param.9) | copy-start | bytes 6291460
Sparse Core Ops, SparseCore 0:
  28.2 67.8 all-gather.2

commit v3 on v2

--- a/solution.py
+++ b/solution.py
@@ -8,10 +8,11 @@
 from jax.sharding import Mesh
 from jax.sharding import PartitionSpec as P
 
-TENSOR = ("tensor_0", "tensor_1")
+TENSOR = ("line", "side", "core")
 PLANE = ("section", "dp")
-SPREAD = ("section", "tensor_1")
-NEAR = ("dp", "tensor_1")
+SPREAD = ("section", "core")
+NEAR = ("side", "dp")
+REST = ("side", "dp", "core")
 
 norm_eps = 1e-06
 grad_eps = 1e-06
@@ -29,10 +30,7 @@
     return lax.all_to_all(x, axes, 0, 0, tiled=True)
 
 
-def total_over(x, axes):
-    peers = 1
-    for axis in axes if isinstance(axes, tuple) else (axes,):
-        peers *= lax.axis_size(axis)
+def total_over(x, axes, peers):
     return jnp.sum(exchange(jnp.broadcast_to(x[None], (peers, *x.shape)), axes), axis=0)
 
 
@@ -86,11 +84,15 @@
 
     @pl.when(chip == 0)
     def _():
-        for owner in range(4):
-            out_ref[owner, pl.ds(ROWS_K, 3 * GAIN_ROWS), :] = gain_ref[...].astype(jnp.bfloat16)
-
-
-def make_weight(words, rounding, scale, gain_terms):
+        rest = gain_ref[...]
+        for term in range(3):
+            part = rest.astype(jnp.bfloat16)
+            rest = rest - part.astype(jnp.float32)
+            for owner in range(4):
+                out_ref[owner, pl.ds(ROWS_K + term * GAIN_ROWS, GAIN_ROWS), :] = part
+
+
+def make_weight(words, rounding, scale, gain):
     rows = ROWS_K + 3 * GAIN_ROWS
     return pl.pallas_call(
         weight_kernel,
@@ -99,26 +101,43 @@
             pl.BlockSpec((128, 256), lambda i: (i, 0)),
             pl.BlockSpec((512, 256), lambda i: (i, 0)),
             pl.BlockSpec((1, 256), lambda i: (0, 0)),
-            pl.BlockSpec((3 * GAIN_ROWS, LANES), lambda i: (0, 0)),
+            pl.BlockSpec((GAIN_ROWS, LANES), lambda i: (0, 0)),
         ],
         out_specs=pl.BlockSpec((4, rows, LANES), lambda i: (0, 0, 0)),
         out_shape=jax.ShapeDtypeStruct((4, rows, LANES), jnp.bfloat16),
         scratch_shapes=[pltpu.VMEM((2, 512, LANES), jnp.float32)],
         name="make_weight",
-    )(words, rounding, scale, gain_terms)
-
-
-def block_kernel(width, place_ref, x_ref, w_ref, cur_ref, held_ref, sent_ref, spread_ref, next_ref, rate, acc, gains):
+    )(words, rounding, scale, gain)
+
+
+def block_kernel(first, width, place_ref, x_ref, w_ref, cur_ref, sent_ref, spread_ref, next_ref, rate, acc, gains):
     slab = pl.program_id(0)
     owner = place_ref[0]
+    low = low_half((RUN, LANES))
+
+    def features(side, line):
+        if not first:
+            return [x_ref[side, y, line].astype(jnp.float32) for y in range(4)]
+        values = []
+        for pair in range(2):
+            lanes = pl.ds(pair * LANES, LANES)
+            a, b = (
+                jnp.concatenate(
+                    [x_ref[side, y, cs, line, :, lanes].astype(jnp.float32) for y in range(4)], axis=0
+                )
+                for cs in range(2)
+            )
+            values.append(jnp.where(low, a, swap_halves(b)))
+            values.append(jnp.where(low, swap_halves(a), b))
+        return values
 
     @pl.when(slab == 0)
     def _():
         total = jnp.zeros((RUN, LANES), jnp.float32)
-        for y in range(4):
-            for z in range(16):
-                value = x_ref[y, z].astype(jnp.float32)
-                total += value * value
+        for side in range(2):
+            for line in range(8):
+                for value in features(side, line):
+                    total += value * value
         mean_sq = jnp.sum(total, axis=1, keepdims=True) / width
         rate[...] = jnp.broadcast_to(lax.rsqrt(mean_sq + norm_eps), (RUN, LANES))
         acc[...] = jnp.zeros_like(acc)
@@ -128,14 +147,12 @@
         terms[:GAIN_ROWS] + terms[GAIN_ROWS : 2 * GAIN_ROWS] + terms[2 * GAIN_ROWS :]
     )
     scale = rate[...]
-
-    def normed(y, chip, row):
-        value = x_ref[y, slab * 4 + chip].astype(jnp.float32)
-        return (value * scale * gains[pl.ds(row, 1), :]).astype(jnp.bfloat16)
-
     total = acc[...]
     for chip in range(4):
-        parts = [normed(y, chip, chip * 4 + y) for y in range(4)]
+        parts = [
+            (value * scale * gains[pl.ds(chip * 4 + y, 1), :]).astype(jnp.bfloat16)
+            for y, value in enumerate(features(chip % 2, slab * 2 + chip // 2))
+        ]
         left = jnp.concatenate(
             [
                 jnp.concatenate([parts[0], parts[1]], axis=1),
@@ -146,58 +163,61 @@
         rows = pl.ds(chip * 256, 256)
         right = jnp.concatenate([w_ref[0, 0, rows, :], w_ref[1, 0, rows, :]], axis=1)
         total += jnp.dot(left, right, preferred_element_type=jnp.float32)
-        sent_ref[0, slab, pl.ds(chip * RUN, RUN), :] = normed(owner, chip, chip * 4 + owner)
+        for y in range(4):
+
+            @pl.when(owner == y)
+            def _():
+                sent_ref[0, slab, pl.ds(chip * RUN, RUN), :] = parts[y]
+
     acc[...] = total
 
     @pl.when(slab == 3)
     def _():
-        first, second = total[:RUN], total[RUN:]
+        upper, lower = total[:RUN], total[RUN:]
         branch = jnp.where(
-            low_half((RUN, LANES)),
-            first[:, :LANES] + swap_halves(second[:, :LANES]),
-            swap_halves(first[:, LANES:]) + second[:, LANES:],
+            low,
+            upper[:, :LANES] + swap_halves(lower[:, :LANES]),
+            swap_halves(upper[:, LANES:]) + lower[:, LANES:],
         )
         result = (cur_ref[...].astype(jnp.float32) + branch).astype(jnp.bfloat16)
         next_ref[...] = result
-        for z in range(16):
-            spread_ref[z] = result
+        for line in range(8):
+            spread_ref[line] = result
         for d in range(4):
             sent_ref[0, d, pl.ds(4 * RUN, RUN), :] = result
 
 
 def run_block(block, width, place, features, weights, current, sent):
     rows = ROWS_K + 3 * GAIN_ROWS
-    sent_shape = jax.ShapeDtypeStruct((4, 4, 5 * RUN, LANES), jnp.bfloat16)
     in_specs = [
         pl.BlockSpec(memory_space=pltpu.SMEM),
-        pl.BlockSpec((4, 16, RUN, LANES), lambda i: (0, 0, 0, 0)),
+        pl.BlockSpec(features.shape, lambda i: (0,) * features.ndim),
         pl.BlockSpec((2, 1, rows, LANES), lambda i: (block, i, 0, 0)),
         pl.BlockSpec((RUN, LANES), lambda i: (0, 0)),
     ]
     operands = [place, features, weights, current]
-    body = functools.partial(block_kernel, width)
+    body = functools.partial(block_kernel, block == 0, width)
     aliases = {}
-    if sent is None:
-
-        def body(place_ref, x_ref, w_ref, cur_ref, *rest):
-            block_kernel(width, place_ref, x_ref, w_ref, cur_ref, None, *rest)
-
-    else:
+    if block > 0:
         in_specs.append(pl.BlockSpec(memory_space=pl.ANY))
         operands.append(sent)
         aliases = {4: 0}
+
+    def kernel(place_ref, x_ref, w_ref, cur_ref, *rest):
+        body(place_ref, x_ref, w_ref, cur_ref, *rest[len(aliases) :])
+
     return pl.pallas_call(
-        body,
+        kernel,
         grid=(4,),
         in_specs=in_specs,
         out_specs=[
             pl.BlockSpec((1, 4, 5 * RUN, LANES), lambda i: (block, 0, 0, 0)),
-            pl.BlockSpec((16, RUN, LANES), lambda i: (0, 0, 0)),
+            pl.BlockSpec((8, RUN, LANES), lambda i: (0, 0, 0)),
             pl.BlockSpec((RUN, LANES), lambda i: (0, 0)),
         ],
         out_shape=[
-            sent_shape,
-            jax.ShapeDtypeStruct((16, RUN, LANES), jnp.bfloat16),
+            jax.ShapeDtypeStruct((4, 4, 5 * RUN, LANES), jnp.bfloat16),
+            jax.ShapeDtypeStruct((8, RUN, LANES), jnp.bfloat16),
             jax.ShapeDtypeStruct((RUN, LANES), jnp.bfloat16),
         ],
         scratch_shapes=[
@@ -210,13 +230,10 @@
     )(*operands)
 
 
-def grad_kernel(coef, place_ref, mine_ref, other_ref, target_ref, rounding_ref, scale_ref, grad_ref, out_ref, sums_ref, delta, stage):
+def grad_kernel(coef, place_ref, mine_ref, other_ref, target_ref, rounding_ref, scale_ref, grad_ref, out_ref, sums_ref, delta, stage, parts):
     chip = pl.program_id(0)
     owner, core = place_ref[0], place_ref[1]
     sources = (mine_ref, other_ref)
-
-    def tile_sum(x):
-        return jnp.sum(x.reshape(-1, 8, x.shape[1] // LANES, LANES), axis=(0, 2))
 
     @pl.when(chip == 0)
     def _():
@@ -250,8 +267,8 @@
                     )
                 own = stage[pl.ds(pl.multiple_of(owner * 16, 16), 16), :]
                 out_ref[pl.ds(start, 16), :] = own.astype(jnp.bfloat16)
-        sums_ref[...] = jnp.zeros_like(sums_ref)
-        sums_ref[0] = recon
+        parts[...] = jnp.zeros_like(parts)
+        parts[0] = recon
 
     error = delta[...]
     scale = scale_ref[...]
@@ -279,8 +296,16 @@
                     cut = (slice(8 * k, 8 * k + 8), slice(lane * LANES, (lane + 1) * LANES))
                     squares += square[cut]
                     penalty += fine[cut]
-    sums_ref[1] += penalty
-    sums_ref[2] += squares
+    parts[1] += penalty
+    parts[2] += squares
+
+    @pl.when(chip == 3)
+    def _():
+        lane = lax.broadcasted_iota(jnp.int32, (8, LANES), 1)
+        row = jnp.zeros((8, LANES), jnp.float32)
+        for k in range(3):
+            row = jnp.where(lane == k, jnp.sum(parts[k]), row)
+        sums_ref[...] = row
 
 
 def make_grad(coef, place, mine, other, target, rounding, scale):
@@ -299,16 +324,17 @@
         out_specs=[
             pl.BlockSpec((rows // 4, cols), lambda i: (i, 0)),
             pl.BlockSpec((128, cols), lambda i: (0, 0)),
-            pl.BlockSpec((3, 8, LANES), lambda i: (0, 0, 0)),
+            pl.BlockSpec((8, LANES), lambda i: (0, 0)),
         ],
         out_shape=[
             jax.ShapeDtypeStruct((rows, cols), jnp.float32),
             jax.ShapeDtypeStruct((128, cols), jnp.bfloat16),
-            jax.ShapeDtypeStruct((3, 8, LANES), jnp.float32),
+            jax.ShapeDtypeStruct((8, LANES), jnp.float32),
         ],
         scratch_shapes=[
             pltpu.VMEM((8 * RUN, cols), jnp.bfloat16),
             pltpu.VMEM((RUN, cols), jnp.float32),
+            pltpu.VMEM((3, 8, LANES), jnp.float32),
         ],
         name="make_grad",
     )(place, mine, other, target, rounding, scale)
@@ -319,7 +345,7 @@
     dps = lax.axis_size("dp")
     section_index = lax.axis_index("section")
     dp_index = lax.axis_index("dp")
-    core_index = lax.axis_index("tensor_1")
+    core_index = lax.axis_index("core")
     tok_dev, width_local = activations.shape
     width_full = norm_gains.shape[1]
     token_total = tok_dev * dps
@@ -327,34 +353,39 @@
 
     gain = lax.dynamic_slice_in_dim(norm_gains[0], dp_index * (width_full // dps), width_full // dps)
     gain = gain.reshape(4, 2, 4, RUN).transpose(0, 2, 1, 3).reshape(GAIN_ROWS, LANES)
-    high = lax.reduce_precision(gain, 8, 7)
-    middle = lax.reduce_precision(gain - high, 8, 7)
-    gain_terms = jnp.concatenate([high, middle, gain - high - middle], axis=0)
-    weight = make_weight(packed_floors[0], rounding[0], scales, gain_terms)
+    weight = make_weight(packed_floors[0], rounding[0], scales, gain)
     weight = exchange(weight, "dp")
     weights = lax.all_gather(weight, SPREAD, axis=0)
 
     fresh = lax.dynamic_slice_in_dim(activations, section_index * 32, 32, 0)
-    fresh = fresh.reshape(2, 16, 4, RUN).transpose(2, 0, 1, 3).reshape(8, 16, RUN)
-    fresh = exchange(fresh, NEAR)
-    current = fresh.reshape(4, 2, 16, RUN).transpose(0, 2, 1, 3).reshape(RUN, LANES)
+    line = exchange(jnp.broadcast_to(fresh[None], (8, *fresh.shape)), "line")
+    line = line.reshape(8, 2, 16, 256).transpose(1, 0, 2, 3)
+    features = exchange(jnp.broadcast_to(line[None], (8, *line.shape)).reshape(16, 8, 16, 256), REST)
+    features = features.reshape(2, 4, 2, 8, 16, 256)
+    current = lax.dynamic_slice(
+        features,
+        (lax.axis_index("side"), 0, 0, lax.axis_index("line"), 0, dp_index * RUN),
+        (1, 4, 2, 1, 16, RUN),
+    )
+    current = current.reshape(4, 2, 16, RUN).transpose(0, 2, 1, 3).reshape(RUN, LANES)
     target_all = lax.all_gather(targets[0], "dp", axis=0)
-
-    spread = jnp.broadcast_to(current[None], (16, RUN, LANES))
+    features, target_all = lax.optimization_barrier((features, target_all))
+
     sent = None
     for block in range(sections):
-        line = exchange(spread, "tensor_0")
-        features = exchange(jnp.broadcast_to(line[None], (4, *line.shape)), "dp")
+        if block > 0:
+            line = exchange(spread, "line")
+            features = exchange(jnp.broadcast_to(line[None], (8, *line.shape)), NEAR)
+            features = features.reshape(2, 4, 8, RUN, LANES)
         sent, spread, current = run_block(
             block, width_full, place, features, weights, current, sent
         )
     mine = exchange(sent.reshape(16, 5 * RUN, LANES), PLANE)
-    other = lax.ppermute(mine, "tensor_1", [(0, 1), (1, 0)])
+    other = lax.ppermute(mine, "core", [(0, 1), (1, 0)])
     grad, outputs, sums = make_grad(
         error_scale / token_total**0.5, place, mine, other, target_all, rounding[0], scales
     )
-    sums = jnp.pad(jnp.sum(sums, axis=1), ((0, 5), (0, 0)))
-    sums = jnp.sum(total_over(total_over(sums, NEAR), "tensor_0"), axis=1)
+    sums = total_over(total_over(sums[:1], "line", 8), REST, 16)[0]
     mean_grad = sums[2] / (width_full * width_full) + grad_eps
     rounding_next = rounding[0] - step_rate * grad * lax.rsqrt(mean_grad)
     loss_value = sums[0] / dps / (token_total * width_full) + reg_weight * sums[1] / (
@@ -365,8 +396,8 @@
 
 def solution(mesh):
     torus = Mesh(
-        mesh.devices.reshape(mesh.shape["section"], mesh.shape["dp"], 16, 2),
-        ("section", "dp", "tensor_0", "tensor_1"),
+        mesh.devices.reshape(mesh.shape["section"], mesh.shape["dp"], 8, 2, 2),
+        ("section", "dp", "line", "side", "core"),
     )
     return jax.shard_map(
         per_device,

time: 325 us -> 300 us (0.923)
  blocking collectives: 233 us -> 213 us
  waiting for transfers between devices: 20.7 us -> 8.24 us
  Pallas kernels: 28 us -> 31.8 us
    all_to_all x12 -> x11, blocking collectives: 223 us -> 193 us  [exchange(): return lax.all_to_all(x, axes, 0, 0, tiled=True)]
    all_gather x1, blocking collectives: 10.1 us -> 20.4 us  [per_device(): target_all = lax.all_gather(targets[0], 'dp', axis=0)]
    all_to_all x1, waiting for transfers between devices: 9.17 us -> 0.01 us  [exchange(): return lax.all_to_all(x, axes, 0, 0, tiled=True)]
    all_gather x1, waiting for transfers between devices: 11.5 us -> 5.45 us  [per_device(): weights = lax.all_gather(weight, SPREAD, axis=0)]
    pallas_call x4, Pallas kernels: 17.6 us -> 21.4 us  [run_block(): pl.pallas_call(kernel, grid=(4,), in_specs=in_specs, out_specs=[pl.BlockS...]
    all_to_all x1, starting transfers between devices: 3.52 us -> 6.78 us  [exchange(): return lax.all_to_all(x, axes, 0, 0, tiled=True)]
where the time goes in v3:
time: 300 us; the launch traced here: 298 us
  blocking collectives  213 us (71%)
  Pallas kernels  31.8 us (11%)
  starting transfers between devices  18.1 us (6%)
  between operations  17.3 us (6%)
  waiting for transfers between devices  8.24 us (3%)
  local copies, waits for them, and re-layouts  5.62 us (2%)
  other arithmetic  3.81 us (1%)
    all_to_all x11, blocking collectives, exchange(): return lax.all_to_all(x, axes, 0, 0, tiled=True)  193 us
    pallas_call x4, Pallas kernels, run_block(): pl.pallas_call(kernel, grid=(4,), in_specs=in_specs, out_specs=[pl.BlockS...  21.4 us
    all_gather x1, blocking collectives, per_device(): target_all = lax.all_gather(targets[0], 'dp', axis=0)  20.4 us
    ppermute x1, starting transfers between devices, per_device(): other = lax.ppermute(mine, 'core', [(0, 1), (1, 0)])  11.3 us
    all_to_all x1, starting transfers between devices, exchange(): return lax.all_to_all(x, axes, 0, 0, tiled=True)  6.78 us
    pallas_call x1, Pallas kernels, make_grad(): pl.pallas_call(functools.partial(grad_kernel, coef), grid=(4,), in_specs=...  6.2 us
  transfers between devices with their start and end apart: 3, of which 2 were waited for; matrix products, arithmetic and copies ran while one was open for 1% of the time, Pallas kernels for 0%

profile of v3, /device:TPU:1, one launch (start us, length us, event | category | flops | bytes accessed | tf_op | source)
XLA Modules:
  0.0 298.3 jit_solution(5932079012350380836)
XLA Ops:
  8.7 4.2 %make_weight.1 = bf16[4,1072,128]{2,1,0:T(8,128)(2,1)} custom-call(s32[512,256]{1,0:T(8,128)} %bitcast.43, f32[2048,256]{1,0:T(8,128)} %bitcast.35, f32[1,256]{1,0:T(1,128)} %scale_ref.3, f32[16,128]{1,0:T(8,128)} %reshape.81.gain_ref), custom_call_target="tpu_custom_call" | custom-call | tf_op jit(solution)/shard_map/make_weight/pallas_call | solution.py:97
  12.9 15.1 %all_to_all.60 = bf16[4,1072,128]{2,1,0:T(8,128)(2,1)} all-to-all(bf16[4,1072,128]{2,1,0:T(8,128)(2,1)} %make_weight.1), channel_id=1, replica_groups=mesh['section'=4,'dp'=4,'line'=8,'side'=2,'core'=2] {'dp'}, dimensions={0} | all-to-all | bytes 2195456 | tf_op jit(solution)/shard_map/all_to_all | solution.py:30
  28.1 32.6 %all_to_all.61 = bf16[8,32,256]{2,1,0:T(8,128)(2,1)S(1)} all-to-all(bf16[8,32,256]{2,1,0:T(8,128)(2,1)S(1)} %broadcast_in_dim.20), channel_id=1, replica_groups=mesh['section'=4,'dp'=4,'line'=8,'side'=2,'core'=2] {'line'}, dimensions={0} | all-to-all | bytes 262144 | tf_op jit(solution)/shard_map/all_to_all | solution.py:30
  60.8 1.1 broadcast_in_dim.21
  61.8 6.8 %all-to-all-start.1 = ((bf16[16,8,16,256]{3,2,1,0:T(8,128)(2,1)}), bf16[16,8,16,256]{3,2,1,0:T(8,128)(2,1)S(1)}, u32[]{:S(2)}, u32[]{:S(2)}) async-start(bf16[16,8,16,256]{3,2,1,0:T(8,128)(2,1)} %bitcast.5), calls=%async_computation.1 | async-start | bytes 2097152 | tf_op jit(solution)/shard_map/all_to_all | solution.py:30
  68.6 20.4 %all_gather.9.target_ref = bf16[4,128,256]{2,1,0:T(8,128)(2,1)} all-gather(bf16[1,128,256]{2,1,0:T(8,128)(2,1)S(1)} %copy-done.4), channel_id=1, replica_groups=mesh['section'=4,'dp'=4,'line'=8,'side'=2,'core'=2] {'dp'}, dimensions={0}, use_global_device_ids=true | all-gather | bytes 327680 | tf_op jit(solution)/shard_map/all_gather | solution.py:371
  90.6 5.4 %all-gather.3.cloned.1.call-done = bf16[32,1072,128]{2,1,0:T(8,128)(2,1)} async-done(((bf16[4,1072,128]{2,1,0:T(8,128)(2,1)}), bf16[32,1072,128]{2,1,0:T(8,128)(2,1)}) %all-gather.3.cloned.1.call-update) | async-done | bytes 8781840 | tf_op jit(solution)/shard_map/all_gather | solution.py:358
  96.0 6.1 %block_0.1 = (bf16[4,4,320,128]{3,2,1,0:T(8,128)(2,1)}, bf16[8,64,128]{2,1,0:T(8,128)(2,1)}, bf16[64,128]{1,0:T(8,128)(2,1)}) custom-call(s32[2]{0:T(128)} %pad_add_fusion.place_ref, bf16[2,4,2,8,16,256]{5,4,3,2,1,0:T(8,128)(2,1)} %bitcast.38, bf16[8,4,1072,128]{3,2,1,0:T(8,128)(2,1)} %bitcast.30, bf16[64,128]{1,0:T(8,128)(2,1)} %reshape.83.cur_ref), custom_call_target="tpu_custom_call" | custom-call | tf_op jit(solution)/shard_map/block_0/pallas_call | solution.py:209
  102.1 25.1 %all_to_all.62 = bf16[8,64,128]{2,1,0:T(8,128)(2,1)S(1)} all-to-all(bf16[8,64,128]{2,1,0:T(8,128)(2,1)} %get-tuple-element.19), channel_id=1, replica_groups=mesh['section'=4,'dp'=4,'line'=8,'side'=2,'core'=2] {'line'}, dimensions={0} | all-to-all | bytes 262144 | tf_op jit(solution)/shard_map/all_to_all | solution.py:30
  127.4 17.7 %all_to_all.63 = bf16[8,8,64,128]{3,2,1,0:T(8,128)(2,1)} all-to-all(bf16[8,8,64,128]{3,2,1,0:T(8,128)(2,1)S(1)} %broadcast_in_dim.22), channel_id=1, replica_groups=mesh['section'=4,'dp'=4,'line'=8,'side'=2,'core'=2] {'side','dp'}, dimensions={0} | all-to-all | bytes 2097152 | tf_op jit(solution)/shard_map/all_to_all | solution.py:30
  145.1 5.1 %block_1.1 = (bf16[4,4,320,128]{3,2,1,0:T(8,128)(2,1)}, bf16[8,64,128]{2,1,0:T(8,128)(2,1)}, bf16[64,128]{1,0:T(8,128)(2,1)}) custom-call(s32[2]{0:T(128)} %pad_add_fusion.place_ref, bf16[2,4,8,64,128]{4,3,2,1,0:T(8,128)(2,1)} %bitcast.40, bf16[8,4,1072,128]{3,2,1,0:T(8,128)(2,1)} %bitcast.31, ...), custom_call_target="tpu_custom_call", output_to_operand_aliasing={{0}: (4, {})} | custom-call | tf_op jit(solution)/shard_map/block_1/pallas_call | solution.py:209
  150.2 17.9 %all_to_all.64 = bf16[8,64,128]{2,1,0:T(8,128)(2,1)S(1)} all-to-all(bf16[8,64,128]{2,1,0:T(8,128)(2,1)} %get-tuple-element.22), channel_id=1, replica_groups=mesh['section'=4,'dp'=4,'line'=8,'side'=2,'core'=2] {'line'}, dimensions={0} | all-to-all | bytes 262144 | tf_op jit(solution)/shard_map/all_to_all | solution.py:30
  168.4 14.1 %all_to_all.65 = bf16[8,8,64,128]{3,2,1,0:T(8,128)(2,1)} all-to-all(bf16[8,8,64,128]{3,2,1,0:T(8,128)(2,1)S(1)} %broadcast_in_dim.23), channel_id=1, replica_groups=mesh['section'=4,'dp'=4,'line'=8,'side'=2,'core'=2] {'side','dp'}, dimensions={0} | all-to-all | bytes 2097152 | tf_op jit(solution)/shard_map/all_to_all | solution.py:30
  182.5 5.1 %block_2.1 = (bf16[4,4,320,128]{3,2,1,0:T(8,128)(2,1)}, bf16[8,64,128]{2,1,0:T(8,128)(2,1)}, bf16[64,128]{1,0:T(8,128)(2,1)}) custom-call(s32[2]{0:T(128)} %pad_add_fusion.place_ref, bf16[2,4,8,64,128]{4,3,2,1,0:T(8,128)(2,1)} %bitcast.41, bf16[8,4,1072,128]{3,2,1,0:T(8,128)(2,1)} %bitcast.32, ...), custom_call_target="tpu_custom_call", output_to_operand_aliasing={{0}: (4, {})} | custom-call | tf_op jit(solution)/shard_map/block_2/pallas_call | solution.py:209
  187.6 16.6 %all_to_all.66 = bf16[8,64,128]{2,1,0:T(8,128)(2,1)S(1)} all-to-all(bf16[8,64,128]{2,1,0:T(8,128)(2,1)} %get-tuple-element.25), channel_id=1, replica_groups=mesh['section'=4,'dp'=4,'line'=8,'side'=2,'core'=2] {'line'}, dimensions={0} | all-to-all | bytes 262144 | tf_op jit(solution)/shard_map/all_to_all | solution.py:30
  204.4 13.4 %all_to_all.67 = bf16[8,8,64,128]{3,2,1,0:T(8,128)(2,1)} all-to-all(bf16[8,8,64,128]{3,2,1,0:T(8,128)(2,1)S(1)} %broadcast_in_dim.24), channel_id=1, replica_groups=mesh['section'=4,'dp'=4,'line'=8,'side'=2,'core'=2] {'side','dp'}, dimensions={0} | all-to-all | bytes 2097152 | tf_op jit(solution)/shard_map/all_to_all | solution.py:30
  217.8 5.1 %block_3.1 = (bf16[4,4,320,128]{3,2,1,0:T(8,128)(2,1)}, bf16[8,64,128]{2,1,0:T(8,128)(2,1)}, bf16[64,128]{1,0:T(8,128)(2,1)}) custom-call(s32[2]{0:T(128)} %pad_add_fusion.place_ref, bf16[2,4,8,64,128]{4,3,2,1,0:T(8,128)(2,1)} %bitcast.39, bf16[8,4,1072,128]{3,2,1,0:T(8,128)(2,1)} %bitcast.33, ...), custom_call_target="tpu_custom_call", output_to_operand_aliasing={{0}: (4, {})} | custom-call | tf_op jit(solution)/shard_map/block_3/pallas_call | solution.py:209
  223.0 16.7 %all_to_all.68.mine_ref = bf16[16,320,128]{2,1,0:T(8,128)(2,1)S(1)} all-to-all(bf16[16,320,128]{2,1,0:T(8,128)(2,1)} %bitcast.34), channel_id=1, replica_groups=mesh['section'=4,'dp'=4,'line'=8,'side'=2,'core'=2] {'section','dp'}, dimensions={0} | all-to-all | bytes 2621440 | tf_op jit(solution)/shard_map/all_to_all | solution.py:30
  239.6 11.3 %collective-permute-start = (bf16[16,320,128]{2,1,0:T(8,128)(2,1)S(1)}, bf16[16,320,128]{2,1,0:T(8,128)(2,1)}, u32[]{:S(2)}, u32[]{:S(2)}) collective-permute-start(bf16[16,320,128]{2,1,0:T(8,128)(2,1)S(1)} %all_to_all.68.mine_ref), channel_id=1, source_target_pairs={{0,1},{1,0},{2,3},{3,2},{4,5},{5,4},{6,7},{7,6},{8,9},{9,8},{10,11... | collective-permute-start | bytes 3932168 | tf_op jit(solution)/shard_map/ppermute | solution.py:384
  250.9 2.8 collective-permute-done.other_ref
  253.7 6.2 %make_grad.1 = (f32[2048,256]{1,0:T(8,128)}, bf16[128,256]{1,0:T(8,128)(2,1)}, f32[8,128]{1,0:T(8,128)}) custom-call(s32[2]{0:T(128)} %pad_add_fusion.place_ref, bf16[16,320,128]{2,1,0:T(8,128)(2,1)} %copy-done.2, bf16[16,320,128]{2,1,0:T(8,128)(2,1)} %collective-permute-done.other_ref, bf16[4,128,256]{2,1,0:T(8,128)(2,1)} %all_gather.9.target_ref, ...), custom_call_target="tpu_custom_call" | custom-call | tf_op jit(solution)/shard_map/make_grad/pallas_call | solution.py:313
  260.6 13.7 %all_to_all.69 = f32[8,1,128]{2,1,0:T(1,128)S(1)} all-to-all(f32[8,1,128]{2,1,0:T(1,128)S(1)} %broadcast_in_dim.26), channel_id=1, replica_groups=mesh['section'=4,'dp'=4,'line'=8,'side'=2,'core'=2] {'line'}, dimensions={0} | all-to-all | bytes 8192 | tf_op jit(solution)/shard_map/all_to_all | solution.py:30
  274.3 10.2 %all_to_all.70 = f32[16,1,128]{2,1,0:T(1,128)S(1)} all-to-all(f32[16,1,128]{2,1,0:T(1,128)S(1)} %broadcast_in_dim.27), channel_id=1, replica_groups=mesh['section'=4,'dp'=4,'line'=8,'side'=2,'core'=2] {'side','dp','core'}, dimensions={0} | all-to-all | bytes 16384 | tf_op jit(solution)/shard_map/all_to_all | solution.py:30
  287.1 3.2 %subtract_bitcast_fusion = f32[1,2048,256]{2,1,0:T(8,128)} fusion(f32[2048,256]{1,0:T(8,128)} %get-tuple-element.30, f32[]{:T(128)} %bitcast.20, f32[1,2048,256]{2,1,0:T(8,128)S(1)} %copy-done.1), kind=kLoop, calls=%fused_computation | loop fusion | flops 1048576 | bytes 6291460 | tf_op jit(solution)/shard_map/broadcast_in_dim | solution.py:394
  (33 shorter events, 5.2 us)
Async XLA Ops:
  7.2 20.9 %copy-start = (bf16[128,256]{1,0:T(8,128)(2,1)S(1)}, bf16[128,256]{1,0:T(8,128)(2,1)}, u32[]{:S(2)}) copy-start(bf16[128,256]{1,0:T(8,128)(2,1)} %param.6) | copy-start | bytes 196612
  7.2 88.9 %all-gather.3.cloned.1.call-start = ((), (), s32[]{:S(2)}) async-start(), calls=%async_computation.12 | async-start | bytes 9879552 | tf_op jit(solution)/shard_map/all_gather | solution.py:358
  28.1 40.6 %copy-start.4 = (bf16[1,128,256]{2,1,0:T(8,128)(2,1)S(1)}, bf16[1,128,256]{2,1,0:T(8,128)(2,1)}, u32[]{:S(2)}) copy-start(bf16[1,128,256]{2,1,0:T(8,128)(2,1)} %param.7) | copy-start | bytes 196612
  61.8 27.8 %all-to-all-start.1 = ((bf16[16,8,16,256]{3,2,1,0:T(8,128)(2,1)}), bf16[16,8,16,256]{3,2,1,0:T(8,128)(2,1)S(1)}, u32[]{:S(2)}, u32[]{:S(2)}) async-start(bf16[16,8,16,256]{3,2,1,0:T(8,128)(2,1)} %bitcast.5), calls=%async_computation.1 | async-start | bytes 2097152 | tf_op jit(solution)/shard_map/all_to_all | solution.py:30
  89.6 6.4 %copy-start.3 = (bf16[16,8,16,256]{3,2,1,0:T(8,128)(2,1)}, bf16[16,8,16,256]{3,2,1,0:T(8,128)(2,1)S(1)}, u32[]{:S(2)}) copy-start(bf16[16,8,16,256]{3,2,1,0:T(8,128)(2,1)S(1)} %all-to-all-done.1) | copy-start | bytes 3145732
  239.6 14.1 %copy-start.2 = (bf16[16,320,128]{2,1,0:T(8,128)(2,1)}, bf16[16,320,128]{2,1,0:T(8,128)(2,1)S(1)}, u32[]{:S(2)}) copy-start(bf16[16,320,128]{2,1,0:T(8,128)(2,1)S(1)} %all_to_all.68.mine_ref) | copy-start | bytes 3932164
  239.6 47.5 %copy-start.1 = (f32[1,2048,256]{2,1,0:T(8,128)S(1)}, f32[1,2048,256]{2,1,0:T(8,128)}, u32[]{:S(2)}) copy-start(f32[1,2048,256]{2,1,0:T(8,128)} %param.9) | copy-start | bytes 6291460
  239.6 14.1 %collective-permute-start = (bf16[16,320,128]{2,1,0:T(8,128)(2,1)S(1)}, bf16[16,320,128]{2,1,0:T(8,128)(2,1)}, u32[]{:S(2)}, u32[]{:S(2)}) collective-permute-start(bf16[16,320,128]{2,1,0:T(8,128)(2,1)S(1)} %all_to_all.68.mine_ref), channel_id=1, source_target_pairs={{0,1},{1,0},{2,3},{3,2},{4,5},{5,4},{6,7},{7,6},{8,9},{9,8},{10,11... | collective-permute-start | bytes 3932168 | tf_op jit(solution)/shard_map/ppermute | solution.py:384
Sparse Core Ops, SparseCore 0:
  28.2 67.8 all-gather.2

commit v4 on v1

v4 whole, which is shorter than its diff:
```python
import functools

import jax
import jax.numpy as jnp
from jax import lax
from jax.experimental import pallas as pl
from jax.experimental.pallas import tpu as pltpu
from jax.sharding import Mesh
from jax.sharding import PartitionSpec as P

TENSOR = ("line", "side", "core")
PLANE = ("section", "dp")
SPREAD = ("section", "core")
NEAR = ("side", "dp")
REST = ("side", "dp", "core")

norm_eps = 1e-06
grad_eps = 1e-06
reg_weight = 0.3
step_rate = 0.25
error_scale = 600.0

RUN = 64
LANES = 128
ROWS_K = 1024
GAIN_ROWS = 16


def exchange(x, axes):
    return lax.all_to_all(x, axes, 0, 0, tiled=True)


def soft_round(values):
    sig = jax.nn.sigmoid(values)
    linear = 1.2 * sig - 0.1
    soft_part = jnp.clip(linear, 0.0, 1.0)
    soft_slope = jnp.where((linear > 0.0) & (linear < 1.0), 1.2 * sig * (1.0 - sig), 0.0)
    return (soft_part, soft_slope)


def low_half(shape):
    return lax.broadcasted_iota(jnp.int32, shape, 1) < RUN


def swap_halves(x):
    return pltpu.roll(x, RUN, 1)


IN_VMEM = pl.BlockSpec(memory_space=pltpu.VMEM)
IN_SMEM = pl.BlockSpec(memory_space=pltpu.SMEM)
IN_PLACE = pl.BlockSpec(memory_space=pl.ANY)


def weight_kernel(*refs):
    words_buf, rounding_buf = refs[:4], refs[4:8]
    scale_ref, gain_ref, out_ref, floors = refs[8:]
    rest = gain_ref[...]
    for term in range(3):
        part = rest.astype(jnp.bfloat16)
        rest = rest - part.astype(jnp.float32)
        for owner in range(4):
            out_ref[owner, pl.ds(ROWS_K + term * GAIN_ROWS, GAIN_ROWS), :] = part
    scale = scale_ref[...]
    low = low_half((RUN, LANES))
    for chip in range(4):
        words = words_buf[chip][...]
        for k in range(4):
            code = lax.shift_right_logical(words, 3 * k) & 7
            floor = code.astype(jnp.float32) - 4.0
            for pair in range(2):
                floors[chip, pair, pl.ds(k, 128, stride=4), :] = floor[
                    :, pair * LANES : (pair + 1) * LANES
                ]

        def rows(start):
            values = pl.ds(start, RUN)
            soft_part, _ = soft_round(rounding_buf[chip][values, :])
            floor = jnp.concatenate([floors[chip, pair, values, :] for pair in range(2)], axis=1)
            return scale * (floor + soft_part)

        for core in range(2):
            for part in range(2):
                first = rows((core * 4 + part) * RUN)
                second = rows((core * 4 + 2 + part) * RUN)
                place = pl.ds(chip * 256 + (part * 2 + core) * RUN, RUN)
                for pair in range(2):
                    a = first[:, pair * LANES : (pair + 1) * LANES]
                    b = second[:, pair * LANES : (pair + 1) * LANES]
                    out_ref[2 * pair, place, :] = jnp.where(low, a, swap_halves(b)).astype(
                        jnp.bfloat16
                    )
                    out_ref[2 * pair + 1, place, :] = jnp.where(low, swap_halves(a), b).astype(
                        jnp.bfloat16
                    )


def pieces_of(count, shape, place):
    return [pl.BlockSpec(shape, functools.partial(place, k)) for k in range(count)]


IN_VMEM = pl.BlockSpec(memory_space=pltpu.VMEM)
IN_SMEM = pl.BlockSpec(memory_space=pltpu.SMEM)
IN_PLACE = pl.BlockSpec(memory_space=pl.ANY)


def make_weight(words, rounding, scale, gain):
    shape = (4, ROWS_K + 3 * GAIN_ROWS, LANES)
    return pl.pallas_call(
        weight_kernel,
        grid=(1,),
        in_specs=pieces_of(4, (128, 256), lambda k, i: (k, 0))
        + pieces_of(4, (512, 256), lambda k, i: (k, 0))
        + [pl.BlockSpec(scale.shape, lambda i: (0, 0)), pl.BlockSpec(gain.shape, lambda i: (0, 0))],
        out_specs=pl.BlockSpec(shape, lambda i: (0, 0, 0)),
        out_shape=jax.ShapeDtypeStruct(shape, jnp.bfloat16),
        scratch_shapes=[pltpu.VMEM((4, 2, 512, LANES), jnp.float32)],
        compiler_params=pltpu.CompilerParams(vmem_limit_bytes=24 << 20),
        name="make_weight",
    )(*[words] * 4, *[rounding] * 4, scale, gain)


def block_kernel(block, width, place_ref, x_ref, w_refs, cur_ref, earlier, sent_ref, spread_ref, next_ref, normed, moved):
    moves = [
        pltpu.make_async_copy(piece, sent_ref.at[k], moved.at[k]) for k, piece in enumerate(earlier)
    ]
    for move in moves:
        move.start()
    slot = len(earlier)
    owner = place_ref[0]
    low = low_half((RUN, LANES))

    def features(chip):
        side, line = chip % 2, chip // 2
        if block > 0:
            return [x_ref[side, y, line].astype(jnp.float32) for y in range(4)]
        values = []
        for pair in range(2):
            lanes = pl.ds(pair * LANES, LANES)
            a, b = (
                jnp.concatenate(
                    [x_ref[side, y, cs, line, :, lanes].astype(jnp.float32) for y in range(4)], axis=0
                )
                for cs in range(2)
            )
            values.append(jnp.where(low, a, swap_halves(b)))
            values.append(jnp.where(low, swap_halves(a), b))
        return values

    squares = jnp.zeros((RUN, LANES), jnp.float32)
    for chip in range(16):
        for value in features(chip):
            squares += value * value
    mean_sq = jnp.sum(squares, axis=1, keepdims=True) / width
    rate = jnp.broadcast_to(lax.rsqrt(mean_sq + norm_eps), (RUN, LANES))
    total = jnp.zeros((2 * RUN, 256), jnp.float32)
    for d in range(4):
        terms = w_refs[d][0, 0, pl.ds(ROWS_K, 3 * GAIN_ROWS), :].astype(jnp.float32)
        gain = terms[:GAIN_ROWS] + terms[GAIN_ROWS : 2 * GAIN_ROWS] + terms[2 * GAIN_ROWS :]
        upper, lower = [], []
        for chip in range(4):
            parts = [
                (value * rate * gain[chip * 4 + y : chip * 4 + y + 1]).astype(jnp.bfloat16)
                for y, value in enumerate(features(d * 4 + chip))
            ]
            for y in range(4):
                normed[y, d, pl.ds(chip * RUN, RUN), :] = parts[y]
            upper += parts[:2]
            lower += parts[2:]
        left = jnp.concatenate(
            [jnp.concatenate(upper, axis=1), jnp.concatenate(lower, axis=1)], axis=0
        )
        rows = pl.ds(0, ROWS_K)
        right = jnp.concatenate([w_refs[d][0, 0, rows, :], w_refs[d][1, 0, rows, :]], axis=1)
        total += jnp.dot(left, right, preferred_element_type=jnp.float32)
        sent_ref[slot, d, pl.ds(0, 4 * RUN), :] = normed[owner, d]
    upper, lower = total[:RUN], total[RUN:]
    branch = jnp.where(
        low,
        upper[:, :LANES] + swap_halves(lower[:, :LANES]),
        swap_halves(upper[:, LANES:]) + lower[:, LANES:],
    )
    result = (cur_ref[...].astype(jnp.float32) + branch).astype(jnp.bfloat16)
    next_ref[...] = result
    for line in range(8):
        spread_ref[line] = result
    for d in range(4):
        sent_ref[slot, d, pl.ds(4 * RUN, RUN), :] = result
    for move in moves:
        move.wait()


def run_block(block, width, place, features, weights, current, earlier):
    count = len(earlier)

    def kernel(place_ref, x_ref, w0, w1, w2, w3, cur_ref, *rest):
        block_kernel(
            block, width, place_ref, x_ref, (w0, w1, w2, w3), cur_ref, [r.at[0] for r in rest[:count]], *rest[count:]
        )

    return pl.pallas_call(
        kernel,
        grid=(1,),
        in_specs=[IN_SMEM, IN_VMEM]
        + pieces_of(4, (2, 1, ROWS_K + 3 * GAIN_ROWS, LANES), lambda k, i: (block, k, 0, 0))
        + [IN_VMEM]
        + [IN_PLACE] * count,
        out_specs=[IN_VMEM] * 3,
        out_shape=[
            jax.ShapeDtypeStruct((count + 1, 4, 5 * RUN, LANES), jnp.bfloat16),
            jax.ShapeDtypeStruct((8, RUN, LANES), jnp.bfloat16),
            jax.ShapeDtypeStruct((RUN, LANES), jnp.bfloat16),
        ],
        scratch_shapes=[
            pltpu.VMEM((4, 4, 4 * RUN, LANES), jnp.bfloat16),
            pltpu.SemaphoreType.DMA((max(count, 1),)),
        ],
        compiler_params=pltpu.CompilerParams(vmem_limit_bytes=24 << 20),
        name=f"block_{block}",
    )(place, features, *[weights] * 4, current, *earlier)


def grad_kernel(coef, place_ref, mine_ref, other_ref, target_ref, rounding_ref, scale_ref, grad_ref, out_ref, sums_ref, delta, stage):
    owner, core = place_ref[0], place_ref[1]
    sources = (mine_ref, other_ref)
    low = low_half((RUN, LANES))

    def folded(total, value):
        for k in range(0, value.shape[0], 8):
            for lane in range(0, value.shape[1], LANES):
                total += value[k : k + 8, lane : lane + LANES]
        return total

    recon, penalty, squares = (jnp.zeros((8, LANES), jnp.float32) for _ in range(3))
    for half in range(2):
        token_core = core if half == 0 else 1 - core
        for x in range(4):
            start = pl.multiple_of(x * 32 + token_core * 16, 16)
            for pair in range(2):
                lanes = pl.ds(pair * LANES, LANES)
                even = sources[half][x * 4 + 2 * pair, pl.ds(4 * RUN, RUN), :].astype(jnp.float32)
                odd = sources[half][x * 4 + 2 * pair + 1, pl.ds(4 * RUN, RUN), :].astype(jnp.float32)
                even = jnp.where(core == 0, even, swap_halves(even))
                odd = jnp.where(core == 0, swap_halves(odd), odd)
                result = jnp.where(low, even, odd)
                stage[:, lanes] = result
                goal = jnp.concatenate(
                    [target_ref[y, pl.ds(start, 16), lanes].astype(jnp.float32) for y in range(4)],
                    axis=0,
                )
                residue = result - goal
                recon = folded(recon, residue * residue)
                delta[pl.ds((half * 4 + x) * RUN, RUN), lanes] = (coef * residue).astype(
                    jnp.bfloat16
                )
            own = stage[pl.ds(pl.multiple_of(owner * 16, 16), 16), :]
            out_ref[pl.ds(start, 16), :] = own.astype(jnp.bfloat16)

    error = delta[...]
    scale = scale_ref[...]
    for chip in range(4):
        left = jnp.concatenate(
            [
                jnp.concatenate(
                    [
                        sources[half][x * 4 + y, pl.ds(chip * RUN, RUN), :]
                        for half in range(2)
                        for x in range(4)
                    ],
                    axis=0,
                )
                for y in range(4)
            ],
            axis=1,
        )
        whole = lax.dot_general(
            left, error, (((0,), (0,)), ((), ())), preferred_element_type=jnp.float32
        )
        for y in range(4):
            for cs in range(2):
                place = pl.ds(chip * 512 + (cs * 4 + y) * RUN, RUN)
                product = whole[y * LANES + cs * RUN : y * LANES + (cs + 1) * RUN]
                soft_part, soft_slope = soft_round(rounding_ref[place, :])
                polarity = 2.0 * soft_part - 1.0
                grad = soft_slope * (scale * product - 8.0 * reg_weight * polarity**3)
                grad_ref[place, :] = grad
                squares = folded(squares, grad * grad)
                penalty = folded(penalty, 1.0 - polarity**4)
    lane = lax.broadcasted_iota(jnp.int32, (1, LANES), 1)
    row = jnp.zeros((1, LANES), jnp.float32)
    for k, value in enumerate((recon, penalty, squares)):
        row = jnp.where(lane == k, jnp.sum(value), row)
    for k in range(8):
        sums_ref[k] = row


def make_grad(coef, place, mine, other, target, rounding, scale):
    rows, cols = rounding.shape
    return pl.pallas_call(
        functools.partial(grad_kernel, coef),
        in_specs=[IN_SMEM] + [IN_VMEM] * 5,
        out_specs=[IN_VMEM] * 3,
        out_shape=[
            jax.ShapeDtypeStruct((rows, cols), jnp.float32),
            jax.ShapeDtypeStruct((128, cols), jnp.bfloat16),
            jax.ShapeDtypeStruct((8, 1, LANES), jnp.float32),
        ],
        scratch_shapes=[
            pltpu.VMEM((8 * RUN, cols), jnp.bfloat16),
            pltpu.VMEM((RUN, cols), jnp.float32),
        ],
        compiler_params=pltpu.CompilerParams(vmem_limit_bytes=16 << 20),
        name="make_grad",
    )(place, mine, other, target, rounding, scale)


def finish_kernel(recon_count, penalty_count, sums_ref, grad_ref, rounding_ref, out_ref, loss_ref):
    sums = jnp.sum(sums_ref[...], axis=0)
    lane = lax.broadcasted_iota(jnp.int32, sums.shape, 1)
    recon, penalty, squares = (jnp.sum(jnp.where(lane == k, sums, 0.0)) for k in range(3))
    mean_grad = jnp.full((8, 256), squares, jnp.float32) / penalty_count + grad_eps
    rate = lax.rsqrt(mean_grad)[:1]
    out_ref[...] = rounding_ref[...] - step_rate * grad_ref[...] * rate
    loss_ref[0] = recon * (1.0 / recon_count) + reg_weight * (penalty * (1.0 / penalty_count))


def finish(recon_count, penalty_count, sums, grad, rounding):
    rows, cols = rounding.shape
    part = pl.BlockSpec((rows // 2, cols), lambda i: (i, 0))
    return pl.pallas_call(
        functools.partial(finish_kernel, recon_count, penalty_count),
        grid=(2,),
        in_specs=[pl.BlockSpec(sums.shape, lambda i: (0, 0, 0)), part, part],
        out_specs=[part, IN_SMEM],
        out_shape=[
            jax.ShapeDtypeStruct(rounding.shape, jnp.float32),
            jax.ShapeDtypeStruct((1,), jnp.float32),
        ],
        compiler_params=pltpu.CompilerParams(vmem_limit_bytes=24 << 20),
        name="finish",
    )(sums, grad, rounding)


def per_device(activations, targets, packed_floors, rounding, scales, norm_gains):
    sections = lax.axis_size("section")
    dps = lax.axis_size("dp")
    section_index = lax.axis_index("section")
    dp_index = lax.axis_index("dp")
    core_index = lax.axis_index("core")
    tok_dev, width_local = activations.shape
    width_full = norm_gains.shape[1]
    token_total = tok_dev * dps
    place = jnp.stack([dp_index, core_index]).astype(jnp.int32)

    gain = lax.dynamic_slice_in_dim(norm_gains[0], dp_index * (width_full // dps), width_full // dps)
    gain = gain.reshape(4, 2, 4, RUN).transpose(0, 2, 1, 3).reshape(GAIN_ROWS, LANES)
    weight = make_weight(packed_floors[0], rounding[0], scales, gain)
    weight = exchange(weight, "dp")
    weights = lax.all_gather(weight, SPREAD, axis=0)

    fresh = lax.dynamic_slice_in_dim(activations, section_index * 32, 32, 0)
    line = exchange(jnp.broadcast_to(fresh[None], (8, *fresh.shape)), "line")
    line = line.reshape(8, 2, 16, 256).transpose(1, 0, 2, 3)
    features = exchange(jnp.broadcast_to(line[None], (8, *line.shape)).reshape(16, 8, 16, 256), REST)
    features = features.reshape(2, 4, 2, 8, 16, 256)
    current = lax.dynamic_slice(
        features,
        (lax.axis_index("side"), 0, 0, lax.axis_index("line"), 0, dp_index * RUN),
        (1, 4, 2, 1, 16, RUN),
    )
    current = current.reshape(4, 2, 16, RUN).transpose(0, 2, 1, 3).reshape(RUN, LANES)
    target_all = lax.all_gather(targets[0], "dp", axis=0)
    features, target_all = lax.optimization_barrier((features, target_all))

    pieces = []
    for block in range(sections):
        if block > 0:
            line = exchange(spread, "line")
            features = exchange(jnp.broadcast_to(line[None], (8, *line.shape)), NEAR)
            features = features.reshape(2, 4, 8, RUN, LANES)
        earlier = pieces if block == sections - 1 else []
        sent, spread, current = run_block(
            block,
            width_full,
            place,
            features,
            weights[:2] if block == 0 else weights,
            current,
            earlier,
        )
        pieces.append(sent)
    mine = exchange(sent.reshape(16, 5 * RUN, LANES), PLANE)
    other = lax.ppermute(mine, "core", [(0, 1), (1, 0)])
    grad, outputs, sums = make_grad(
        error_scale / token_total**0.5, place, mine, other, target_all, rounding[0], scales
    )
    sums = jnp.sum(exchange(sums, "line"), axis=0, keepdims=True)
    sums = exchange(jnp.broadcast_to(sums, (16, *sums.shape[1:])), REST)
    rounding_next, loss_value = finish(
        float(dps * token_total * width_full), float(width_full * width_full), sums, grad, rounding[0]
    )
    return (rounding_next[None], outputs[None], loss_value)


def solution(mesh):
    torus = Mesh(
        mesh.devices.reshape(mesh.shape["section"], mesh.shape["dp"], 8, 2, 2),
        ("section", "dp", "line", "side", "core"),
    )
    return jax.shard_map(
        per_device,
        mesh=torus,
        in_specs=(
            P("dp", TENSOR),
            P("section", "dp", TENSOR),
            P("section", "dp", TENSOR),
            P("section", "dp", TENSOR),
            P("section", TENSOR),
            P("section", None),
        ),
        out_specs=(P("section", "dp", TENSOR), P("section", "dp", TENSOR), P("section")),
        check_vma=False,
    )
```

time: 360 us -> 278 us (0.77)
  other arithmetic: 28.4 us -> 0.1 us
  starting transfers between devices: 40 us -> 16.3 us
  waiting for transfers between devices: 31.4 us -> 9.82 us
  local copies, waits for them, and re-layouts: 31.9 us -> 10.9 us
  blocking collectives: 196 us -> 213 us
  Pallas kernels: 0 us -> 12.8 us
  matrix products: 11 us -> 0 us
  between operations: 18.2 us -> 14.2 us
    all_to_all x1 -> x11, blocking collectives: 14.7 us -> 193 us  [exchange(): return lax.all_to_all(x, axes, 0, 0, tiled=True)]
    all_gather x5 -> x0, blocking collectives: 151 us -> none  [the longest x4 137 us: per_device(): lax.all_gather(current, TENSOR, axis=0, tiled=True).astype(jnp.float32)]
    all_to_all x8 -> x1, starting transfers between devices: 40 us -> 6.8 us  [exchange(): return lax.all_to_all(x, axes, 0, 0, tiled=True)]
    all_to_all x8 -> x1, waiting for transfers between devices: 29.3 us -> 0.01 us  [exchange(): return lax.all_to_all(x, axes, 0, 0, tiled=True)]
    dot_general x5 -> x0, local copies, waits for them, and re-layouts: 13.4 us -> none  [per_device(): lax.dot_general(weights[block], scaled, (((0,), (0,)), ((), ())), preferr...]
    pallas_call x0 -> x7, Pallas kernels: none -> 12.8 us  [the longest x4 6.99 us: run_block(): pl.pallas_call(kernel, grid=(1,), in_specs=[IN_SMEM, IN_VMEM] + pieces_of...]
    dot_general x5 -> x0, matrix products: 11 us -> none  [the longest x4 7.06 us: per_device(): lax.dot_general(weights[block], scaled, (((0,), (0,)), ((), ())), preferr...]
    all_gather x1, blocking collectives: 30 us -> 20 us  [per_device(): target_all = lax.all_gather(targets[0], 'dp', axis=0)]
  transfers between devices with their start and end apart: 9 -> 3, of which waited for: 6 -> 2; matrix products, arithmetic and copies ran while one was open for 6% -> 0% of each run, Pallas kernels for 0% -> 0%
where the time goes in v4:
time: 278 us; the launch traced here: 277 us
  blocking collectives  213 us (77%)
  starting transfers between devices  16.3 us (6%)
  between operations  14.2 us (5%)
  Pallas kernels  12.8 us (5%)
  local copies, waits for them, and re-layouts  10.9 us (4%)
  waiting for transfers between devices  9.82 us (4%)
    all_to_all x11, blocking collectives, exchange(): return lax.all_to_all(x, axes, 0, 0, tiled=True)  193 us
    all_gather x1, blocking collectives, per_device(): target_all = lax.all_gather(targets[0], 'dp', axis=0)  20 us
    ppermute x1, starting transfers between devices, per_device(): other = lax.ppermute(mine, 'core', [(0, 1), (1, 0)])  9.51 us
    all_gather x1, waiting for transfers between devices, per_device(): weights = lax.all_gather(weight, SPREAD, axis=0)  7.16 us
    pallas_call x4, Pallas kernels, run_block(): pl.pallas_call(kernel, grid=(1,), in_specs=[IN_SMEM, IN_VMEM] + pieces_of...  6.99 us
    all_to_all x1, starting transfers between devices, exchange(): return lax.all_to_all(x, axes, 0, 0, tiled=True)  6.8 us
    unnamed x20, local copies, waits for them, and re-layouts  6.25 us
  transfers between devices with their start and end apart: 3, of which 2 were waited for; matrix products, arithmetic and copies ran while one was open for 0% of the time, Pallas kernels for 0%

profile of v4, /device:TPU:1, one launch (start us, length us, event | category | flops | bytes accessed | tf_op | source)
XLA Modules:
  0.0 276.8 jit_solution(6310198138618714849)
XLA Ops:
  8.1 1.6 copy-done.2
  12.6 15.1 %all_to_all.60 = bf16[4,1072,128]{2,1,0:T(8,128)(2,1)} all-to-all(bf16[4,1072,128]{2,1,0:T(8,128)(2,1)S(1)} %make_weight.1), channel_id=1, replica_groups=mesh['section'=4,'dp'=4,'line'=8,'side'=2,'core'=2] {'dp'}, dimensions={0} | all-to-all | bytes 2195456 | tf_op jit(solution)/shard_map/all_to_all | solution.py:30
  27.8 32.3 %all_to_all.61 = bf16[8,32,256]{2,1,0:T(8,128)(2,1)S(1)} all-to-all(bf16[8,32,256]{2,1,0:T(8,128)(2,1)S(1)} %broadcast_in_dim.16), channel_id=1, replica_groups=mesh['section'=4,'dp'=4,'line'=8,'side'=2,'core'=2] {'line'}, dimensions={0} | all-to-all | bytes 262144 | tf_op jit(solution)/shard_map/all_to_all | solution.py:30
  61.2 6.8 %all-to-all-start.1 = ((bf16[16,8,16,256]{3,2,1,0:T(8,128)(2,1)}), bf16[16,8,16,256]{3,2,1,0:T(8,128)(2,1)S(1)}, u32[]{:S(2)}, u32[]{:S(2)}) async-start(bf16[16,8,16,256]{3,2,1,0:T(8,128)(2,1)} %bitcast.4), calls=%async_computation.1 | async-start | bytes 2097152 | tf_op jit(solution)/shard_map/all_to_all | solution.py:30
  68.0 20.0 %all_gather.9.target_ref = bf16[4,128,256]{2,1,0:T(8,128)(2,1)S(1)} all-gather(bf16[1,128,256]{2,1,0:T(8,128)(2,1)S(1)} %copy-done.9), channel_id=1, replica_groups=mesh['section'=4,'dp'=4,'line'=8,'side'=2,'core'=2] {'dp'}, dimensions={0}, use_global_device_ids=true | all-gather | bytes 327680 | tf_op jit(solution)/shard_map/all_gather | solution.py:371
  88.3 7.2 %all-gather.3.cloned.1.call-done = bf16[32,1072,128]{2,1,0:T(8,128)(2,1)} async-done(((bf16[4,1072,128]{2,1,0:T(8,128)(2,1)}), bf16[32,1072,128]{2,1,0:T(8,128)(2,1)}) %all-gather.3.cloned.1.call-update) | async-done | bytes 8781840 | tf_op jit(solution)/shard_map/all_gather | solution.py:358
  95.5 1.8 slice.5
  97.3 1.9 block_0.1
  99.1 25.0 %all_to_all.62 = bf16[8,64,128]{2,1,0:T(8,128)(2,1)S(1)} all-to-all(bf16[8,64,128]{2,1,0:T(8,128)(2,1)S(1)} %get-tuple-element.21), channel_id=1, replica_groups=mesh['section'=4,'dp'=4,'line'=8,'side'=2,'core'=2] {'line'}, dimensions={0} | all-to-all | bytes 262144 | tf_op jit(solution)/shard_map/all_to_all | solution.py:30
  124.4 17.6 %all_to_all.63 = bf16[8,8,64,128]{3,2,1,0:T(8,128)(2,1)S(1)} all-to-all(bf16[8,8,64,128]{3,2,1,0:T(8,128)(2,1)S(1)} %broadcast_in_dim.18), channel_id=1, replica_groups=mesh['section'=4,'dp'=4,'line'=8,'side'=2,'core'=2] {'side','dp'}, dimensions={0} | all-to-all | bytes 2097152 | tf_op jit(solution)/shard_map/all_to_all | solution.py:30
  143.4 17.7 %all_to_all.64 = bf16[8,64,128]{2,1,0:T(8,128)(2,1)S(1)} all-to-all(bf16[8,64,128]{2,1,0:T(8,128)(2,1)S(1)} %get-tuple-element.23), channel_id=1, replica_groups=mesh['section'=4,'dp'=4,'line'=8,'side'=2,'core'=2] {'line'}, dimensions={0} | all-to-all | bytes 262144 | tf_op jit(solution)/shard_map/all_to_all | solution.py:30
  161.3 14.4 %all_to_all.65 = bf16[8,8,64,128]{3,2,1,0:T(8,128)(2,1)S(1)} all-to-all(bf16[8,8,64,128]{3,2,1,0:T(8,128)(2,1)S(1)} %broadcast_in_dim.19), channel_id=1, replica_groups=mesh['section'=4,'dp'=4,'line'=8,'side'=2,'core'=2] {'side','dp'}, dimensions={0} | all-to-all | bytes 2097152 | tf_op jit(solution)/shard_map/all_to_all | solution.py:30
  175.7 1.4 block_2.1
  177.1 16.1 %all_to_all.66 = bf16[8,64,128]{2,1,0:T(8,128)(2,1)S(1)} all-to-all(bf16[8,64,128]{2,1,0:T(8,128)(2,1)S(1)} %get-tuple-element.25), channel_id=1, replica_groups=mesh['section'=4,'dp'=4,'line'=8,'side'=2,'core'=2] {'line'}, dimensions={0} | all-to-all | bytes 262144 | tf_op jit(solution)/shard_map/all_to_all | solution.py:30
  193.4 13.4 %all_to_all.67 = bf16[8,8,64,128]{3,2,1,0:T(8,128)(2,1)S(1)} all-to-all(bf16[8,8,64,128]{3,2,1,0:T(8,128)(2,1)S(1)} %broadcast_in_dim.20), channel_id=1, replica_groups=mesh['section'=4,'dp'=4,'line'=8,'side'=2,'core'=2] {'side','dp'}, dimensions={0} | all-to-all | bytes 2097152 | tf_op jit(solution)/shard_map/all_to_all | solution.py:30
  206.8 2.4 block_3.1
  209.2 16.7 %all_to_all.68.mine_ref = bf16[16,320,128]{2,1,0:T(8,128)(2,1)S(1)} all-to-all(bf16[16,320,128]{2,1,0:T(8,128)(2,1)S(1)} %bitcast.53), channel_id=1, replica_groups=mesh['section'=4,'dp'=4,'line'=8,'side'=2,'core'=2] {'section','dp'}, dimensions={0} | all-to-all | bytes 2621440 | tf_op jit(solution)/shard_map/all_to_all | solution.py:30
  225.9 9.5 %collective-permute-start = (bf16[16,320,128]{2,1,0:T(8,128)(2,1)S(1)}, bf16[16,320,128]{2,1,0:T(8,128)(2,1)S(1)}, u32[]{:S(2)}, u32[]{:S(2)}) collective-permute-start(bf16[16,320,128]{2,1,0:T(8,128)(2,1)S(1)} %all_to_all.68.mine_ref), channel_id=1, source_target_pairs={{0,1},{1,0},{2,3},{3,2},{4,5},{5,4},{6,7},{7,6},{8,9},{9,8},{10,11... | collective-permute-start | bytes 3932168 | tf_op jit(solution)/shard_map/ppermute | solution.py:392
  235.5 2.6 collective-permute-done.other_ref
  238.1 3.0 %make_grad.1 = (f32[2048,256]{1,0:T(8,128)S(1)}, bf16[128,256]{1,0:T(8,128)(2,1)}, f32[8,1,128]{2,1,0:T(1,128)S(1)}) custom-call(s32[2]{0:T(128)S(1)} %pad_add_fusion.place_ref, bf16[16,320,128]{2,1,0:T(8,128)(2,1)S(1)} %all_to_all.68.mine_ref, bf16[16,320,128]{2,1,0:T(8,128)(2,1)S(1)} %collective-permute-done.other_ref, ...), custom_call_target="tpu_custom_call" | custom-call | tf_op jit(solution)/shard_map/make_grad/pallas_call | solution.py:298
  242.4 13.9 %all_to_all.69 = f32[8,1,128]{2,1,0:T(1,128)S(1)} all-to-all(f32[8,1,128]{2,1,0:T(1,128)S(1)} %get-tuple-element.32), channel_id=1, replica_groups=mesh['section'=4,'dp'=4,'line'=8,'side'=2,'core'=2] {'line'}, dimensions={0} | all-to-all | bytes 8192 | tf_op jit(solution)/shard_map/all_to_all | solution.py:30
  256.3 10.3 %all_to_all.70.sums_ref = f32[16,1,128]{2,1,0:T(1,128)S(1)} all-to-all(f32[16,1,128]{2,1,0:T(1,128)S(1)} %broadcast_in_dim.21), channel_id=1, replica_groups=mesh['section'=4,'dp'=4,'line'=8,'side'=2,'core'=2] {'side','dp','core'}, dimensions={0} | all-to-all | bytes 16384 | tf_op jit(solution)/shard_map/all_to_all | solution.py:30
  266.6 1.6 copy-done.6
  268.2 1.7 finish.1
  (40 shorter events, 8.7 us)
Async XLA Ops:
  7.2 20.6 %copy-start = (bf16[128,256]{1,0:T(8,128)(2,1)S(1)}, bf16[128,256]{1,0:T(8,128)(2,1)}, u32[]{:S(2)}) copy-start(bf16[128,256]{1,0:T(8,128)(2,1)} %param.6) | copy-start | bytes 196612
  7.2 88.3 %all-gather.3.cloned.1.call-start = ((), (), s32[]{:S(2)}) async-start(), calls=%async_computation.12 | async-start | bytes 9879552 | tf_op jit(solution)/shard_map/all_gather | solution.py:358
  8.1 1.6 copy-start.2
  9.7 1.0 copy-start.4
  10.8 0.7 copy-start.7
  27.8 40.3 %copy-start.9 = (bf16[1,128,256]{2,1,0:T(8,128)(2,1)S(1)}, bf16[1,128,256]{2,1,0:T(8,128)(2,1)}, u32[]{:S(2)}) copy-start(bf16[1,128,256]{2,1,0:T(8,128)(2,1)} %param.7) | copy-start | bytes 196612
  61.2 26.9 %all-to-all-start.1 = ((bf16[16,8,16,256]{3,2,1,0:T(8,128)(2,1)}), bf16[16,8,16,256]{3,2,1,0:T(8,128)(2,1)S(1)}, u32[]{:S(2)}, u32[]{:S(2)}) async-start(bf16[16,8,16,256]{3,2,1,0:T(8,128)(2,1)} %bitcast.4), calls=%async_computation.1 | async-start | bytes 2097152 | tf_op jit(solution)/shard_map/all_to_all | solution.py:30
  97.3 44.7 %copy-start.1 = (bf16[32,1072,128]{2,1,0:T(8,128)(2,1)S(1)}, bf16[32,1072,128]{2,1,0:T(8,128)(2,1)}, u32[]{:S(2)}) copy-start(bf16[32,1072,128]{2,1,0:T(8,128)(2,1)} %all-gather.3.cloned.1.call-done) | copy-start | bytes 26345476
  209.2 28.9 %copy-start.3 = (f32[1,2048,256]{2,1,0:T(8,128)S(1)}, f32[1,2048,256]{2,1,0:T(8,128)}, u32[]{:S(2)}) copy-start(f32[1,2048,256]{2,1,0:T(8,128)} %param.9) | copy-start | bytes 6291460
  209.2 28.9 %copy-start.8 = (f32[1,256]{1,0:T(1,128)S(1)}, f32[1,256]{1,0:T(1,128)}, u32[]{:S(2)}) copy-start(f32[1,256]{1,0:T(1,128)} %scale_ref.1) | copy-start | bytes 3076
  225.9 12.2 %collective-permute-start = (bf16[16,320,128]{2,1,0:T(8,128)(2,1)S(1)}, bf16[16,320,128]{2,1,0:T(8,128)(2,1)S(1)}, u32[]{:S(2)}, u32[]{:S(2)}) collective-permute-start(bf16[16,320,128]{2,1,0:T(8,128)(2,1)S(1)} %all_to_all.68.mine_ref), channel_id=1, source_target_pairs={{0,1},{1,0},{2,3},{3,2},{4,5},{5,4},{6,7},{7,6},{8,9},{9,8},{10,11... | collective-permute-start | bytes 3932168 | tf_op jit(solution)/shard_map/ppermute | solution.py:392
  241.1 1.3 copy-start.5
  266.6 1.6 copy-start.6
Sparse Core Ops, SparseCore 0:
  27.9 67.5 all-gather.2

commit v5 on v4

--- a/solution.py
+++ b/solution.py
@@ -52,37 +52,64 @@
 
 
 def weight_kernel(*refs):
-    words_buf, rounding_buf = refs[:4], refs[4:8]
-    scale_ref, gain_ref, out_ref, floors = refs[8:]
-    rest = gain_ref[...]
-    for term in range(3):
-        part = rest.astype(jnp.bfloat16)
-        rest = rest - part.astype(jnp.float32)
-        for owner in range(4):
-            out_ref[owner, pl.ds(ROWS_K + term * GAIN_ROWS, GAIN_ROWS), :] = part
+    words_buf, rounding_buf = refs[:2], refs[2:4]
+    scale_ref, gain_ref, out_ref, floors, gains = refs[4:]
+    step = pl.program_id(0)
+
+    @pl.when(step == 0)
+    def _():
+        start = lax.axis_index("dp") * (gain_ref.shape[1] // 4)
+        even = low_half((8, LANES))
+        for chip in range(4):
+            for pair in range(2):
+                a, b = (
+                    jnp.broadcast_to(
+                        gain_ref[
+                            :,
+                            pl.ds(
+                                pl.multiple_of(start + chip * 512 + cs * 256 + pair * LANES, LANES),
+                                LANES,
+                            ),
+                        ],
+                        (8, LANES),
+                    )
+                    for cs in range(2)
+                )
+                row = chip * 4 + 2 * pair
+                gains[pl.ds(row, 1), :] = jnp.where(even, a, swap_halves(b))[:1]
+                gains[pl.ds(row + 1, 1), :] = jnp.where(even, swap_halves(a), b)[:1]
+        rest = gains[...]
+        for term in range(3):
+            part = rest.astype(jnp.bfloat16)
+            rest = rest - part.astype(jnp.float32)
+            for owner in range(4):
+                out_ref[owner, pl.ds(ROWS_K + term * GAIN_ROWS, GAIN_ROWS), :] = part
+
     scale = scale_ref[...]
     low = low_half((RUN, LANES))
-    for chip in range(4):
-        words = words_buf[chip][...]
+    for k2 in range(2):
+        words = words_buf[k2][...]
         for k in range(4):
             code = lax.shift_right_logical(words, 3 * k) & 7
             floor = code.astype(jnp.float32) - 4.0
             for pair in range(2):
-                floors[chip, pair, pl.ds(k, 128, stride=4), :] = floor[
+                floors[k2, pair, pl.ds(k, 128, stride=4), :] = floor[
                     :, pair * LANES : (pair + 1) * LANES
                 ]
 
         def rows(start):
             values = pl.ds(start, RUN)
-            soft_part, _ = soft_round(rounding_buf[chip][values, :])
-            floor = jnp.concatenate([floors[chip, pair, values, :] for pair in range(2)], axis=1)
+            soft_part, _ = soft_round(rounding_buf[k2][values, :])
+            floor = jnp.concatenate([floors[k2, pair, values, :] for pair in range(2)], axis=1)
             return scale * (floor + soft_part)
 
         for core in range(2):
             for part in range(2):
                 first = rows((core * 4 + part) * RUN)
                 second = rows((core * 4 + 2 + part) * RUN)
-                place = pl.ds(chip * 256 + (part * 2 + core) * RUN, RUN)
+                place = pl.ds(
+                    pl.multiple_of((2 * step + k2) * 256 + (part * 2 + core) * RUN, RUN), RUN
+                )
                 for pair in range(2):
                     a = first[:, pair * LANES : (pair + 1) * LANES]
                     b = second[:, pair * LANES : (pair + 1) * LANES]
@@ -107,16 +134,18 @@
     shape = (4, ROWS_K + 3 * GAIN_ROWS, LANES)
     return pl.pallas_call(
         weight_kernel,
-        grid=(1,),
-        in_specs=pieces_of(4, (128, 256), lambda k, i: (k, 0))
-        + pieces_of(4, (512, 256), lambda k, i: (k, 0))
+        grid=(2,),
+        in_specs=pieces_of(2, (128, 256), lambda k, i: (2 * i + k, 0))
+        + pieces_of(2, (512, 256), lambda k, i: (2 * i + k, 0))
         + [pl.BlockSpec(scale.shape, lambda i: (0, 0)), pl.BlockSpec(gain.shape, lambda i: (0, 0))],
         out_specs=pl.BlockSpec(shape, lambda i: (0, 0, 0)),
         out_shape=jax.ShapeDtypeStruct(shape, jnp.bfloat16),
-        scratch_shapes=[pltpu.VMEM((4, 2, 512, LANES), jnp.float32)],
-        compiler_params=pltpu.CompilerParams(vmem_limit_bytes=24 << 20),
+        scratch_shapes=[
+            pltpu.VMEM((2, 2, 512, LANES), jnp.float32),
+            pltpu.VMEM((GAIN_ROWS, LANES), jnp.float32),
+        ],
         name="make_weight",
-    )(*[words] * 4, *[rounding] * 4, scale, gain)
+    )(*[words] * 2, *[rounding] * 2, scale, gain)
 
 
 def block_kernel(block, width, place_ref, x_ref, w_refs, cur_ref, earlier, sent_ref, spread_ref, next_ref, normed, moved):
@@ -313,6 +342,22 @@
     )(place, mine, other, target, rounding, scale)
 
 
+def add_kernel(parts_ref, out_ref):
+    total = jnp.sum(parts_ref[...], axis=0, keepdims=True)
+    out_ref[...] = jnp.broadcast_to(total, out_ref.shape)
+
+
+def add_copies(parts, count):
+    return pl.pallas_call(
+        add_kernel,
+        in_specs=[IN_VMEM],
+        out_specs=IN_VMEM,
+        out_shape=jax.ShapeDtypeStruct((count, *parts.shape[1:]), parts.dtype),
+        compiler_params=pltpu.CompilerParams(vmem_limit_bytes=2 << 20),
+        name="add_copies",
+    )(parts)
+
+
 def finish_kernel(recon_count, penalty_count, sums_ref, grad_ref, rounding_ref, out_ref, loss_ref):
     sums = jnp.sum(sums_ref[...], axis=0)
     lane = lax.broadcasted_iota(jnp.int32, sums.shape, 1)
@@ -351,9 +396,7 @@
     token_total = tok_dev * dps
     place = jnp.stack([dp_index, core_index]).astype(jnp.int32)
 
-    gain = lax.dynamic_slice_in_dim(norm_gains[0], dp_index * (width_full // dps), width_full // dps)
-    gain = gain.reshape(4, 2, 4, RUN).transpose(0, 2, 1, 3).reshape(GAIN_ROWS, LANES)
-    weight = make_weight(packed_floors[0], rounding[0], scales, gain)
+    weight = make_weight(packed_floors[0], rounding[0], scales, norm_gains)
     weight = exchange(weight, "dp")
     weights = lax.all_gather(weight, SPREAD, axis=0)
 
@@ -393,8 +436,7 @@
     grad, outputs, sums = make_grad(
         error_scale / token_total**0.5, place, mine, other, target_all, rounding[0], scales
     )
-    sums = jnp.sum(exchange(sums, "line"), axis=0, keepdims=True)
-    sums = exchange(jnp.broadcast_to(sums, (16, *sums.shape[1:])), REST)
+    sums = exchange(add_copies(exchange(sums, "line"), 16), REST)
     rounding_next, loss_value = finish(
         float(dps * token_total * width_full), float(width_full * width_full), sums, grad, rounding[0]
     )

time: 278 us -> 273 us (0.982)
  local copies, waits for them, and re-layouts: 10.9 us -> 3.82 us
    unnamed x20 -> x10, local copies, waits for them, and re-layouts: 6.25 us -> 0.03 us
  transfers between devices with their start and end apart: 3 -> 3, of which waited for: 2 -> 2; matrix products, arithmetic and copies ran while one was open for 0% -> 1% of each run, Pallas kernels for 0% -> 0%
where the time goes in v5:
time: 273 us; the launch traced here: 272 us
  blocking collectives  213 us (78%)
  starting transfers between devices  16.4 us (6%)
  Pallas kernels  15.4 us (6%)
  between operations  14.2 us (5%)
  waiting for transfers between devices  9.79 us (4%)
  local copies, waits for them, and re-layouts  3.82 us (1%)
    all_to_all x11, blocking collectives, exchange(): return lax.all_to_all(x, axes, 0, 0, tiled=True)  193 us
    all_gather x1, blocking collectives, per_device(): target_all = lax.all_gather(targets[0], 'dp', axis=0)  20 us
    ppermute x1, starting transfers between devices, per_device(): other = lax.ppermute(mine, 'core', [(0, 1), (1, 0)])  9.57 us
    all_gather x1, waiting for transfers between devices, per_device(): weights = lax.all_gather(weight, SPREAD, axis=0)  7.13 us
    pallas_call x4, Pallas kernels, run_block(): pl.pallas_call(kernel, grid=(1,), in_specs=[IN_SMEM, IN_VMEM] + pieces_of...  6.99 us
    all_to_all x1, starting transfers between devices, exchange(): return lax.all_to_all(x, axes, 0, 0, tiled=True)  6.76 us
  transfers between devices with their start and end apart: 3, of which 2 were waited for; matrix products, arithmetic and copies ran while one was open for 1% of the time, Pallas kernels for 0%

profile of v5, /device:TPU:1, one launch (start us, length us, event | category | flops | bytes accessed | tf_op | source)
XLA Modules:
  0.0 272.4 jit_solution(368771857923075686)
XLA Ops:
  7.2 3.7 %make_weight.1 = bf16[4,1072,128]{2,1,0:T(8,128)(2,1)} custom-call(s32[512,256]{1,0:T(8,128)} %bitcast.47, s32[512,256]{1,0:T(8,128)} %bitcast.48, f32[2048,256]{1,0:T(8,128)} %bitcast.37, f32[2048,256]{1,0:T(8,128)} %bitcast.38, f32[1,256]{1,0:T(1,128)} %scale_ref.1, f32[1,8192]{1,0:T(1,128)} %refs_5_.1), custom_call_target="tpu_custom_call" | custom-call | tf_op jit(solution)/shard_map/make_weight/pallas_call | solution.py:135
  10.9 15.1 %all_to_all.60 = bf16[4,1072,128]{2,1,0:T(8,128)(2,1)} all-to-all(bf16[4,1072,128]{2,1,0:T(8,128)(2,1)} %make_weight.1), channel_id=1, replica_groups=mesh['section'=4,'dp'=4,'line'=8,'side'=2,'core'=2] {'dp'}, dimensions={0} | all-to-all | bytes 2195456 | tf_op jit(solution)/shard_map/all_to_all | solution.py:30
  26.1 32.7 %all_to_all.61 = bf16[8,32,256]{2,1,0:T(8,128)(2,1)S(1)} all-to-all(bf16[8,32,256]{2,1,0:T(8,128)(2,1)S(1)} %broadcast_in_dim.14), channel_id=1, replica_groups=mesh['section'=4,'dp'=4,'line'=8,'side'=2,'core'=2] {'line'}, dimensions={0} | all-to-all | bytes 262144 | tf_op jit(solution)/shard_map/all_to_all | solution.py:30
  59.9 6.8 %all-to-all-start.1 = ((bf16[16,8,16,256]{3,2,1,0:T(8,128)(2,1)}), bf16[16,8,16,256]{3,2,1,0:T(8,128)(2,1)S(1)}, u32[]{:S(2)}, u32[]{:S(2)}) async-start(bf16[16,8,16,256]{3,2,1,0:T(8,128)(2,1)} %bitcast.4), calls=%async_computation.1 | async-start | bytes 2097152 | tf_op jit(solution)/shard_map/all_to_all | solution.py:30
  66.6 20.0 %all_gather.9.target_ref = bf16[4,128,256]{2,1,0:T(8,128)(2,1)S(1)} all-gather(bf16[1,128,256]{2,1,0:T(8,128)(2,1)S(1)} %copy-done.4), channel_id=1, replica_groups=mesh['section'=4,'dp'=4,'line'=8,'side'=2,'core'=2] {'dp'}, dimensions={0}, use_global_device_ids=true | all-gather | bytes 327680 | tf_op jit(solution)/shard_map/all_gather | solution.py:414
  86.9 7.1 %all-gather.3.cloned.1.call-done = bf16[32,1072,128]{2,1,0:T(8,128)(2,1)} async-done(((bf16[4,1072,128]{2,1,0:T(8,128)(2,1)}), bf16[32,1072,128]{2,1,0:T(8,128)(2,1)}) %all-gather.3.cloned.1.call-update) | async-done | bytes 8781840 | tf_op jit(solution)/shard_map/all_gather | solution.py:401
  94.0 1.8 slice.5
  95.8 1.9 block_0.1
  97.7 25.0 %all_to_all.62 = bf16[8,64,128]{2,1,0:T(8,128)(2,1)S(1)} all-to-all(bf16[8,64,128]{2,1,0:T(8,128)(2,1)S(1)} %get-tuple-element.21), channel_id=1, replica_groups=mesh['section'=4,'dp'=4,'line'=8,'side'=2,'core'=2] {'line'}, dimensions={0} | all-to-all | bytes 262144 | tf_op jit(solution)/shard_map/all_to_all | solution.py:30
  123.0 17.6 %all_to_all.63 = bf16[8,8,64,128]{3,2,1,0:T(8,128)(2,1)S(1)} all-to-all(bf16[8,8,64,128]{3,2,1,0:T(8,128)(2,1)S(1)} %broadcast_in_dim.16), channel_id=1, replica_groups=mesh['section'=4,'dp'=4,'line'=8,'side'=2,'core'=2] {'side','dp'}, dimensions={0} | all-to-all | bytes 2097152 | tf_op jit(solution)/shard_map/all_to_all | solution.py:30
  140.5 1.4 block_1.1
  141.9 17.7 %all_to_all.64 = bf16[8,64,128]{2,1,0:T(8,128)(2,1)S(1)} all-to-all(bf16[8,64,128]{2,1,0:T(8,128)(2,1)S(1)} %get-tuple-element.23), channel_id=1, replica_groups=mesh['section'=4,'dp'=4,'line'=8,'side'=2,'core'=2] {'line'}, dimensions={0} | all-to-all | bytes 262144 | tf_op jit(solution)/shard_map/all_to_all | solution.py:30
  159.9 14.4 %all_to_all.65 = bf16[8,8,64,128]{3,2,1,0:T(8,128)(2,1)S(1)} all-to-all(bf16[8,8,64,128]{3,2,1,0:T(8,128)(2,1)S(1)} %broadcast_in_dim.17), channel_id=1, replica_groups=mesh['section'=4,'dp'=4,'line'=8,'side'=2,'core'=2] {'side','dp'}, dimensions={0} | all-to-all | bytes 2097152 | tf_op jit(solution)/shard_map/all_to_all | solution.py:30
  174.2 1.4 block_2.1
  175.6 16.1 %all_to_all.66 = bf16[8,64,128]{2,1,0:T(8,128)(2,1)S(1)} all-to-all(bf16[8,64,128]{2,1,0:T(8,128)(2,1)S(1)} %get-tuple-element.25), channel_id=1, replica_groups=mesh['section'=4,'dp'=4,'line'=8,'side'=2,'core'=2] {'line'}, dimensions={0} | all-to-all | bytes 262144 | tf_op jit(solution)/shard_map/all_to_all | solution.py:30
  192.0 13.4 %all_to_all.67 = bf16[8,8,64,128]{3,2,1,0:T(8,128)(2,1)S(1)} all-to-all(bf16[8,8,64,128]{3,2,1,0:T(8,128)(2,1)S(1)} %broadcast_in_dim.18), channel_id=1, replica_groups=mesh['section'=4,'dp'=4,'line'=8,'side'=2,'core'=2] {'side','dp'}, dimensions={0} | all-to-all | bytes 2097152 | tf_op jit(solution)/shard_map/all_to_all | solution.py:30
  205.4 2.4 block_3.1
  207.8 16.7 %all_to_all.68.mine_ref = bf16[16,320,128]{2,1,0:T(8,128)(2,1)S(1)} all-to-all(bf16[16,320,128]{2,1,0:T(8,128)(2,1)S(1)} %bitcast.46), channel_id=1, replica_groups=mesh['section'=4,'dp'=4,'line'=8,'side'=2,'core'=2] {'section','dp'}, dimensions={0} | all-to-all | bytes 2621440 | tf_op jit(solution)/shard_map/all_to_all | solution.py:30
  224.4 9.6 %collective-permute-start = (bf16[16,320,128]{2,1,0:T(8,128)(2,1)S(1)}, bf16[16,320,128]{2,1,0:T(8,128)(2,1)S(1)}, u32[]{:S(2)}, u32[]{:S(2)}) collective-permute-start(bf16[16,320,128]{2,1,0:T(8,128)(2,1)S(1)} %all_to_all.68.mine_ref), channel_id=1, source_target_pairs={{0,1},{1,0},{2,3},{3,2},{4,5},{5,4},{6,7},{7,6},{8,9},{9,8},{10,11... | collective-permute-start | bytes 3932168 | tf_op jit(solution)/shard_map/ppermute | solution.py:435
  234.0 2.6 collective-permute-done.other_ref
  236.7 3.0 %make_grad.1 = (f32[2048,256]{1,0:T(8,128)S(1)}, bf16[128,256]{1,0:T(8,128)(2,1)}, f32[8,1,128]{2,1,0:T(1,128)S(1)}) custom-call(s32[2]{0:T(128)S(1)} %pad_add_fusion.place_ref, bf16[16,320,128]{2,1,0:T(8,128)(2,1)S(1)} %all_to_all.68.mine_ref, bf16[16,320,128]{2,1,0:T(8,128)(2,1)S(1)} %collective-permute-done.other_ref, ...), custom_call_target="tpu_custom_call" | custom-call | tf_op jit(solution)/shard_map/make_grad/pallas_call | solution.py:327
  239.7 13.9 %all_to_all.69.parts_ref = f32[8,1,128]{2,1,0:T(1,128)S(1)} all-to-all(f32[8,1,128]{2,1,0:T(1,128)S(1)} %get-tuple-element.32), channel_id=1, replica_groups=mesh['section'=4,'dp'=4,'line'=8,'side'=2,'core'=2] {'line'}, dimensions={0} | all-to-all | bytes 8192 | tf_op jit(solution)/shard_map/all_to_all | solution.py:30
  253.5 10.3 %all_to_all.70.sums_ref = f32[16,1,128]{2,1,0:T(1,128)S(1)} all-to-all(f32[16,1,128]{2,1,0:T(1,128)S(1)} %add_copies.1), channel_id=1, replica_groups=mesh['section'=4,'dp'=4,'line'=8,'side'=2,'core'=2] {'side','dp','core'}, dimensions={0} | all-to-all | bytes 16384 | tf_op jit(solution)/shard_map/all_to_all | solution.py:30
  263.9 1.7 finish.1
  (25 shorter events, 2.2 us)
Async XLA Ops:
  7.2 18.9 %copy-start = (bf16[128,256]{1,0:T(8,128)(2,1)S(1)}, bf16[128,256]{1,0:T(8,128)(2,1)}, u32[]{:S(2)}) copy-start(bf16[128,256]{1,0:T(8,128)(2,1)} %param.6) | copy-start | bytes 196612
  7.2 86.9 %all-gather.3.cloned.1.call-start = ((), (), s32[]{:S(2)}) async-start(), calls=%async_computation.12 | async-start | bytes 9879552 | tf_op jit(solution)/shard_map/all_gather | solution.py:401
  26.0 40.6 %copy-start.4 = (bf16[1,128,256]{2,1,0:T(8,128)(2,1)S(1)}, bf16[1,128,256]{2,1,0:T(8,128)(2,1)}, u32[]{:S(2)}) copy-start(bf16[1,128,256]{2,1,0:T(8,128)(2,1)} %param.7) | copy-start | bytes 196612
  59.9 26.8 %all-to-all-start.1 = ((bf16[16,8,16,256]{3,2,1,0:T(8,128)(2,1)}), bf16[16,8,16,256]{3,2,1,0:T(8,128)(2,1)S(1)}, u32[]{:S(2)}, u32[]{:S(2)}) async-start(bf16[16,8,16,256]{3,2,1,0:T(8,128)(2,1)} %bitcast.4), calls=%async_computation.1 | async-start | bytes 2097152 | tf_op jit(solution)/shard_map/all_to_all | solution.py:30
  95.8 44.7 %copy-start.1 = (bf16[32,1072,128]{2,1,0:T(8,128)(2,1)S(1)}, bf16[32,1072,128]{2,1,0:T(8,128)(2,1)}, u32[]{:S(2)}) copy-start(bf16[32,1072,128]{2,1,0:T(8,128)(2,1)} %all-gather.3.cloned.1.call-done) | copy-start | bytes 26345476
  207.7 28.9 %copy-start.2 = (f32[1,2048,256]{2,1,0:T(8,128)S(1)}, f32[1,2048,256]{2,1,0:T(8,128)}, u32[]{:S(2)}) copy-start(f32[1,2048,256]{2,1,0:T(8,128)} %param.9) | copy-start | bytes 6291460
  207.8 28.9 %copy-start.3 = (f32[1,256]{1,0:T(1,128)S(1)}, f32[1,256]{1,0:T(1,128)}, u32[]{:S(2)}) copy-start(f32[1,256]{1,0:T(1,128)} %scale_ref.1) | copy-start | bytes 3076
  224.4 12.2 %collective-permute-start = (bf16[16,320,128]{2,1,0:T(8,128)(2,1)S(1)}, bf16[16,320,128]{2,1,0:T(8,128)(2,1)S(1)}, u32[]{:S(2)}, u32[]{:S(2)}) collective-permute-start(bf16[16,320,128]{2,1,0:T(8,128)(2,1)S(1)} %all_to_all.68.mine_ref), channel_id=1, source_target_pairs={{0,1},{1,0},{2,3},{3,2},{4,5},{5,4},{6,7},{7,6},{8,9},{9,8},{10,11... | collective-permute-start | bytes 3932168 | tf_op jit(solution)/shard_map/ppermute | solution.py:435
Sparse Core Ops, SparseCore 0:
  26.2 67.8 all-gather.2

commit v6 on v4

--- a/solution.py
+++ b/solution.py
@@ -13,6 +13,8 @@
 SPREAD = ("section", "core")
 NEAR = ("side", "dp")
 REST = ("side", "dp", "core")
+FAR = ("dp", "line")
+CLOSE = ("side", "core")
 
 norm_eps = 1e-06
 grad_eps = 1e-06
@@ -53,8 +55,28 @@
 
 def weight_kernel(*refs):
     words_buf, rounding_buf = refs[:4], refs[4:8]
-    scale_ref, gain_ref, out_ref, floors = refs[8:]
-    rest = gain_ref[...]
+    scale_ref, gain_ref, out_ref, floors, gains = refs[8:]
+    start = lax.axis_index("dp") * (gain_ref.shape[1] // 4)
+    even = low_half((8, LANES))
+    for chip in range(4):
+        for pair in range(2):
+            a, b = (
+                jnp.broadcast_to(
+                    gain_ref[
+                        :,
+                        pl.ds(
+                            pl.multiple_of(start + chip * 512 + cs * 256 + pair * LANES, LANES),
+                            LANES,
+                        ),
+                    ],
+                    (8, LANES),
+                )
+                for cs in range(2)
+            )
+            row = chip * 4 + 2 * pair
+            gains[pl.ds(row, 1), :] = jnp.where(even, a, swap_halves(b))[:1]
+            gains[pl.ds(row + 1, 1), :] = jnp.where(even, swap_halves(a), b)[:1]
+    rest = gains[...]
     for term in range(3):
         part = rest.astype(jnp.bfloat16)
         rest = rest - part.astype(jnp.float32)
@@ -113,15 +135,19 @@
         + [pl.BlockSpec(scale.shape, lambda i: (0, 0)), pl.BlockSpec(gain.shape, lambda i: (0, 0))],
         out_specs=pl.BlockSpec(shape, lambda i: (0, 0, 0)),
         out_shape=jax.ShapeDtypeStruct(shape, jnp.bfloat16),
-        scratch_shapes=[pltpu.VMEM((4, 2, 512, LANES), jnp.float32)],
-        compiler_params=pltpu.CompilerParams(vmem_limit_bytes=24 << 20),
+        scratch_shapes=[
+            pltpu.VMEM((4, 2, 512, LANES), jnp.float32),
+            pltpu.VMEM((GAIN_ROWS, LANES), jnp.float32),
+        ],
         name="make_weight",
     )(*[words] * 4, *[rounding] * 4, scale, gain)
 
 
 def block_kernel(block, width, place_ref, x_ref, w_refs, cur_ref, earlier, sent_ref, spread_ref, next_ref, normed, moved):
     moves = [
-        pltpu.make_async_copy(piece, sent_ref.at[k], moved.at[k]) for k, piece in enumerate(earlier)
+        pltpu.make_async_copy(piece.at[d], sent_ref.at[k, d], moved.at[k, d])
+        for k, piece in enumerate(earlier)
+        for d in range(4)
     ]
     for move in moves:
         move.start()
@@ -212,7 +238,7 @@
         ],
         scratch_shapes=[
             pltpu.VMEM((4, 4, 4 * RUN, LANES), jnp.bfloat16),
-            pltpu.SemaphoreType.DMA((max(count, 1),)),
+            pltpu.SemaphoreType.DMA((max(count, 1), 4)),
         ],
         compiler_params=pltpu.CompilerParams(vmem_limit_bytes=24 << 20),
         name=f"block_{block}",
@@ -289,7 +315,7 @@
     row = jnp.zeros((1, LANES), jnp.float32)
     for k, value in enumerate((recon, penalty, squares)):
         row = jnp.where(lane == k, jnp.sum(value), row)
-    for k in range(8):
+    for k in range(32):
         sums_ref[k] = row
 
 
@@ -302,7 +328,7 @@
         out_shape=[
             jax.ShapeDtypeStruct((rows, cols), jnp.float32),
             jax.ShapeDtypeStruct((128, cols), jnp.bfloat16),
-            jax.ShapeDtypeStruct((8, 1, LANES), jnp.float32),
+            jax.ShapeDtypeStruct((32, 1, LANES), jnp.float32),
         ],
         scratch_shapes=[
             pltpu.VMEM((8 * RUN, cols), jnp.bfloat16),
@@ -311,6 +337,22 @@
         compiler_params=pltpu.CompilerParams(vmem_limit_bytes=16 << 20),
         name="make_grad",
     )(place, mine, other, target, rounding, scale)
+
+
+def add_kernel(parts_ref, out_ref):
+    total = jnp.sum(parts_ref[...], axis=0, keepdims=True)
+    out_ref[...] = jnp.broadcast_to(total, out_ref.shape)
+
+
+def add_copies(parts, count):
+    return pl.pallas_call(
+        add_kernel,
+        in_specs=[IN_VMEM],
+        out_specs=IN_VMEM,
+        out_shape=jax.ShapeDtypeStruct((count, *parts.shape[1:]), parts.dtype),
+        compiler_params=pltpu.CompilerParams(vmem_limit_bytes=2 << 20),
+        name="add_copies",
+    )(parts)
 
 
 def finish_kernel(recon_count, penalty_count, sums_ref, grad_ref, rounding_ref, out_ref, loss_ref):
@@ -351,9 +393,7 @@
     token_total = tok_dev * dps
     place = jnp.stack([dp_index, core_index]).astype(jnp.int32)
 
-    gain = lax.dynamic_slice_in_dim(norm_gains[0], dp_index * (width_full // dps), width_full // dps)
-    gain = gain.reshape(4, 2, 4, RUN).transpose(0, 2, 1, 3).reshape(GAIN_ROWS, LANES)
-    weight = make_weight(packed_floors[0], rounding[0], scales, gain)
+    weight = make_weight(packed_floors[0], rounding[0], scales, norm_gains)
     weight = exchange(weight, "dp")
     weights = lax.all_gather(weight, SPREAD, axis=0)
 
@@ -393,8 +433,7 @@
     grad, outputs, sums = make_grad(
         error_scale / token_total**0.5, place, mine, other, target_all, rounding[0], scales
     )
-    sums = jnp.sum(exchange(sums, "line"), axis=0, keepdims=True)
-    sums = exchange(jnp.broadcast_to(sums, (16, *sums.shape[1:])), REST)
+    sums = exchange(add_copies(exchange(sums, FAR), 4), CLOSE)
     rounding_next, loss_value = finish(
         float(dps * token_total * width_full), float(width_full * width_full), sums, grad, rounding[0]
     )

time: 278 us -> 275 us (0.989)
  local copies, waits for them, and re-layouts: 10.9 us -> 3.82 us
  Pallas kernels: 12.8 us -> 16.7 us
    unnamed x20 -> x10, local copies, waits for them, and re-layouts: 6.25 us -> 0.03 us
  transfers between devices with their start and end apart: 3 -> 3, of which waited for: 2 -> 2; matrix products, arithmetic and copies ran while one was open for 0% -> 1% of each run, Pallas kernels for 0% -> 0%
where the time goes in v6:
time: 275 us; the launch traced here: 274 us
  blocking collectives  213 us (77%)
  Pallas kernels  16.7 us (6%)
  starting transfers between devices  16.3 us (6%)
  between operations  14.2 us (5%)
  waiting for transfers between devices  9.79 us (4%)
  local copies, waits for them, and re-layouts  3.82 us (1%)
    all_to_all x11, blocking collectives, exchange(): return lax.all_to_all(x, axes, 0, 0, tiled=True)  193 us
    all_gather x1, blocking collectives, per_device(): target_all = lax.all_gather(targets[0], 'dp', axis=0)  20 us
    ppermute x1, starting transfers between devices, per_device(): other = lax.ppermute(mine, 'core', [(0, 1), (1, 0)])  9.51 us
    pallas_call x4, Pallas kernels, run_block(): pl.pallas_call(kernel, grid=(1,), in_specs=[IN_SMEM, IN_VMEM] + pieces_of...  8.13 us
    all_gather x1, waiting for transfers between devices, per_device(): weights = lax.all_gather(weight, SPREAD, axis=0)  7.13 us
    all_to_all x1, starting transfers between devices, exchange(): return lax.all_to_all(x, axes, 0, 0, tiled=True)  6.76 us
  transfers between devices with their start and end apart: 3, of which 2 were waited for; matrix products, arithmetic and copies ran while one was open for 1% of the time, Pallas kernels for 0%

profile of v6, /device:TPU:1, one launch (start us, length us, event | category | flops | bytes accessed | tf_op | source)
XLA Modules:
  0.0 274.0 jit_solution(2133863456065896346)
XLA Ops:
  7.2 3.9 %make_weight.1 = bf16[4,1072,128]{2,1,0:T(8,128)(2,1)} custom-call(s32[512,256]{1,0:T(8,128)} %bitcast.49, s32[512,256]{1,0:T(8,128)} %bitcast.50, s32[512,256]{1,0:T(8,128)} %bitcast.51, s32[512,256]{1,0:T(8,128)} %bitcast.52, f32[2048,256]{1,0:T(8,128)} %bitcast.33, f32[2048,256]{1,0:T(8,128)} %bitcast.34, f32[2048,256]{1,0:T(8,128)} %bitcast.35, ...), custom_call_target="tpu_custom_call" | custom-call | tf_op jit(solution)/shard_map/make_weight/pallas_call | solution.py:130
  11.1 15.1 %all_to_all.60 = bf16[4,1072,128]{2,1,0:T(8,128)(2,1)} all-to-all(bf16[4,1072,128]{2,1,0:T(8,128)(2,1)} %make_weight.1), channel_id=1, replica_groups=mesh['section'=4,'dp'=4,'line'=8,'side'=2,'core'=2] {'dp'}, dimensions={0} | all-to-all | bytes 2195456 | tf_op jit(solution)/shard_map/all_to_all | solution.py:32
  26.3 32.7 %all_to_all.61 = bf16[8,32,256]{2,1,0:T(8,128)(2,1)S(1)} all-to-all(bf16[8,32,256]{2,1,0:T(8,128)(2,1)S(1)} %broadcast_in_dim.14), channel_id=1, replica_groups=mesh['section'=4,'dp'=4,'line'=8,'side'=2,'core'=2] {'line'}, dimensions={0} | all-to-all | bytes 262144 | tf_op jit(solution)/shard_map/all_to_all | solution.py:32
  60.1 6.8 %all-to-all-start.1 = ((bf16[16,8,16,256]{3,2,1,0:T(8,128)(2,1)}), bf16[16,8,16,256]{3,2,1,0:T(8,128)(2,1)S(1)}, u32[]{:S(2)}, u32[]{:S(2)}) async-start(bf16[16,8,16,256]{3,2,1,0:T(8,128)(2,1)} %bitcast.4), calls=%async_computation.1 | async-start | bytes 2097152 | tf_op jit(solution)/shard_map/all_to_all | solution.py:32
  66.9 20.0 %all_gather.9.target_ref = bf16[4,128,256]{2,1,0:T(8,128)(2,1)S(1)} all-gather(bf16[1,128,256]{2,1,0:T(8,128)(2,1)S(1)} %copy-done.4), channel_id=1, replica_groups=mesh['section'=4,'dp'=4,'line'=8,'side'=2,'core'=2] {'dp'}, dimensions={0}, use_global_device_ids=true | all-gather | bytes 327680 | tf_op jit(solution)/shard_map/all_gather | solution.py:411
  87.1 7.1 %all-gather.3.cloned.1.call-done = bf16[32,1072,128]{2,1,0:T(8,128)(2,1)} async-done(((bf16[4,1072,128]{2,1,0:T(8,128)(2,1)}), bf16[32,1072,128]{2,1,0:T(8,128)(2,1)}) %all-gather.3.cloned.1.call-update) | async-done | bytes 8781840 | tf_op jit(solution)/shard_map/all_gather | solution.py:398
  94.3 1.8 slice.5
  96.0 1.9 block_0.1
  98.0 25.0 %all_to_all.62 = bf16[8,64,128]{2,1,0:T(8,128)(2,1)S(1)} all-to-all(bf16[8,64,128]{2,1,0:T(8,128)(2,1)S(1)} %get-tuple-element.21), channel_id=1, replica_groups=mesh['section'=4,'dp'=4,'line'=8,'side'=2,'core'=2] {'line'}, dimensions={0} | all-to-all | bytes 262144 | tf_op jit(solution)/shard_map/all_to_all | solution.py:32
  123.2 17.6 %all_to_all.63 = bf16[8,8,64,128]{3,2,1,0:T(8,128)(2,1)S(1)} all-to-all(bf16[8,8,64,128]{3,2,1,0:T(8,128)(2,1)S(1)} %broadcast_in_dim.16), channel_id=1, replica_groups=mesh['section'=4,'dp'=4,'line'=8,'side'=2,'core'=2] {'side','dp'}, dimensions={0} | all-to-all | bytes 2097152 | tf_op jit(solution)/shard_map/all_to_all | solution.py:32
  140.8 1.4 block_1.1
  142.2 17.6 %all_to_all.64 = bf16[8,64,128]{2,1,0:T(8,128)(2,1)S(1)} all-to-all(bf16[8,64,128]{2,1,0:T(8,128)(2,1)S(1)} %get-tuple-element.23), channel_id=1, replica_groups=mesh['section'=4,'dp'=4,'line'=8,'side'=2,'core'=2] {'line'}, dimensions={0} | all-to-all | bytes 262144 | tf_op jit(solution)/shard_map/all_to_all | solution.py:32
  160.1 14.4 %all_to_all.65 = bf16[8,8,64,128]{3,2,1,0:T(8,128)(2,1)S(1)} all-to-all(bf16[8,8,64,128]{3,2,1,0:T(8,128)(2,1)S(1)} %broadcast_in_dim.17), channel_id=1, replica_groups=mesh['section'=4,'dp'=4,'line'=8,'side'=2,'core'=2] {'side','dp'}, dimensions={0} | all-to-all | bytes 2097152 | tf_op jit(solution)/shard_map/all_to_all | solution.py:32
  174.5 1.4 block_2.1
  175.9 16.1 %all_to_all.66 = bf16[8,64,128]{2,1,0:T(8,128)(2,1)S(1)} all-to-all(bf16[8,64,128]{2,1,0:T(8,128)(2,1)S(1)} %get-tuple-element.25), channel_id=1, replica_groups=mesh['section'=4,'dp'=4,'line'=8,'side'=2,'core'=2] {'line'}, dimensions={0} | all-to-all | bytes 262144 | tf_op jit(solution)/shard_map/all_to_all | solution.py:32
  192.3 13.3 %all_to_all.67 = bf16[8,8,64,128]{3,2,1,0:T(8,128)(2,1)S(1)} all-to-all(bf16[8,8,64,128]{3,2,1,0:T(8,128)(2,1)S(1)} %broadcast_in_dim.18), channel_id=1, replica_groups=mesh['section'=4,'dp'=4,'line'=8,'side'=2,'core'=2] {'side','dp'}, dimensions={0} | all-to-all | bytes 2097152 | tf_op jit(solution)/shard_map/all_to_all | solution.py:32
  205.6 3.4 %block_3.1 = (bf16[4,4,320,128]{3,2,1,0:T(8,128)(2,1)S(1)}, bf16[8,64,128]{2,1,0:T(8,128)(2,1)}, bf16[64,128]{1,0:T(8,128)(2,1)}) custom-call(s32[2]{0:T(128)S(1)} %pad_add_fusion.place_ref, bf16[2,4,8,64,128]{4,3,2,1,0:T(8,128)(2,1)S(1)} %bitcast.45, bf16[8,4,1072,128]{3,2,1,0:T(8,128)(2,1)S(1)} %bitcast.29, bf16[8,4,1072,128]{3,2,1,0:T(8,128)(2,1)S(1)} %bitcast.30, ...), custom_call_target="tpu_custom_call" | custom-call | tf_op jit(solution)/shard_map/block_3/pallas_call | solution.py:226
  209.1 16.7 %all_to_all.68.mine_ref = bf16[16,320,128]{2,1,0:T(8,128)(2,1)S(1)} all-to-all(bf16[16,320,128]{2,1,0:T(8,128)(2,1)S(1)} %bitcast.48), channel_id=1, replica_groups=mesh['section'=4,'dp'=4,'line'=8,'side'=2,'core'=2] {'section','dp'}, dimensions={0} | all-to-all | bytes 2621440 | tf_op jit(solution)/shard_map/all_to_all | solution.py:32
  225.8 9.5 %collective-permute-start = (bf16[16,320,128]{2,1,0:T(8,128)(2,1)S(1)}, bf16[16,320,128]{2,1,0:T(8,128)(2,1)S(1)}, u32[]{:S(2)}, u32[]{:S(2)}) collective-permute-start(bf16[16,320,128]{2,1,0:T(8,128)(2,1)S(1)} %all_to_all.68.mine_ref), channel_id=1, source_target_pairs={{0,1},{1,0},{2,3},{3,2},{4,5},{5,4},{6,7},{7,6},{8,9},{9,8},{10,11... | collective-permute-start | bytes 3932168 | tf_op jit(solution)/shard_map/ppermute | solution.py:432
  235.3 2.6 collective-permute-done.other_ref
  238.0 3.0 %make_grad.1 = (f32[2048,256]{1,0:T(8,128)S(1)}, bf16[128,256]{1,0:T(8,128)(2,1)}, f32[32,1,128]{2,1,0:T(1,128)S(1)}) custom-call(s32[2]{0:T(128)S(1)} %pad_add_fusion.place_ref, bf16[16,320,128]{2,1,0:T(8,128)(2,1)S(1)} %all_to_all.68.mine_ref, bf16[16,320,128]{2,1,0:T(8,128)(2,1)S(1)} %collective-permute-done.other_ref, ...), custom_call_target="tpu_custom_call" | custom-call | tf_op jit(solution)/shard_map/make_grad/pallas_call | solution.py:324
  241.0 17.3 %all_to_all.69.parts_ref = f32[32,1,128]{2,1,0:T(1,128)S(1)} all-to-all(f32[32,1,128]{2,1,0:T(1,128)S(1)} %get-tuple-element.32), channel_id=1, replica_groups=mesh['section'=4,'dp'=4,'line'=8,'side'=2,'core'=2] {'dp','line'}, dimensions={0} | all-to-all | bytes 32768 | tf_op jit(solution)/shard_map/all_to_all | solution.py:32
  258.3 7.2 %all_to_all.70.sums_ref = f32[4,1,128]{2,1,0:T(1,128)S(1)} all-to-all(f32[4,1,128]{2,1,0:T(1,128)S(1)} %add_copies.1), channel_id=1, replica_groups=mesh['section'=4,'dp'=4,'line'=8,'side'=2,'core'=2] {'side','core'}, dimensions={0} | all-to-all | bytes 4096 | tf_op jit(solution)/shard_map/all_to_all | solution.py:32
  265.5 1.7 finish.1
  (25 shorter events, 2.2 us)
Async XLA Ops:
  7.2 19.1 %copy-start = (bf16[128,256]{1,0:T(8,128)(2,1)S(1)}, bf16[128,256]{1,0:T(8,128)(2,1)}, u32[]{:S(2)}) copy-start(bf16[128,256]{1,0:T(8,128)(2,1)} %param.6) | copy-start | bytes 196612
  7.2 87.1 %all-gather.3.cloned.1.call-start = ((), (), s32[]{:S(2)}) async-start(), calls=%async_computation.12 | async-start | bytes 9879552 | tf_op jit(solution)/shard_map/all_gather | solution.py:398
  26.3 40.6 %copy-start.4 = (bf16[1,128,256]{2,1,0:T(8,128)(2,1)S(1)}, bf16[1,128,256]{2,1,0:T(8,128)(2,1)}, u32[]{:S(2)}) copy-start(bf16[1,128,256]{2,1,0:T(8,128)(2,1)} %param.7) | copy-start | bytes 196612
  60.1 26.8 %all-to-all-start.1 = ((bf16[16,8,16,256]{3,2,1,0:T(8,128)(2,1)}), bf16[16,8,16,256]{3,2,1,0:T(8,128)(2,1)S(1)}, u32[]{:S(2)}, u32[]{:S(2)}) async-start(bf16[16,8,16,256]{3,2,1,0:T(8,128)(2,1)} %bitcast.4), calls=%async_computation.1 | async-start | bytes 2097152 | tf_op jit(solution)/shard_map/all_to_all | solution.py:32
  96.0 44.8 %copy-start.1 = (bf16[32,1072,128]{2,1,0:T(8,128)(2,1)S(1)}, bf16[32,1072,128]{2,1,0:T(8,128)(2,1)}, u32[]{:S(2)}) copy-start(bf16[32,1072,128]{2,1,0:T(8,128)(2,1)} %all-gather.3.cloned.1.call-done) | copy-start | bytes 26345476
  209.1 28.9 %copy-start.2 = (f32[1,2048,256]{2,1,0:T(8,128)S(1)}, f32[1,2048,256]{2,1,0:T(8,128)}, u32[]{:S(2)}) copy-start(f32[1,2048,256]{2,1,0:T(8,128)} %param.9) | copy-start | bytes 6291460
  209.1 28.9 %copy-start.3 = (f32[1,256]{1,0:T(1,128)S(1)}, f32[1,256]{1,0:T(1,128)}, u32[]{:S(2)}) copy-start(f32[1,256]{1,0:T(1,128)} %scale_ref.1) | copy-start | bytes 3076
  225.8 12.2 %collective-permute-start = (bf16[16,320,128]{2,1,0:T(8,128)(2,1)S(1)}, bf16[16,320,128]{2,1,0:T(8,128)(2,1)S(1)}, u32[]{:S(2)}, u32[]{:S(2)}) collective-permute-start(bf16[16,320,128]{2,1,0:T(8,128)(2,1)S(1)} %all_to_all.68.mine_ref), channel_id=1, source_target_pairs={{0,1},{1,0},{2,3},{3,2},{4,5},{5,4},{6,7},{7,6},{8,9},{9,8},{10,11... | collective-permute-start | bytes 3932168 | tf_op jit(solution)/shard_map/ppermute | solution.py:432
Sparse Core Ops, SparseCore 0:
  26.4 67.8 all-gather.2

commit v7 on v5

--- a/solution.py
+++ b/solution.py
@@ -48,7 +48,6 @@
 
 IN_VMEM = pl.BlockSpec(memory_space=pltpu.VMEM)
 IN_SMEM = pl.BlockSpec(memory_space=pltpu.SMEM)
-IN_PLACE = pl.BlockSpec(memory_space=pl.ANY)
 
 
 def weight_kernel(*refs):
@@ -127,7 +126,6 @@
 
 IN_VMEM = pl.BlockSpec(memory_space=pltpu.VMEM)
 IN_SMEM = pl.BlockSpec(memory_space=pltpu.SMEM)
-IN_PLACE = pl.BlockSpec(memory_space=pl.ANY)
 
 
 def make_weight(words, rounding, scale, gain):
@@ -148,12 +146,9 @@
     )(*[words] * 2, *[rounding] * 2, scale, gain)
 
 
-def block_kernel(block, width, place_ref, x_ref, w_refs, cur_ref, earlier, sent_ref, spread_ref, next_ref, normed, moved):
-    moves = [
-        pltpu.make_async_copy(piece, sent_ref.at[k], moved.at[k]) for k, piece in enumerate(earlier)
-    ]
-    for move in moves:
-        move.start()
+def block_kernel(block, width, place_ref, x_ref, w_refs, cur_ref, earlier, sent_ref, spread_ref, next_ref, normed):
+    for k, piece in enumerate(earlier):
+        sent_ref[k] = piece[...]
     slot = len(earlier)
     owner = place_ref[0]
     low = low_half((RUN, LANES))
@@ -214,8 +209,6 @@
         spread_ref[line] = result
     for d in range(4):
         sent_ref[slot, d, pl.ds(4 * RUN, RUN), :] = result
-    for move in moves:
-        move.wait()
 
 
 def run_block(block, width, place, features, weights, current, earlier):
@@ -232,7 +225,7 @@
         in_specs=[IN_SMEM, IN_VMEM]
         + pieces_of(4, (2, 1, ROWS_K + 3 * GAIN_ROWS, LANES), lambda k, i: (block, k, 0, 0))
         + [IN_VMEM]
-        + [IN_PLACE] * count,
+        + [IN_VMEM] * count,
         out_specs=[IN_VMEM] * 3,
         out_shape=[
             jax.ShapeDtypeStruct((count + 1, 4, 5 * RUN, LANES), jnp.bfloat16),
@@ -241,7 +234,6 @@
         ],
         scratch_shapes=[
             pltpu.VMEM((4, 4, 4 * RUN, LANES), jnp.bfloat16),
-            pltpu.SemaphoreType.DMA((max(count, 1),)),
         ],
         compiler_params=pltpu.CompilerParams(vmem_limit_bytes=24 << 20),
         name=f"block_{block}",

time: 273 us -> 273 us (level)
  no operation moved by 1% of the time
where the time goes in v7:
time: 273 us; the launch traced here: 272 us
  blocking collectives  213 us (78%)
  starting transfers between devices  16.3 us (6%)
  Pallas kernels  15 us (5%)
  between operations  14.2 us (5%)
  waiting for transfers between devices  9.79 us (4%)
  local copies, waits for them, and re-layouts  3.81 us (1%)
    all_to_all x11, blocking collectives, exchange(): return lax.all_to_all(x, axes, 0, 0, tiled=True)  193 us
    all_gather x1, blocking collectives, per_device(): target_all = lax.all_gather(targets[0], 'dp', axis=0)  20 us
    ppermute x1, starting transfers between devices, per_device(): other = lax.ppermute(mine, 'core', [(0, 1), (1, 0)])  9.49 us
    all_gather x1, waiting for transfers between devices, per_device(): weights = lax.all_gather(weight, SPREAD, axis=0)  7.13 us
    all_to_all x1, starting transfers between devices, exchange(): return lax.all_to_all(x, axes, 0, 0, tiled=True)  6.76 us
    pallas_call x4, Pallas kernels, run_block(): pl.pallas_call(kernel, grid=(1,), in_specs=[IN_SMEM, IN_VMEM] + pieces_of...  6.69 us
  transfers between devices with their start and end apart: 3, of which 2 were waited for; matrix products, arithmetic and copies ran while one was open for 1% of the time, Pallas kernels for 0%

profile of v7, /device:TPU:1, one launch (start us, length us, event | category | flops | bytes accessed | tf_op | source)
XLA Modules:
  0.0 272.0 jit_solution(10256888745774976732)
XLA Ops:
  7.2 3.7 %make_weight.1 = bf16[4,1072,128]{2,1,0:T(8,128)(2,1)} custom-call(s32[512,256]{1,0:T(8,128)} %bitcast.47, s32[512,256]{1,0:T(8,128)} %bitcast.48, f32[2048,256]{1,0:T(8,128)} %bitcast.37, f32[2048,256]{1,0:T(8,128)} %bitcast.38, f32[1,256]{1,0:T(1,128)} %scale_ref.1, f32[1,8192]{1,0:T(1,128)} %refs_5_.1), custom_call_target="tpu_custom_call" | custom-call | tf_op jit(solution)/shard_map/make_weight/pallas_call | solution.py:133
  10.9 15.1 %all_to_all.60 = bf16[4,1072,128]{2,1,0:T(8,128)(2,1)} all-to-all(bf16[4,1072,128]{2,1,0:T(8,128)(2,1)} %make_weight.1), channel_id=1, replica_groups=mesh['section'=4,'dp'=4,'line'=8,'side'=2,'core'=2] {'dp'}, dimensions={0} | all-to-all | bytes 2195456 | tf_op jit(solution)/shard_map/all_to_all | solution.py:30
  26.1 32.7 %all_to_all.61 = bf16[8,32,256]{2,1,0:T(8,128)(2,1)S(1)} all-to-all(bf16[8,32,256]{2,1,0:T(8,128)(2,1)S(1)} %broadcast_in_dim.14), channel_id=1, replica_groups=mesh['section'=4,'dp'=4,'line'=8,'side'=2,'core'=2] {'line'}, dimensions={0} | all-to-all | bytes 262144 | tf_op jit(solution)/shard_map/all_to_all | solution.py:30
  59.9 6.8 %all-to-all-start.1 = ((bf16[16,8,16,256]{3,2,1,0:T(8,128)(2,1)}), bf16[16,8,16,256]{3,2,1,0:T(8,128)(2,1)S(1)}, u32[]{:S(2)}, u32[]{:S(2)}) async-start(bf16[16,8,16,256]{3,2,1,0:T(8,128)(2,1)} %bitcast.4), calls=%async_computation.1 | async-start | bytes 2097152 | tf_op jit(solution)/shard_map/all_to_all | solution.py:30
  66.6 20.0 %all_gather.9.target_ref = bf16[4,128,256]{2,1,0:T(8,128)(2,1)S(1)} all-gather(bf16[1,128,256]{2,1,0:T(8,128)(2,1)S(1)} %copy-done.4), channel_id=1, replica_groups=mesh['section'=4,'dp'=4,'line'=8,'side'=2,'core'=2] {'dp'}, dimensions={0}, use_global_device_ids=true | all-gather | bytes 327680 | tf_op jit(solution)/shard_map/all_gather | solution.py:406
  86.9 7.1 %all-gather.3.cloned.1.call-done = bf16[32,1072,128]{2,1,0:T(8,128)(2,1)} async-done(((bf16[4,1072,128]{2,1,0:T(8,128)(2,1)}), bf16[32,1072,128]{2,1,0:T(8,128)(2,1)}) %all-gather.3.cloned.1.call-update) | async-done | bytes 8781840 | tf_op jit(solution)/shard_map/all_gather | solution.py:393
  94.0 1.8 slice.5
  95.8 1.9 block_0.1
  97.7 25.0 %all_to_all.62 = bf16[8,64,128]{2,1,0:T(8,128)(2,1)S(1)} all-to-all(bf16[8,64,128]{2,1,0:T(8,128)(2,1)S(1)} %get-tuple-element.21), channel_id=1, replica_groups=mesh['section'=4,'dp'=4,'line'=8,'side'=2,'core'=2] {'line'}, dimensions={0} | all-to-all | bytes 262144 | tf_op jit(solution)/shard_map/all_to_all | solution.py:30
  122.9 17.6 %all_to_all.63 = bf16[8,8,64,128]{3,2,1,0:T(8,128)(2,1)S(1)} all-to-all(bf16[8,8,64,128]{3,2,1,0:T(8,128)(2,1)S(1)} %broadcast_in_dim.16), channel_id=1, replica_groups=mesh['section'=4,'dp'=4,'line'=8,'side'=2,'core'=2] {'side','dp'}, dimensions={0} | all-to-all | bytes 2097152 | tf_op jit(solution)/shard_map/all_to_all | solution.py:30
  140.5 1.4 block_1.1
  141.9 17.7 %all_to_all.64 = bf16[8,64,128]{2,1,0:T(8,128)(2,1)S(1)} all-to-all(bf16[8,64,128]{2,1,0:T(8,128)(2,1)S(1)} %get-tuple-element.23), channel_id=1, replica_groups=mesh['section'=4,'dp'=4,'line'=8,'side'=2,'core'=2] {'line'}, dimensions={0} | all-to-all | bytes 262144 | tf_op jit(solution)/shard_map/all_to_all | solution.py:30
  159.8 14.4 %all_to_all.65 = bf16[8,8,64,128]{3,2,1,0:T(8,128)(2,1)S(1)} all-to-all(bf16[8,8,64,128]{3,2,1,0:T(8,128)(2,1)S(1)} %broadcast_in_dim.17), channel_id=1, replica_groups=mesh['section'=4,'dp'=4,'line'=8,'side'=2,'core'=2] {'side','dp'}, dimensions={0} | all-to-all | bytes 2097152 | tf_op jit(solution)/shard_map/all_to_all | solution.py:30
  174.2 1.4 block_2.1
  175.6 16.1 %all_to_all.66 = bf16[8,64,128]{2,1,0:T(8,128)(2,1)S(1)} all-to-all(bf16[8,64,128]{2,1,0:T(8,128)(2,1)S(1)} %get-tuple-element.25), channel_id=1, replica_groups=mesh['section'=4,'dp'=4,'line'=8,'side'=2,'core'=2] {'line'}, dimensions={0} | all-to-all | bytes 262144 | tf_op jit(solution)/shard_map/all_to_all | solution.py:30
  191.9 13.4 %all_to_all.67 = bf16[8,8,64,128]{3,2,1,0:T(8,128)(2,1)S(1)} all-to-all(bf16[8,8,64,128]{3,2,1,0:T(8,128)(2,1)S(1)} %broadcast_in_dim.18), channel_id=1, replica_groups=mesh['section'=4,'dp'=4,'line'=8,'side'=2,'core'=2] {'side','dp'}, dimensions={0} | all-to-all | bytes 2097152 | tf_op jit(solution)/shard_map/all_to_all | solution.py:30
  205.3 2.1 block_3.1
  207.4 16.7 %all_to_all.68.mine_ref = bf16[16,320,128]{2,1,0:T(8,128)(2,1)S(1)} all-to-all(bf16[16,320,128]{2,1,0:T(8,128)(2,1)S(1)} %bitcast.46), channel_id=1, replica_groups=mesh['section'=4,'dp'=4,'line'=8,'side'=2,'core'=2] {'section','dp'}, dimensions={0} | all-to-all | bytes 2621440 | tf_op jit(solution)/shard_map/all_to_all | solution.py:30
  224.2 9.5 %collective-permute-start = (bf16[16,320,128]{2,1,0:T(8,128)(2,1)S(1)}, bf16[16,320,128]{2,1,0:T(8,128)(2,1)S(1)}, u32[]{:S(2)}, u32[]{:S(2)}) collective-permute-start(bf16[16,320,128]{2,1,0:T(8,128)(2,1)S(1)} %all_to_all.68.mine_ref), channel_id=1, source_target_pairs={{0,1},{1,0},{2,3},{3,2},{4,5},{5,4},{6,7},{7,6},{8,9},{9,8},{10,11... | collective-permute-start | bytes 3932168 | tf_op jit(solution)/shard_map/ppermute | solution.py:427
  233.7 2.6 collective-permute-done.other_ref
  236.3 3.0 %make_grad.1 = (f32[2048,256]{1,0:T(8,128)S(1)}, bf16[128,256]{1,0:T(8,128)(2,1)}, f32[8,1,128]{2,1,0:T(1,128)S(1)}) custom-call(s32[2]{0:T(128)S(1)} %pad_add_fusion.place_ref, bf16[16,320,128]{2,1,0:T(8,128)(2,1)S(1)} %all_to_all.68.mine_ref, bf16[16,320,128]{2,1,0:T(8,128)(2,1)S(1)} %collective-permute-done.other_ref, ...), custom_call_target="tpu_custom_call" | custom-call | tf_op jit(solution)/shard_map/make_grad/pallas_call | solution.py:319
  239.3 13.9 %all_to_all.69.parts_ref = f32[8,1,128]{2,1,0:T(1,128)S(1)} all-to-all(f32[8,1,128]{2,1,0:T(1,128)S(1)} %get-tuple-element.32), channel_id=1, replica_groups=mesh['section'=4,'dp'=4,'line'=8,'side'=2,'core'=2] {'line'}, dimensions={0} | all-to-all | bytes 8192 | tf_op jit(solution)/shard_map/all_to_all | solution.py:30
  253.2 10.3 %all_to_all.70.sums_ref = f32[16,1,128]{2,1,0:T(1,128)S(1)} all-to-all(f32[16,1,128]{2,1,0:T(1,128)S(1)} %add_copies.1), channel_id=1, replica_groups=mesh['section'=4,'dp'=4,'line'=8,'side'=2,'core'=2] {'side','dp','core'}, dimensions={0} | all-to-all | bytes 16384 | tf_op jit(solution)/shard_map/all_to_all | solution.py:30
  263.5 1.7 finish.1
  (25 shorter events, 2.2 us)
Async XLA Ops:
  7.2 18.9 %copy-start = (bf16[128,256]{1,0:T(8,128)(2,1)S(1)}, bf16[128,256]{1,0:T(8,128)(2,1)}, u32[]{:S(2)}) copy-start(bf16[128,256]{1,0:T(8,128)(2,1)} %param.6) | copy-start | bytes 196612
  7.2 86.9 %all-gather.3.cloned.1.call-start = ((), (), s32[]{:S(2)}) async-start(), calls=%async_computation.12 | async-start | bytes 9879552 | tf_op jit(solution)/shard_map/all_gather | solution.py:393
  26.0 40.6 %copy-start.4 = (bf16[1,128,256]{2,1,0:T(8,128)(2,1)S(1)}, bf16[1,128,256]{2,1,0:T(8,128)(2,1)}, u32[]{:S(2)}) copy-start(bf16[1,128,256]{2,1,0:T(8,128)(2,1)} %param.7) | copy-start | bytes 196612
  59.9 26.8 %all-to-all-start.1 = ((bf16[16,8,16,256]{3,2,1,0:T(8,128)(2,1)}), bf16[16,8,16,256]{3,2,1,0:T(8,128)(2,1)S(1)}, u32[]{:S(2)}, u32[]{:S(2)}) async-start(bf16[16,8,16,256]{3,2,1,0:T(8,128)(2,1)} %bitcast.4), calls=%async_computation.1 | async-start | bytes 2097152 | tf_op jit(solution)/shard_map/all_to_all | solution.py:30
  95.8 44.7 %copy-start.1 = (bf16[32,1072,128]{2,1,0:T(8,128)(2,1)S(1)}, bf16[32,1072,128]{2,1,0:T(8,128)(2,1)}, u32[]{:S(2)}) copy-start(bf16[32,1072,128]{2,1,0:T(8,128)(2,1)} %all-gather.3.cloned.1.call-done) | copy-start | bytes 26345476
  207.4 28.9 %copy-start.2 = (f32[1,2048,256]{2,1,0:T(8,128)S(1)}, f32[1,2048,256]{2,1,0:T(8,128)}, u32[]{:S(2)}) copy-start(f32[1,2048,256]{2,1,0:T(8,128)} %param.9) | copy-start | bytes 6291460
  207.4 28.9 %copy-start.3 = (f32[1,256]{1,0:T(1,128)S(1)}, f32[1,256]{1,0:T(1,128)}, u32[]{:S(2)}) copy-start(f32[1,256]{1,0:T(1,128)} %scale_ref.1) | copy-start | bytes 3076
  224.2 12.1 %collective-permute-start = (bf16[16,320,128]{2,1,0:T(8,128)(2,1)S(1)}, bf16[16,320,128]{2,1,0:T(8,128)(2,1)S(1)}, u32[]{:S(2)}, u32[]{:S(2)}) collective-permute-start(bf16[16,320,128]{2,1,0:T(8,128)(2,1)S(1)} %all_to_all.68.mine_ref), channel_id=1, source_target_pairs={{0,1},{1,0},{2,3},{3,2},{4,5},{5,4},{6,7},{7,6},{8,9},{9,8},{10,11... | collective-permute-start | bytes 3932168 | tf_op jit(solution)/shard_map/ppermute | solution.py:427
Sparse Core Ops, SparseCore 0:
  26.2 67.8 all-gather.2
